TPU v7x, 128 devices: a whole 4x4x4 slice. The times are simulated.
128 devices in a mesh: seq: 32 (over y, x, z_lo), mp: 4 (over z_hi, core).
Axes of the slice: x: 4, y: 4, z: 4 (z_hi: 2, z_lo: 2; z = z_hi * 2 + z_lo), core: 2. Of those that a mesh axis runs over, the one named last changes fastest.
Arguments:
- frames: bfloat16 [768, 250, 256], P('seq'), may hold values from -7.5 to 7.5
- intra_qkv: bfloat16 [256, 3, 256], P(None, None, 'mp'), may hold values from -20 to 20
- intra_out: bfloat16 [256, 256], P('mp'), may hold values from -0.375 to 0.375
- intra_up: bfloat16 [256, 1024], P(None, 'mp'), may hold values from -0.375 to 0.375
- intra_down: bfloat16 [1024, 256], P('mp'), may hold values from -0.1875 to 0.1875
- inter_qkv: bfloat16 [256, 3, 256], P(None, None, 'mp'), may hold values from -20 to 20
- inter_out: bfloat16 [256, 256], P('mp'), may hold values from -0.375 to 0.375
- inter_up: bfloat16 [256, 1024], P(None, 'mp'), may hold values from -0.375 to 0.375
- inter_down: bfloat16 [1024, 256], P('mp'), may hold values from -0.1875 to 0.1875
Outputs:
- margin_sum: bfloat16 [96000, 256], P('seq')
All inputs are finite; a program needn't handle non-finite values.
Results may differ from a plain program's by a relative error of at most 0.014.
Values may be sent and summed in bfloat16 or wider, within the bound.
No kernel may reach another device: no remote copies, remote signals or barrier semaphores. Data moves between devices by JAX's collectives and lax.ppermute only.
A program may use at most 128 MiB of HBM per device.

v0:
```python
import jax
import jax.numpy as jnp
from jax import lax
from jax.sharding import PartitionSpec as P

HEADS = 8
HD = 32
K = 250


def in_order(blocks, dim):
    lengths = list(blocks.shape[1:])
    lengths[dim] *= blocks.shape[0]
    return jnp.moveaxis(blocks, 0, dim).reshape(lengths)


def gather_together(arrays, axis, dims):
    vector = jnp.concatenate([a.reshape(-1) for a in arrays])
    lines, at, done = (lax.all_gather(vector, axis), 0, [])
    for a, dim in zip(arrays, dims):
        blocks = lines[:, at : at + a.size].reshape(-1, *a.shape)
        done.append(in_order(blocks, dim))
        at += a.size
    return tuple(done)


def passed_along(shard, axis, by):
    peers = lax.axis_size(axis)
    pairs = [(i, i + by) for i in range(peers) if 0 <= i + by < peers]
    return lax.ppermute(shard, axis, pairs)


def layer_norm(values):
    values = values.astype(jnp.float32)
    centre = values - jnp.mean(values, axis=-1, keepdims=True)
    spread = jnp.mean(centre * centre, axis=-1, keepdims=True)
    return (centre * lax.rsqrt(spread + 1e-05)).astype(jnp.bfloat16)


def attend(query_rows, key_rows, value_rows):
    factor = query_rows.shape[-1] ** (-0.5)
    scores = (
        jnp.einsum("bqhe,bkhe->bhqk", query_rows, key_rows, preferred_element_type=jnp.float32)
        * factor
    )
    scores = scores - jnp.max(scores, axis=-1, keepdims=True)
    weights = jnp.exp(scores)
    weights = (weights / jnp.sum(weights, axis=-1, keepdims=True)).astype(jnp.bfloat16)
    return jnp.einsum(
        "bhqk,bkhe->bqhe", weights, value_rows, preferred_element_type=jnp.float32
    ).astype(jnp.bfloat16)


def attend_rows(query_rows, key_rows, value_rows, per_step):
    blocks = query_rows.shape[0] // per_step
    stacked = tuple(
        (
            member.reshape((blocks, per_step) + member.shape[1:])
            for member in (query_rows, key_rows, value_rows)
        )
    )
    attended = lax.map(lambda pieces: attend(pieces[0], pieces[1], pieces[2]), stacked)
    return attended.reshape(query_rows.shape)


def whole_block(stream, qkv_weight, out_weight, up_weight, down_weight):
    normed = layer_norm(stream)
    projected = jnp.einsum(
        "pcd,dtj->tpcj", normed, qkv_weight, preferred_element_type=jnp.float32
    ).astype(jnp.bfloat16)
    projected = projected.reshape(3, stream.shape[0], stream.shape[1], HEADS, HD)
    attended = attend_rows(projected[0], projected[1], projected[2], 1)
    branch = jnp.einsum(
        "pche,hed->pcd",
        attended,
        out_weight.reshape(HEADS, HD, -1),
        preferred_element_type=jnp.float32,
    )
    middle = (stream.astype(jnp.float32) + branch).astype(jnp.bfloat16)
    normed = layer_norm(middle)
    hidden = jax.nn.relu(
        jnp.einsum("pcd,df->pcf", normed, up_weight, preferred_element_type=jnp.float32)
    ).astype(jnp.bfloat16)
    branch = jnp.einsum("pcf,fd->pcd", hidden, down_weight, preferred_element_type=jnp.float32)
    return (middle.astype(jnp.float32) + branch).astype(jnp.bfloat16)


def on_device(
    frames, intra_qkv, intra_out, intra_up, intra_down, inter_qkv, inter_out, inter_up, inter_down
):
    seq_count = lax.axis_size("seq")
    model_count = lax.axis_size("mp")
    intra_full = gather_together((intra_qkv, intra_out, intra_up, intra_down), "mp", (2, 0, 1, 0))
    span_count = frames.shape[0] // model_count
    own_spans = lax.dynamic_slice_in_dim(frames, lax.axis_index("mp") * span_count, span_count, 0)
    finished = whole_block(own_spans, intra_full[0], intra_full[1], intra_full[2], intra_full[3])
    stream = lax.all_gather(finished, "mp", axis=0, tiled=True)
    spread_devices = seq_count * model_count
    padded_len = (K + spread_devices - 1) // spread_devices * spread_devices
    full_weights = gather_together((inter_qkv, inter_out, inter_up, inter_down), "mp", (2, 0, 1, 0))
    per_device = padded_len // spread_devices
    arranged = jnp.pad(jnp.transpose(stream, (1, 0, 2)), ((0, padded_len - K), (0, 0), (0, 0)))
    arranged = arranged.reshape(
        seq_count, model_count, per_device, stream.shape[0], stream.shape[2]
    )
    mine = lax.dynamic_index_in_dim(arranged, lax.axis_index("mp"), 1, keepdims=False)
    mine = mine.reshape(seq_count * per_device, stream.shape[0], stream.shape[2])
    spread_rows = lax.all_to_all(mine, "seq", split_axis=0, concat_axis=1, tiled=True)
    spread_rows = whole_block(
        spread_rows, full_weights[0], full_weights[1], full_weights[2], full_weights[3]
    )
    returned = lax.all_to_all(spread_rows, "seq", split_axis=1, concat_axis=0, tiled=True)
    returned = returned.reshape(seq_count, 1, per_device, stream.shape[0], stream.shape[2])
    collected = lax.all_gather(returned, "mp", axis=1, tiled=True)
    collected = collected.reshape(padded_len, stream.shape[0], stream.shape[2])
    stream = jnp.transpose(collected[:K], (1, 0, 2))
    hop_len = K // 2
    tail_rows = stream[:, hop_len:]
    carried = passed_along(tail_rows[-1], "seq", 1)
    earlier = jnp.concatenate([carried[None], tail_rows[:-1]], axis=0)
    summed = stream[:, :hop_len].astype(jnp.float32) + earlier.astype(jnp.float32)
    return summed.astype(jnp.bfloat16).reshape(-1, stream.shape[2])


def solution(mesh):
    return jax.shard_map(
        on_device,
        mesh=mesh,
        in_specs=(
            P("seq", None, None),
            P(None, None, "mp"),
            P("mp", None),
            P(None, "mp"),
            P("mp", None),
            P(None, None, "mp"),
            P("mp", None),
            P(None, "mp"),
            P("mp", None),
        ),
        out_specs=P("seq", None),
        check_vma=False,
    )
```

profile of v0, /device:TPU:8, one launch (start us, length us, event | category | flops | bytes accessed | tf_op | source)
XLA Modules:
  0.0 260.5 jit_solution(12997414813802845133)
XLA Ops:
  6.5 1.2 copy.99
  7.9 1.0 copy.140
  8.9 1.0 copy.141
  10.0 0.8 copy.139
  10.7 0.8 pad_maximum_fusion
  11.9 1.0 copy.144
  13.0 1.0 copy.145
  14.0 0.8 copy.143
  14.8 0.8 pad_maximum_fusion.1
  16.3 0.6 copy-done.2
  17.4 20.4 %all-gather.10.cloned.1.call-done = bf16[786432]{0:T(1024)(128)(2,1)} async-done(((bf16[196608]{0:T(1024)(128)(2,1)}), bf16[786432]{0:T(1024)(128)(2,1)}) %all-gather.10.cloned.1.call-update) | async-done | bytes 1572880 | tf_op jit(solution)/shard_map/all_gather | solution.py:19
  37.8 2.0 reshape.242
  40.0 1.2 fusion.147
  41.2 1.7 reshape.220
  42.9 1.5 copy.100
  44.4 1.0 convert_bitcast_fusion.1
  45.4 1.5 fusion.145
  47.2 1.2 reshape.251
  48.4 27.5 %while.20 = (s32[]{:T(128)}, bf16[6,1,250,8,32]{2,4,3,1,0:T(8,128)(2,1)}, bf16[6,1,250,8,32]{2,4,3,1,0:T(8,128)(2,1)}, bf16[6,1,250,8,32]{2,4,3,1,0:T(8,128)(2,1...) while((s32[]{:T(128)}, bf16[6,1,250,8,32]{2,4,3,1,0:T(8,128)(2,1)}, bf16[6,1,250,8,32]{2,4,3,1,0:T(8,128)(2,1)}, ...), condition=%wide.region_5.6_spmd, body=%wide.region_2.5_spmd.sunk | while | flops 99566496 | bytes 805573 | solution.py:62
  48.4 1.8 fusion.176
  50.3 2.7 %fusion.177 = bf16[6,1,250,8,32]{2,4,3,1,0:T(8,128)(2,1)} fusion(bf16[6,1,250,8,32]{2,4,3,1,0:T(8,128)(2,1)} %get-tuple-element.220, s32[]{:T(128)} %get-tuple-element.219, f32[8,250]{1,0:T(8,128)S(1)} %fusion.176, bf16[6,1,250,8,32]{2,4,3,1,0:T(8,128)(2,1)} %get-tuple-element.227, bf16[6,1,250,8,32]{2,4,3,1,0:T(8,128)(2,1)} %get-tuple-element.229, ...), kind=kOutput, calls=%fused_computation.7.clone.1 | convolution fusion | flops 66066248 | bytes 534336 | tf_op jit(solution)/shard_map/while/body/eval_jaxpr/bhqk,bkhe->bqhe/dot_general | solution.py:49
  53.0 1.8 fusion.176
  54.9 2.7 %fusion.177 = bf16[6,1,250,8,32]{2,4,3,1,0:T(8,128)(2,1)} fusion(bf16[6,1,250,8,32]{2,4,3,1,0:T(8,128)(2,1)} %get-tuple-element.220, s32[]{:T(128)} %get-tuple-element.219, f32[8,250]{1,0:T(8,128)S(1)} %fusion.176, bf16[6,1,250,8,32]{2,4,3,1,0:T(8,128)(2,1)} %get-tuple-element.227, bf16[6,1,250,8,32]{2,4,3,1,0:T(8,128)(2,1)} %get-tuple-element.229, ...), kind=kOutput, calls=%fused_computation.7.clone.1 | convolution fusion | flops 66066248 | bytes 534336 | tf_op jit(solution)/shard_map/while/body/eval_jaxpr/bhqk,bkhe->bqhe/dot_general | solution.py:49
  57.6 1.8 fusion.176
  59.4 2.8 %fusion.177 = bf16[6,1,250,8,32]{2,4,3,1,0:T(8,128)(2,1)} fusion(bf16[6,1,250,8,32]{2,4,3,1,0:T(8,128)(2,1)} %get-tuple-element.220, s32[]{:T(128)} %get-tuple-element.219, f32[8,250]{1,0:T(8,128)S(1)} %fusion.176, bf16[6,1,250,8,32]{2,4,3,1,0:T(8,128)(2,1)} %get-tuple-element.227, bf16[6,1,250,8,32]{2,4,3,1,0:T(8,128)(2,1)} %get-tuple-element.229, ...), kind=kOutput, calls=%fused_computation.7.clone.1 | convolution fusion | flops 66066248 | bytes 534336 | tf_op jit(solution)/shard_map/while/body/eval_jaxpr/bhqk,bkhe->bqhe/dot_general | solution.py:49
  62.2 1.8 fusion.176
  64.1 2.8 %fusion.177 = bf16[6,1,250,8,32]{2,4,3,1,0:T(8,128)(2,1)} fusion(bf16[6,1,250,8,32]{2,4,3,1,0:T(8,128)(2,1)} %get-tuple-element.220, s32[]{:T(128)} %get-tuple-element.219, f32[8,250]{1,0:T(8,128)S(1)} %fusion.176, bf16[6,1,250,8,32]{2,4,3,1,0:T(8,128)(2,1)} %get-tuple-element.227, bf16[6,1,250,8,32]{2,4,3,1,0:T(8,128)(2,1)} %get-tuple-element.229, ...), kind=kOutput, calls=%fused_computation.7.clone.1 | convolution fusion | flops 66066248 | bytes 534336 | tf_op jit(solution)/shard_map/while/body/eval_jaxpr/bhqk,bkhe->bqhe/dot_general | solution.py:49
  66.8 1.8 fusion.176
  68.7 2.7 %fusion.177 = bf16[6,1,250,8,32]{2,4,3,1,0:T(8,128)(2,1)} fusion(bf16[6,1,250,8,32]{2,4,3,1,0:T(8,128)(2,1)} %get-tuple-element.220, s32[]{:T(128)} %get-tuple-element.219, f32[8,250]{1,0:T(8,128)S(1)} %fusion.176, bf16[6,1,250,8,32]{2,4,3,1,0:T(8,128)(2,1)} %get-tuple-element.227, bf16[6,1,250,8,32]{2,4,3,1,0:T(8,128)(2,1)} %get-tuple-element.229, ...), kind=kOutput, calls=%fused_computation.7.clone.1 | convolution fusion | flops 66066248 | bytes 534336 | tf_op jit(solution)/shard_map/while/body/eval_jaxpr/bhqk,bkhe->bqhe/dot_general | solution.py:49
  71.4 1.8 fusion.176
  73.2 2.7 %fusion.177 = bf16[6,1,250,8,32]{2,4,3,1,0:T(8,128)(2,1)} fusion(bf16[6,1,250,8,32]{2,4,3,1,0:T(8,128)(2,1)} %get-tuple-element.220, s32[]{:T(128)} %get-tuple-element.219, f32[8,250]{1,0:T(8,128)S(1)} %fusion.176, bf16[6,1,250,8,32]{2,4,3,1,0:T(8,128)(2,1)} %get-tuple-element.227, bf16[6,1,250,8,32]{2,4,3,1,0:T(8,128)(2,1)} %get-tuple-element.229, ...), kind=kOutput, calls=%fused_computation.7.clone.1 | convolution fusion | flops 66066248 | bytes 534336 | tf_op jit(solution)/shard_map/while/body/eval_jaxpr/bhqk,bkhe->bqhe/dot_general | solution.py:49
  76.0 1.7 convert_reduce_fusion.1
  78.2 2.8 %fusion.105 = bf16[6,250,256]{2,1,0:T(8,128)(2,1)} fusion(bf16[6,250,256]{2,1,0:T(8,128)(2,1)S(1)} %get-tuple-element.144, bf16[1024,256,1]{1,0,2:T(8,128)(2,1)S(1)} %copy-done.10, bf16[256,1024,1]{0,1,2:T(8,128)(2,1)S(1)} %bitcast.240, f32[6,250]{1,0:T(8,128)S(1)} %add_rsqrt_fusion.1, f32[6,250]{1,0:T(8,128)S(1)} %broadcast_multiply_fusion.1), kind=kOutput, calls=%fused_computation.87 | convolution fusion | flops 1578624000 | bytes 2596576 | tf_op jit(solution)/shard_map/pcf,fd->pcd/dot_general | solution.py:84
  81.1 3.1 %reshape.243 = bf16[4,196608]{1,0:T(4,128)(2,1)} reshape(bf16[786432]{0:T(1024)(128)(2,1)} %all-gather.12.cloned.1.call-done) | data formatting | bytes 3145728 | tf_op jit(solution)/shard_map/all_gather | solution.py:19
  84.3 28.9 %all-gather.8.cloned.1.call-done = bf16[24,250,256]{2,1,0:T(8,128)(2,1)} async-done(((bf16[6,250,256]{2,1,0:T(8,128)(2,1)}), bf16[24,250,256]{2,1,0:T(8,128)(2,1)}) %all-gather.8.cloned.1.call-update) | async-done | bytes 3072016 | tf_op jit(solution)/shard_map/all_gather | solution.py:97
  113.2 2.1 pad.4
  115.3 3.2 %reshape.225 = bf16[32,4,2,24,256]{4,2,1,0,3:T(2,128)(2,1)} reshape(bf16[256,24,256]{2,0,1:T(8,128)(2,1)S(1)} %pad.4) | data formatting | bytes 6291456 | tf_op jit(solution)/shard_map/reshape | solution.py:103
  118.5 1.8 constant_dynamic-slice_fusion
  120.3 1.5 copy.138
  121.9 7.5 %all-to-all-start = ((bf16[64,24,256]{2,1,0:T(8,128)(2,1)}), bf16[64,24,256]{2,1,0:T(8,128)(2,1)S(1)}, u32[]{:S(2)}, u32[]{:S(2)}) async-start(bf16[64,24,256]{2,1,0:T(8,128)(2,1)} %bitcast.31), calls=%async_computation | async-start | bytes 1572864 | tf_op jit(solution)/shard_map/all_to_all | solution.py:108
  129.6 1.2 fusion.146
  130.8 0.7 reshape.231
  131.5 0.6 copy.109
  132.6 1.0 copy.115
  133.6 1.2 reshape.257
  134.8 7.5 %all-to-all-done = bf16[64,24,256]{2,1,0:T(8,128)(2,1)S(1)} async-done(((bf16[64,24,256]{2,1,0:T(8,128)(2,1)}), bf16[64,24,256]{2,1,0:T(8,128)(2,1)S(1)}, u32[]{:S(2)}, u32[]{:S(2)}) %all-to-all-start) | async-done | bytes 786464 | tf_op jit(solution)/shard_map/all_to_all | solution.py:108
  143.8 0.8 convert_bitcast_fusion
  144.8 36.6 %while.21 = (s32[]{:T(128)}, bf16[2,1,768,8,32]{2,4,3,1,0:T(8,128)(2,1)}, bf16[2,1,768,8,32]{2,4,3,1,0:T(8,128)(2,1)S(1)}, bf16[2,1,768,8,32]{2,4,3,1,0:T(8,128)...) while((s32[]{:T(128)}, bf16[2,1,768,8,32]{2,4,3,1,0:T(8,128)(2,1)}, ...), condition=%wide.region_13.14_spmd, body=%wide.region_10.13_spmd.sunk | while | flops 627770112 | bytes 39372868 | solution.py:62
  144.8 9.4 %fusion.181 = (f32[8,768]{1,0:T(8,128)S(1)}, f32[8,768,768]{1,2,0:T(8,128)}) fusion(bf16[2,1,768,8,32]{2,4,3,1,0:T(8,128)(2,1)S(1)} %get-tuple-element.247, s32[]{:T(128)} %get-tuple-element.237, bf16[2,1,768,8,32]{2,4,3,1,0:T(8,128)(2,1)S(1)} %get-tuple-element.246), kind=kOutput, calls=%fused_computation.123.clone.1 | convolution fusion | flops 316146432 | bytes 19686400 | tf_op jit(solution)/shard_map/while/body/eval_jaxpr/sub | solution.py:46
  154.2 8.8 %fusion.182 = bf16[2,1,768,8,32]{2,4,3,1,0:T(8,128)(2,1)} fusion(bf16[2,1,768,8,32]{2,4,3,1,0:T(8,128)(2,1)} %get-tuple-element.238, s32[]{:T(128)} %get-tuple-element.237, f32[8,768,768]{1,2,0:T(8,128)} %get-tuple-element.211, f32[8,768]{1,0:T(8,128)S(1)} %get-tuple-element.212, bf16[2,1,768,8,32]{2,4,3,1,0:T(8,128)(2,1)S(1)} %get-tuple-element.245), kind=kOutput, calls=%fused_computation.37.clone.1 | convolution fusion | flops 311623680 | bytes 19686400 | tf_op jit(solution)/shard_map/while/body/eval_jaxpr/bhqk,bkhe->bqhe/dot_general | solution.py:49
  163.1 9.4 %fusion.181 = (f32[8,768]{1,0:T(8,128)S(1)}, f32[8,768,768]{1,2,0:T(8,128)}) fusion(bf16[2,1,768,8,32]{2,4,3,1,0:T(8,128)(2,1)S(1)} %get-tuple-element.247, s32[]{:T(128)} %get-tuple-element.237, bf16[2,1,768,8,32]{2,4,3,1,0:T(8,128)(2,1)S(1)} %get-tuple-element.246), kind=kOutput, calls=%fused_computation.123.clone.1 | convolution fusion | flops 316146432 | bytes 19686400 | tf_op jit(solution)/shard_map/while/body/eval_jaxpr/sub | solution.py:46
  172.5 8.9 %fusion.182 = bf16[2,1,768,8,32]{2,4,3,1,0:T(8,128)(2,1)} fusion(bf16[2,1,768,8,32]{2,4,3,1,0:T(8,128)(2,1)} %get-tuple-element.238, s32[]{:T(128)} %get-tuple-element.237, f32[8,768,768]{1,2,0:T(8,128)} %get-tuple-element.211, f32[8,768]{1,0:T(8,128)S(1)} %get-tuple-element.212, bf16[2,1,768,8,32]{2,4,3,1,0:T(8,128)(2,1)S(1)} %get-tuple-element.245), kind=kOutput, calls=%fused_computation.37.clone.1 | convolution fusion | flops 311623680 | bytes 19686400 | tf_op jit(solution)/shard_map/while/body/eval_jaxpr/bhqk,bkhe->bqhe/dot_general | solution.py:49
  182.2 1.7 convert_reduce_fusion
  184.1 1.9 fusion.106
  186.0 0.7 copy.119
  186.6 17.8 %all_to_all.24 = bf16[2,768,256]{2,0,1:T(2,128)(2,1)S(1)} all-to-all(bf16[2,768,256]{2,0,1:T(2,128)(2,1)S(1)} %copy.119), channel_id=1, replica_groups=mesh['seq'=32,'mp'=4] {'seq'}, dimensions={1} | all-to-all | bytes 1572864 | tf_op jit(solution)/shard_map/all_to_all | solution.py:112
  204.4 1.0 copy.120
  205.4 31.4 %all-gather.14.cloned.1.call-done = bf16[32,8,24,256]{3,2,0,1:T(8,128)(2,1)} async-done(((bf16[32,2,24,256]{3,2,0,1:T(8,128)(2,1)}), bf16[32,8,24,256]{3,2,0,1:T(8,128)(2,1)}) %all-gather.14.cloned.1.call-update) | async-done | bytes 3145744 | tf_op jit(solution)/shard_map/all_gather | solution.py:114
  236.8 2.3 copy.121
  239.5 2.6 collective-permute-start
  242.1 6.5 %collective-permute-done = bf16[125,256]{1,0:T(8,128)(2,1)S(1)} collective-permute-done((bf16[125,256]{1,0:T(8,128)(2,1)S(1)}, bf16[125,256]{1,0:T(8,128)(2,1)S(1)}, u32[]{:S(2)}, u32[]{:S(2)}) %collective-permute-start) | collective-permute-done | bytes 64032 | tf_op jit(solution)/shard_map/ppermute | solution.py:30
  248.7 1.1 add_convert_fusion
  249.8 1.5 copy.123
  251.3 2.7 %reshape.238 = bf16[3000,256]{1,0:T(8,128)(2,1)} reshape(bf16[24,125,256]{2,1,0:T(8,128)(2,1)} %copy.123) | data formatting | bytes 3072000 | tf_op jit(solution)/shard_map/reshape | solution.py:122
  (75 shorter events, 6.8 us)
Async XLA Ops:
  6.5 9.1 %copy-start = (bf16[24,250,256]{2,0,1:T(8,128)(2,1)S(1)}, bf16[24,250,256]{2,0,1:T(8,128)(2,1)}, u32[]{:S(2)}) copy-start(bf16[24,250,256]{2,0,1:T(8,128)(2,1)} %param.13) | copy-start | bytes 9216004
  6.5 5.1 %copy-start.11 = (bf16[256,3,64]{0,2,1:T(8,128)(2,1)S(1)}, bf16[256,3,64]{0,2,1:T(8,128)(2,1)}, u32[]{:S(2)}) copy-start(bf16[256,3,64]{0,2,1:T(8,128)(2,1)} %param.18) | copy-start | bytes 294916
  6.5 31.3 %all-gather.10.cloned.1.call-start = ((), (), s32[]{:S(2)}) async-start(), calls=%async_computation.3 | async-start | bytes 1966080 | tf_op jit(solution)/shard_map/all_gather | solution.py:19
  11.5 69.6 %all-gather.12.cloned.1.call-start = ((), (), s32[]{:S(2)}) async-start(), calls=%async_computation.4 | async-start | bytes 1966080 | tf_op jit(solution)/shard_map/all_gather | solution.py:19
  15.6 97.6 %all-gather.8.cloned.1.call-start = ((), (), s32[]{:S(2)}) async-start(), calls=%async_computation.2 | async-start | bytes 3932160 | tf_op jit(solution)/shard_map/all_gather | solution.py:97
  15.9 1.0 copy-start.2
  39.8 1.4 copy-start.5
  41.2 3.2 %copy-start.3 = (bf16[6,250,256]{2,0,1:T(8,128)(2,1)S(1)}, bf16[6,250,256]{2,0,1:T(8,128)(2,1)}, u32[]{:S(2)}) copy-start(bf16[6,250,256]{2,0,1:T(8,128)(2,1)} %copy-done.2) | copy-start | bytes 2304004
  45.4 1.5 slice-start.2
  45.4 1.6 copy-start.6
  76.0 2.3 copy-start.10
  120.3 9.3 %copy-start.4 = (bf16[4,196608]{1,0:T(4,128)(2,1)S(1)}, bf16[4,196608]{1,0:T(4,128)(2,1)}, u32[]{:S(2)}) copy-start(bf16[4,196608]{1,0:T(4,128)(2,1)} %reshape.243) | copy-start | bytes 4718596
  121.9 20.4 %all-to-all-start = ((bf16[64,24,256]{2,1,0:T(8,128)(2,1)}), bf16[64,24,256]{2,1,0:T(8,128)(2,1)S(1)}, u32[]{:S(2)}, u32[]{:S(2)}) async-start(bf16[64,24,256]{2,1,0:T(8,128)(2,1)} %bitcast.31), calls=%async_computation | async-start | bytes 1572864 | tf_op jit(solution)/shard_map/all_to_all | solution.py:108
  129.4 1.4 slice-start
  129.4 107.4 %all-gather.14.cloned.1.call-start = ((), (), s32[]{:S(2)}) async-start(), calls=%async_computation.5 | async-start | bytes 3932160 | tf_op jit(solution)/shard_map/all_gather | solution.py:114
  130.8 1.3 slice-start.1
  131.5 1.1 copy-start.7
  182.2 1.9 copy-start.8
  182.2 1.9 copy-start.9
  239.5 9.2 %collective-permute-start = (bf16[125,256]{1,0:T(8,128)(2,1)S(1)}, bf16[125,256]{1,0:T(8,128)(2,1)S(1)}, u32[]{:S(2)}, u32[]{:S(2)}) collective-permute-start(bf16[125,256]{1,0:T(8,128)(2,1)S(1)} %bitcast.251), channel_id=1, source_target_pairs={{0,4},{4,8},{8,12},{12,16},{16,20},{20,24},{24,28},{28,32},{32,36}... | collective-permute-start | bytes 192008 | tf_op jit(solution)/shard_map/ppermute | solution.py:30
  249.8 4.2 %copy-start.1 = (bf16[24,250,256]{2,0,1:T(8,128)(2,1)S(1)}, bf16[24,250,256]{2,0,1:T(8,128)(2,1)}, u32[]{:S(2)}) copy-start(bf16[24,250,256]{2,0,1:T(8,128)(2,1)} %param.13) | copy-start | bytes 9216004
Sparse Core Ops, SparseCore 0:
  11.7 26.1 all-gather.9
  39.5 23.1 all-gather.11
  81.2 31.9 all-gather.7
  205.6 31.2 all-gather.13
where the time goes:
time: 262 us; the launch traced here: 261 us
  waiting for transfers between devices  94.7 us (36%)
  matrix products  73.9 us (28%)
  local copies, waits for them, and re-layouts  44.2 us (17%)
  blocking collectives  17.8 us (7%)
  between operations  13.7 us (5%)
  starting transfers between devices  10.4 us (4%)
  other arithmetic  5.78 us (2%)
    dot_general x8, matrix products, attend(): jnp.einsum('bhqk,bkhe->bqhe', weights, value_rows, preferred_element_type...  34.2 us
    all_gather x1, waiting for transfers between devices, on_device(): collected = lax.all_gather(returned, 'mp', axis=1, tiled=True)  31.4 us
    sub x8, matrix products, attend(): scores = scores - jnp.max(scores, axis=-1, keepdims=True)  29.9 us
    all_gather x1, waiting for transfers between devices, on_device(): stream = lax.all_gather(finished, 'mp', axis=0, tiled=True)  28.9 us
    all_gather x2, waiting for transfers between devices, gather_together(): lines, at, done = (lax.all_gather(vector, axis), 0, [])  20.4 us
    all_to_all x1, blocking collectives, on_device(): lax.all_to_all(spread_rows, 'seq', split_axis=1, concat_axis=0, tiled=True)  17.8 us
    unnamed x36, local copies, waits for them, and re-layouts  9.77 us
    all_to_all x1, starting transfers between devices, on_device(): lax.all_to_all(mine, 'seq', split_axis=0, concat_axis=1, tiled=True)  7.49 us
  transfers between devices with their start and end apart: 6, of which 5 were waited for; matrix products, arithmetic and copies ran while one was open for 22% of the time, Pallas kernels for 0%

commit v1 on v0

v1 whole, which is shorter than its diff:
```python
import jax
import jax.numpy as jnp
from jax import lax
from jax.experimental import pallas as pl
from jax.experimental.pallas import tpu as pltpu
from jax.sharding import PartitionSpec as P

HEADS = 8
HD = 32
K = 250
HALF = K // 2
D = 256
MP = 4
BF = jnp.bfloat16
F32 = jnp.float32
Q_SCALE = 1.4426950408889634 * HD ** (-0.5)
LOW = -1e30
VMEM_BYTES = 56 * 1024 * 1024


def params(**more):
    return pltpu.CompilerParams(vmem_limit_bytes=VMEM_BYTES, **more)


def dot(left, right, left_dim=1, right_dim=0):
    return lax.dot_general(
        left, right, (((left_dim,), (right_dim,)), ((), ())), preferred_element_type=F32
    )


def normed(values):
    centre = values - jnp.mean(values, axis=-1, keepdims=True)
    spread = jnp.mean(centre * centre, axis=-1, keepdims=True)
    return (centre * lax.rsqrt(spread + 1e-05)).astype(BF)


def pack_attention(qkv_ref, out_ref, packed_ref):
    for t in range(3):
        packed_ref[64 * t : 64 * t + 64, :] = qkv_ref[:, t, :].astype(F32).T.astype(BF)
    packed_ref[192:256, :] = out_ref[...]


def pack_rest(up1_ref, down1_ref, qkv_ref, out_ref, up2_ref, down2_ref, packed_ref):
    packed_ref[0:256, :] = up1_ref[...]
    packed_ref[256:512, :] = down1_ref[...]
    for t in range(3):
        packed_ref[512 + 64 * t : 576 + 64 * t, :] = qkv_ref[:, t, :].astype(F32).T.astype(BF)
    packed_ref[704:768, :] = out_ref[...]
    packed_ref[768:1024, :] = up2_ref[...]
    packed_ref[1024:1280, :] = down2_ref[...]


def put_attention_weights(shards, at, weights_ref):
    for k in range(MP):
        for t in range(4):
            weights_ref[t, 64 * k : 64 * k + 64, :] = shards[k][at + 64 * t : at + 64 * t + 64, :]


def project(rows, weights_ref, query_ref, key_ref, value_ref):
    query_ref[...] = (dot(weights_ref[0], rows, 1, 1) * Q_SCALE).astype(BF)
    keys = dot(rows, weights_ref[1], 1, 1).astype(BF)
    lane = lax.broadcasted_iota(jnp.int32, (rows.shape[0], 128), 1) // HD
    for h in range(HEADS):
        part = keys[:, 128 * (h // 4) : 128 * (h // 4) + 128]
        key_ref[h] = jnp.where(lane == h % 4, part, jnp.zeros_like(part))
    values = dot(weights_ref[2], rows, 1, 1).astype(BF)
    for h in range(HEADS):
        value_ref[h, 0:HD, :] = values[HD * h : HD * h + HD, :]
        value_ref[h, HD:48, :] = jnp.ones((48 - HD, rows.shape[0]), BF)


def attend(columns, query_ref, key_ref, value_ref, attended_ref, valid=None):
    def scores(h):
        at = 128 * (h // 4)
        found = dot(key_ref[h], query_ref[at : at + 128, columns])
        return found if valid is None else jnp.where(valid, found, LOW)

    following = scores(0)
    for h in range(HEADS):
        current = following
        if h + 1 < HEADS:
            following = scores(h + 1)
        top = jnp.max(current, axis=0, keepdims=True)
        weights = jnp.exp2(current - top).astype(BF)
        mixed = dot(value_ref[h], weights)
        attended_ref[HD * h : HD * h + HD, columns] = mixed[0:HD] * (1.0 / mixed[HD : HD + 1])


def intra_attention(x_ref, w0, w1, w2, w3, o_ref, weights_ref, query_ref, key_ref, value_ref, attended_ref):
    @pl.when(pl.program_id(0) == 0)
    def _():
        put_attention_weights((w0, w1, w2, w3), 0, weights_ref)

    x = x_ref[0].astype(F32)
    project(normed(x), weights_ref, query_ref, key_ref, value_ref)
    place = lax.broadcasted_iota(jnp.int32, (2 * 128, 2 * 128), 0)
    valid = (place % 128) < HALF
    attend(slice(0, 256), query_ref, key_ref, value_ref, attended_ref, valid)
    attended = attended_ref[...].T.astype(BF)
    o_ref[0] = (x + dot(attended, weights_ref[3])).astype(BF)


def feed_forward(middle, up, down):
    middle = middle.astype(F32)
    rows = normed(middle)
    total = middle
    for u, d in zip(up, down):
        hidden = jnp.maximum(dot(rows, u), 0.0).astype(BF)
        total = total + dot(hidden, d)
    return total.astype(BF)


def intra_feed_forward(x_ref, w0, w1, w2, w3, o_ref):
    shards = (w0, w1, w2, w3)
    o_ref[0] = feed_forward(
        x_ref[0], [w[0:256, :] for w in shards], [w[256:512, :] for w in shards]
    )


def inter_layer(x_ref, w0, w1, w2, w3, o_ref, weights_ref, query_ref, key_ref, value_ref, attended_ref, later_ref):
    shards = (w0, w1, w2, w3)
    step = pl.program_id(0)

    @pl.when(step == 0)
    def _():
        put_attention_weights(shards, 512, weights_ref)

    x = x_ref[0].astype(F32)
    project(normed(x), weights_ref, query_ref, key_ref, value_ref)

    def block(i, carry):
        columns = pl.ds(pl.multiple_of(i * 256, 256), 256)
        attend(columns, query_ref, key_ref, value_ref, attended_ref)
        return carry

    lax.fori_loop(0, x.shape[0] // 256, block, 0)
    attended = attended_ref[...].T.astype(BF)
    middle = (x + dot(attended, weights_ref[3])).astype(BF)
    done = feed_forward(
        middle, [w[768:1024, :] for w in shards], [w[1024:1280, :] for w in shards]
    ).astype(F32)

    @pl.when(step == 0)
    def _():
        later_ref[128:768, :] = done[0:640]
        turned = pltpu.roll(done[640:768], 1, 0)
        first = lax.broadcasted_iota(jnp.int32, turned.shape, 0) == 0
        later_ref[0:128, :] = jnp.where(first, 0.0, turned)

    @pl.when(step == 1)
    def _():
        o_ref[...] = (done + later_ref[...]).astype(BF)


def whole(shape):
    return pl.BlockSpec(shape, lambda i: (0,) * len(shape))


def attention_scratch(length):
    return [
        pltpu.VMEM((4, D, D), BF),
        pltpu.VMEM((D, length), BF),
        pltpu.VMEM((HEADS, length, 128), BF),
        pltpu.VMEM((HEADS, 48, length), BF),
        pltpu.VMEM((D, length), F32),
    ]


def by(shard, k):
    return lax.ppermute(shard, "mp", [(i, i ^ k) for i in range(MP)])


def on_device(
    frames, intra_qkv, intra_out, intra_up, intra_down, inter_qkv, inter_out, inter_up, inter_down
):
    seq_count = lax.axis_size("seq")
    mine = lax.axis_index("mp")
    spans = frames.shape[0] // MP
    total = spans * seq_count * MP

    first = pl.pallas_call(
        pack_attention, out_shape=jax.ShapeDtypeStruct((256, D), BF), name="pack_first"
    )(intra_qkv, intra_out)
    first = [first, by(first, 1), by(first, 2), by(first, 3)]
    rest = pl.pallas_call(
        pack_rest, out_shape=jax.ShapeDtypeStruct((1280, D), BF), name="pack_rest"
    )(intra_up, intra_down, inter_qkv, inter_out, inter_up, inter_down)
    across = by(rest, 2)
    rest = [rest, by(rest, 1), across, by(across, 1)]

    own = lax.dynamic_slice_in_dim(frames, mine * spans, spans, 0)
    own = jnp.pad(own.reshape(spans, 2, HALF, D), ((0, 0), (0, 0), (0, 3), (0, 0)))
    own = own.reshape(spans, 256, D)

    row_block = pl.BlockSpec((1, 256, D), lambda i: (i, 0, 0))
    middle = pl.pallas_call(
        intra_attention,
        out_shape=jax.ShapeDtypeStruct(own.shape, BF),
        grid=(spans,),
        in_specs=[row_block] + [whole((256, D))] * 4,
        out_specs=row_block,
        scratch_shapes=attention_scratch(256),
        compiler_params=params(),
        cost_estimate=pl.CostEstimate(flops=10**10, bytes_accessed=2 * 10**6, transcendentals=3 * 10**6),
        name="intra_attention",
    )(own, *first)
    stream = pl.pallas_call(
        intra_feed_forward,
        out_shape=jax.ShapeDtypeStruct(own.shape, BF),
        grid=(spans,),
        in_specs=[row_block] + [whole((512, D))] * 4,
        out_specs=row_block,
        compiler_params=params(),
        cost_estimate=pl.CostEstimate(flops=3 * 10**9, bytes_accessed=3 * 10**6, transcendentals=0),
        name="intra_feed_forward",
    )(middle, *rest)

    send = stream.reshape(spans, 2, MP, seq_count, D)
    send = jnp.transpose(send, (3, 2, 1, 0, 4)).reshape(seq_count * MP, 2 * spans, D)
    got = lax.all_to_all(send, ("seq", "mp"), split_axis=0, concat_axis=0, tiled=True)
    got = jnp.transpose(got.reshape(seq_count * MP, 2, spans, D), (1, 2, 0, 3))
    got = got.reshape(2, total, D)

    summed = pl.pallas_call(
        inter_layer,
        out_shape=jax.ShapeDtypeStruct((total, D), BF),
        grid=(2,),
        in_specs=[pl.BlockSpec((1, total, D), lambda i: (1 - i, 0, 0))] + [whole((1280, D))] * 4,
        out_specs=whole((total, D)),
        scratch_shapes=attention_scratch(total) + [pltpu.VMEM((total, D), F32)],
        compiler_params=params(),
        cost_estimate=pl.CostEstimate(flops=3 * 10**10, bytes_accessed=4 * 10**6, transcendentals=10**7),
        name="inter_layer",
    )(got, *rest)

    back = jnp.transpose(summed.reshape(spans, seq_count, MP, D), (1, 2, 0, 3))
    back = back.reshape(seq_count, MP * spans, D)
    back = lax.all_to_all(back, "seq", split_axis=0, concat_axis=0, tiled=True)
    back_across = by(back, 2)
    pieces = [back, by(back, 1), back_across, by(back_across, 1)]
    for bit in (1, 2):
        swapped = (mine & bit) > 0
        pieces = [jnp.where(swapped, pieces[k ^ bit], pieces[k]) for k in range(MP)]
    rows = jnp.transpose(jnp.stack(pieces), (2, 0, 1, 3)).reshape(MP * spans, MP * seq_count, D)
    return rows[:, :HALF].reshape(-1, D)


def solution(mesh):
    return jax.shard_map(
        on_device,
        mesh=mesh,
        in_specs=(
            P("seq", None, None),
            P(None, None, "mp"),
            P("mp", None),
            P(None, "mp"),
            P("mp", None),
            P(None, None, "mp"),
            P("mp", None),
            P(None, "mp"),
            P("mp", None),
        ),
        out_specs=P("seq", None),
        check_vma=False,
    )
```

time: 262 us -> 146 us (0.56)
  the two profiles are of different devices: /device:TPU:8 before, /device:TPU:1 now
where the time goes in v1:
time: 146 us
  Pallas kernels  47.4 us (32%)
  blocking collectives  41.4 us (28%)
  waiting for transfers between devices  18.7 us (13%)
  local copies, waits for them, and re-layouts  18.2 us (12%)
  starting transfers between devices  17.3 us (12%)
  other arithmetic  2.76 us (2%)
    all_to_all x1, blocking collectives, on_device(): lax.all_to_all(send, ('seq', 'mp'), split_axis=0, concat_axis=0, tiled=True)  28.5 us
    pallas_call x1, Pallas kernels, on_device(): pl.pallas_call(inter_layer, out_shape=jax.ShapeDtypeStruct((total, D), BF...  22.3 us
    ppermute x9, waiting for transfers between devices, by(): return lax.ppermute(shard, 'mp', [(i, i ^ k) for i in range(MP)])  18.7 us
    ppermute x9, starting transfers between devices, by(): return lax.ppermute(shard, 'mp', [(i, i ^ k) for i in range(MP)])  17.3 us
    pallas_call x1, Pallas kernels, on_device(): pl.pallas_call(intra_attention, out_shape=jax.ShapeDtypeStruct(own.shape,...  13.9 us
    all_to_all x1, blocking collectives, on_device(): back = lax.all_to_all(back, 'seq', split_axis=0, concat_axis=0, tiled=True)  12.9 us
    pallas_call x1, Pallas kernels, on_device(): pl.pallas_call(intra_feed_forward, out_shape=jax.ShapeDtypeStruct(own.sha...  6.77 us
    unnamed x14, local copies, waits for them, and re-layouts  4.28 us
  transfers between devices with their start and end apart: 9, of which 5 were waited for; matrix products, arithmetic and copies ran while one was open for 2% of the time, Pallas kernels for 11%

profile of v1, /device:TPU:1, one launch (start us, length us, event | category | flops | bytes accessed | tf_op | source)
XLA Modules:
  0.0 145.7 jit_solution(14189544270721133473)
XLA Ops:
  0.0 0.0 copy-start
  0.0 0.0 copy-start.1
  0.0 1.9 %copy.43.qkv_ref = bf16[256,3,64]{2,1,0:T(4,128)(2,1)} copy(bf16[256,3,64]{0,2,1:T(8,128)(2,1)} %param.14) | data formatting | bytes 196608 | tf_op args[5]
  1.9 2.4 %pack_rest.1.w0 = bf16[1280,256]{1,0:T(8,128)(2,1)} custom-call(bf16[256,256]{1,0:T(8,128)(2,1)} %up1_ref.1, bf16[256,256]{1,0:T(8,128)(2,1)} %down1_ref.1, bf16[256,3,64]{2,1,0:T(4,128)(2,1)} %copy.43.qkv_ref, bf16[64,256]{1,0:T(8,128)(2,1)} %out_ref.3, bf16[256,256]{1,0:T(8,128)(2,1)} %up2_ref.1, bf16[256,256]{1,0:T(8,128)(2,1)} %down2_ref.1), custom_call_target="tpu_custom_call" | custom-call | tf_op jit(solution)/shard_map/pack_rest/pallas_call | solution.py:185
  4.4 4.4 %collective-permute-start.4 = (bf16[1280,256]{1,0:T(8,128)(2,1)}, bf16[1280,256]{1,0:T(8,128)(2,1)}, u32[]{:S(2)}, u32[]{:S(2)}) collective-permute-start(bf16[1280,256]{1,0:T(8,128)(2,1)} %pack_rest.1.w0), channel_id=1, source_target_pairs={{0,2},{1,3},{2,0},{3,1},{4,6},{5,7},{6,4},{7,5},{8,10},{9,11},{10,... | collective-permute-start | bytes 1966088 | tf_op jit(solution)/shard_map/ppermute | solution.py:170
  8.8 0.0 copy-done.1
  8.8 0.9 copy.42.qkv_ref
  9.7 2.0 %pack_first.1.w0 = bf16[256,256]{1,0:T(8,128)(2,1)} custom-call(bf16[256,3,64]{2,1,0:T(4,128)(2,1)} %copy.42.qkv_ref, bf16[64,256]{1,0:T(8,128)(2,1)} %out_ref.2), custom_call_target="tpu_custom_call" | custom-call | tf_op jit(solution)/shard_map/pack_first/pallas_call | solution.py:181
  11.7 1.0 collective-permute-start
  12.6 0.0 collective-permute-start.1
  12.6 3.1 %collective-permute-start.2 = (bf16[256,256]{1,0:T(8,128)(2,1)}, bf16[256,256]{1,0:T(8,128)(2,1)S(1)}, u32[]{:S(2)}, u32[]{:S(2)}) collective-permute-start(bf16[256,256]{1,0:T(8,128)(2,1)} %pack_first.1.w0), channel_id=1, source_target_pairs={{0,3},{1,2},{2,1},{3,0},{4,7},{5,6},{6,5},{7,4},{8,11},{9,10},{10,... | collective-permute-start | bytes 393224 | tf_op jit(solution)/shard_map/ppermute | solution.py:170
  15.8 0.2 collective-permute-start.3
  16.0 0.0 copy-done
  16.0 0.3 constant_dynamic-slice_fusion
  16.3 0.2 copy.56
  16.5 0.9 pad.4
  17.4 6.2 %collective-permute-done.4.w2 = bf16[1280,256]{1,0:T(8,128)(2,1)} collective-permute-done((bf16[1280,256]{1,0:T(8,128)(2,1)}, bf16[1280,256]{1,0:T(8,128)(2,1)}, u32[]{:S(2)}, u32[]{:S(2)}) %collective-permute-start.4) | collective-permute-done | bytes 655392 | tf_op jit(solution)/shard_map/ppermute | solution.py:170
  23.6 2.1 %collective-permute-start.5 = (bf16[1280,256]{1,0:T(8,128)(2,1)}, bf16[1280,256]{1,0:T(8,128)(2,1)S(1)}, u32[]{:S(2)}, u32[]{:S(2)}) collective-permute-start(bf16[1280,256]{1,0:T(8,128)(2,1)} %collective-permute-done.4.w2), channel_id=1, source_target_pairs={{0,1},{1,0},{2,3},{3,2},{4,5},{5,4},{6,7},{7,6},{8,9},{9,8},{10,11... | collective-permute-start | bytes 1966088 | tf_op jit(solution)/shard_map/ppermute | solution.py:170
  25.6 0.0 collective-permute-done.w1
  25.6 0.0 copy-start.3
  25.6 0.6 collective-permute-done.1.w2
  26.3 0.0 copy-start.4
  26.3 3.3 %collective-permute-done.2.w3 = bf16[256,256]{1,0:T(8,128)(2,1)S(1)} collective-permute-done((bf16[256,256]{1,0:T(8,128)(2,1)}, bf16[256,256]{1,0:T(8,128)(2,1)S(1)}, u32[]{:S(2)}, u32[]{:S(2)}) %collective-permute-start.2) | collective-permute-done | bytes 131104 | tf_op jit(solution)/shard_map/ppermute | solution.py:170
  29.6 0.0 copy-start.5
  29.6 0.0 copy-done.3
  29.6 0.0 copy-done.4
  29.6 0.6 copy-done.5
  30.3 13.9 %intra_attention.1.x_ref = bf16[6,256,256]{2,1,0:T(8,128)(2,1)} custom-call(bf16[6,256,256]{2,1,0:T(8,128)(2,1)} %bitcast.39, bf16[256,256]{1,0:T(8,128)(2,1)} %pack_first.1.w0, bf16[256,256]{1,0:T(8,128)(2,1)} %copy-done.3, bf16[256,256]{1,0:T(8,128)(2,1)} %copy-done.4, bf16[256,256]{1,0:T(8,128)(2,1)} %copy-done.5), custom_call_target="tpu_custom_call" | custom-call | flops 10000000000 | bytes 2000000 | tf_op jit(solution)/shard_map/intra_attention/pallas_call | solution.py:196
  44.1 0.0 collective-permute-done.3.w1
  44.1 0.0 collective-permute-done.5.w3
  44.1 0.0 copy-start.2
  44.1 0.8 copy-done.2
  45.0 6.8 %intra_feed_forward.1 = bf16[6,256,256]{2,1,0:T(8,128)(2,1)} custom-call(bf16[6,256,256]{2,1,0:T(8,128)(2,1)} %intra_attention.1.x_ref, bf16[1280,256]{1,0:T(8,128)(2,1)} %pack_rest.1.w0, bf16[1280,256]{1,0:T(8,128)(2,1)} %collective-permute-done.3.w1, bf16[1280,256]{1,0:T(8,128)(2,1)} %collective-permute-done.4.w2, bf16[1280,256]{1,0:T(8,128)(2,1)} %copy-done.2), custom_call_target="tpu_custom_call" | custom-call | flops 3000000000 | bytes 3000000 | tf_op jit(solution)/shard_map/intra_feed_forward/pallas_call | solution.py:207
  51.7 2.7 %copy.62 = bf16[6,2,4,32,256]{4,2,3,0,1:T(4,128)(2,1)} copy(bf16[6,2,4,32,256]{4,3,2,1,0:T(8,128)(2,1)} %bitcast.40) | data formatting | bytes 1572864 | tf_op jit(solution)/shard_map/reshape | solution.py:218
  54.4 2.3 %reshape.33 = bf16[128,12,256]{2,0,1:T(8,128)(2,1)} reshape(bf16[32,4,2,6,256]{4,1,0,3,2:T(4,128)(2,1)} %bitcast.36) | data formatting | bytes 1572864 | tf_op jit(solution)/shard_map/reshape | solution.py:219
  56.6 1.6 %copy.45 = bf16[128,12,256]{2,1,0:T(8,128)(2,1)S(1)} copy(bf16[128,12,256]{2,0,1:T(8,128)(2,1)} %reshape.33) | data formatting | bytes 1572864 | tf_op jit(solution)/shard_map/reshape | solution.py:219
  58.2 28.5 %all_to_all.10 = bf16[128,12,256]{2,1,0:T(8,128)(2,1)S(1)} all-to-all(bf16[128,12,256]{2,1,0:T(8,128)(2,1)S(1)} %copy.45), channel_id=1, replica_groups=mesh['seq'=32,'mp'=4] {'seq','mp'}, dimensions={0} | all-to-all | bytes 1572864 | tf_op jit(solution)/shard_map/all_to_all | solution.py:220
  86.7 1.1 copy.46
  87.8 22.3 %inter_layer.1 = bf16[768,256]{1,0:T(8,128)(2,1)} custom-call(bf16[2,768,256]{2,1,0:T(8,128)(2,1)} %bitcast.38, bf16[1280,256]{1,0:T(8,128)(2,1)} %pack_rest.1.w0, bf16[1280,256]{1,0:T(8,128)(2,1)} %collective-permute-done.3.w1, bf16[1280,256]{1,0:T(8,128)(2,1)} %collective-permute-done.4.w2, bf16[1280,256]{1,0:T(8,128)(2,1)} %copy-done.2), custom_call_target="tpu_custom_call" | custom-call | flops 30000001024 | bytes 4000000 | tf_op jit(solution)/shard_map/inter_layer/pallas_call | solution.py:224
  110.1 1.1 reshape.36
  111.2 0.1 copy.47
  111.3 0.2 copy.48
  111.5 12.9 %all_to_all.11 = bf16[32,24,256]{2,1,0:T(8,128)(2,1)S(1)} all-to-all(bf16[32,24,256]{2,1,0:T(8,128)(2,1)S(1)} %copy.48), channel_id=1, replica_groups=mesh['seq'=32,'mp'=4] {'seq'}, dimensions={0} | all-to-all | bytes 786432 | tf_op jit(solution)/shard_map/all_to_all | solution.py:238
  124.4 0.8 copy.49
  125.3 0.9 collective-permute-start.6
  126.2 2.5 %collective-permute-start.8 = (bf16[32,24,256]{2,0,1:T(8,128)(2,1)}, bf16[32,24,256]{2,0,1:T(8,128)(2,1)}, u32[]{:S(2)}, u32[]{:S(2)}) collective-permute-start(bf16[32,24,256]{2,0,1:T(8,128)(2,1)} %copy.49), channel_id=1, source_target_pairs={{0,1},{1,0},{2,3},{3,2},{4,5},{5,4},{6,7},{7,6},{8,9},{9,8},{10,11... | collective-permute-start | bytes 1179656 | tf_op jit(solution)/shard_map/ppermute | solution.py:170
  128.7 6.9 %collective-permute-done.6 = bf16[32,24,256]{2,0,1:T(8,128)(2,1)} collective-permute-done((bf16[32,24,256]{2,0,1:T(8,128)(2,1)}, bf16[32,24,256]{2,0,1:T(8,128)(2,1)}, u32[]{:S(2)}, u32[]{:S(2)}) %collective-permute-start.6) | collective-permute-done | bytes 393248 | tf_op jit(solution)/shard_map/ppermute | solution.py:170
  135.5 3.1 %collective-permute-start.7 = (bf16[32,24,256]{2,0,1:T(8,128)(2,1)}, bf16[32,24,256]{2,0,1:T(8,128)(2,1)}, u32[]{:S(2)}, u32[]{:S(2)}) collective-permute-start(bf16[32,24,256]{2,0,1:T(8,128)(2,1)} %collective-permute-done.6), channel_id=1, source_target_pairs={{0,1},{1,0},{2,3},{3,2},{4,5},{5,4},{6,7},{7,6},{8,9},{9,8},{10,11... | collective-permute-start | bytes 1179656 | tf_op jit(solution)/shard_map/ppermute | solution.py:170
  138.6 0.0 collective-permute-done.8
  138.6 1.7 %collective-permute-done.7 = bf16[32,24,256]{2,0,1:T(8,128)(2,1)} collective-permute-done((bf16[32,24,256]{2,0,1:T(8,128)(2,1)}, bf16[32,24,256]{2,0,1:T(8,128)(2,1)}, u32[]{:S(2)}, u32[]{:S(2)}) %collective-permute-start.7) | collective-permute-done | bytes 393248 | tf_op jit(solution)/shard_map/ppermute | solution.py:170
  140.3 1.4 select_bitcast_fusion.3
  141.7 1.4 pad_maximum_fusion
  143.1 2.7 %reshape.39 = bf16[3000,256]{1,0:T(8,128)(2,1)} reshape(bf16[24,125,256]{2,1,0:T(8,128)(2,1)} %bitcast.34) | data formatting | bytes 3072000 | tf_op jit(solution)/shard_map/reshape | solution.py:245
Async XLA Ops:
  0.0 16.0 %copy-start = (bf16[24,250,256]{2,0,1:T(8,128)(2,1)S(1)}, bf16[24,250,256]{2,0,1:T(8,128)(2,1)}, u32[]{:S(2)}) copy-start(bf16[24,250,256]{2,0,1:T(8,128)(2,1)} %param.9) | copy-start | bytes 9216004
  0.0 8.8 %copy-start.1 = (bf16[256,3,64]{0,2,1:T(8,128)(2,1)S(1)}, bf16[256,3,64]{0,2,1:T(8,128)(2,1)}, u32[]{:S(2)}) copy-start(bf16[256,3,64]{0,2,1:T(8,128)(2,1)} %param.10) | copy-start | bytes 294916
  4.4 19.2 %collective-permute-start.4 = (bf16[1280,256]{1,0:T(8,128)(2,1)}, bf16[1280,256]{1,0:T(8,128)(2,1)}, u32[]{:S(2)}, u32[]{:S(2)}) collective-permute-start(bf16[1280,256]{1,0:T(8,128)(2,1)} %pack_rest.1.w0), channel_id=1, source_target_pairs={{0,2},{1,3},{2,0},{3,1},{4,6},{5,7},{6,4},{7,5},{8,10},{9,11},{10,... | collective-permute-start | bytes 1966088 | tf_op jit(solution)/shard_map/ppermute | solution.py:170
  11.7 14.0 %collective-permute-start = (bf16[256,256]{1,0:T(8,128)(2,1)}, bf16[256,256]{1,0:T(8,128)(2,1)S(1)}, u32[]{:S(2)}, u32[]{:S(2)}) collective-permute-start(bf16[256,256]{1,0:T(8,128)(2,1)} %pack_first.1.w0), channel_id=1, source_target_pairs={{0,1},{1,0},{2,3},{3,2},{4,5},{5,4},{6,7},{7,6},{8,9},{9,8},{10,11... | collective-permute-start | bytes 393224 | tf_op jit(solution)/shard_map/ppermute | solution.py:170
  12.6 13.6 %collective-permute-start.1 = (bf16[256,256]{1,0:T(8,128)(2,1)}, bf16[256,256]{1,0:T(8,128)(2,1)S(1)}, u32[]{:S(2)}, u32[]{:S(2)}) collective-permute-start(bf16[256,256]{1,0:T(8,128)(2,1)} %pack_first.1.w0), channel_id=1, source_target_pairs={{0,2},{1,3},{2,0},{3,1},{4,6},{5,7},{6,4},{7,5},{8,10},{9,11},{10,... | collective-permute-start | bytes 393224 | tf_op jit(solution)/shard_map/ppermute | solution.py:170
  12.6 17.0 %collective-permute-start.2 = (bf16[256,256]{1,0:T(8,128)(2,1)}, bf16[256,256]{1,0:T(8,128)(2,1)S(1)}, u32[]{:S(2)}, u32[]{:S(2)}) collective-permute-start(bf16[256,256]{1,0:T(8,128)(2,1)} %pack_first.1.w0), channel_id=1, source_target_pairs={{0,3},{1,2},{2,1},{3,0},{4,7},{5,6},{6,5},{7,4},{8,11},{9,10},{10,... | collective-permute-start | bytes 393224 | tf_op jit(solution)/shard_map/ppermute | solution.py:170
  15.8 28.4 %collective-permute-start.3 = (bf16[1280,256]{1,0:T(8,128)(2,1)}, bf16[1280,256]{1,0:T(8,128)(2,1)}, u32[]{:S(2)}, u32[]{:S(2)}) collective-permute-start(bf16[1280,256]{1,0:T(8,128)(2,1)} %pack_rest.1.w0), channel_id=1, source_target_pairs={{0,1},{1,0},{2,3},{3,2},{4,5},{5,4},{6,7},{7,6},{8,9},{9,8},{10,11... | collective-permute-start | bytes 1966088 | tf_op jit(solution)/shard_map/ppermute | solution.py:170
  23.6 20.6 %collective-permute-start.5 = (bf16[1280,256]{1,0:T(8,128)(2,1)}, bf16[1280,256]{1,0:T(8,128)(2,1)S(1)}, u32[]{:S(2)}, u32[]{:S(2)}) collective-permute-start(bf16[1280,256]{1,0:T(8,128)(2,1)} %collective-permute-done.4.w2), channel_id=1, source_target_pairs={{0,1},{1,0},{2,3},{3,2},{4,5},{5,4},{6,7},{7,6},{8,9},{9,8},{10,11... | collective-permute-start | bytes 1966088 | tf_op jit(solution)/shard_map/ppermute | solution.py:170
  25.6 4.0 %copy-start.3 = (bf16[256,256]{1,0:T(8,128)(2,1)}, bf16[256,256]{1,0:T(8,128)(2,1)S(1)}, u32[]{:S(2)}) copy-start(bf16[256,256]{1,0:T(8,128)(2,1)S(1)} %collective-permute-done.w1) | copy-start | bytes 393220
  26.3 3.4 %copy-start.4 = (bf16[256,256]{1,0:T(8,128)(2,1)}, bf16[256,256]{1,0:T(8,128)(2,1)S(1)}, u32[]{:S(2)}) copy-start(bf16[256,256]{1,0:T(8,128)(2,1)S(1)} %collective-permute-done.1.w2) | copy-start | bytes 393220
  29.6 0.7 copy-start.5
  44.1 0.8 copy-start.2
  125.3 10.3 %collective-permute-start.6 = (bf16[32,24,256]{2,0,1:T(8,128)(2,1)}, bf16[32,24,256]{2,0,1:T(8,128)(2,1)}, u32[]{:S(2)}, u32[]{:S(2)}) collective-permute-start(bf16[32,24,256]{2,0,1:T(8,128)(2,1)} %copy.49), channel_id=1, source_target_pairs={{0,2},{1,3},{2,0},{3,1},{4,6},{5,7},{6,4},{7,5},{8,10},{9,11},{10,... | collective-permute-start | bytes 1179656 | tf_op jit(solution)/shard_map/ppermute | solution.py:170
  126.2 12.4 %collective-permute-start.8 = (bf16[32,24,256]{2,0,1:T(8,128)(2,1)}, bf16[32,24,256]{2,0,1:T(8,128)(2,1)}, u32[]{:S(2)}, u32[]{:S(2)}) collective-permute-start(bf16[32,24,256]{2,0,1:T(8,128)(2,1)} %copy.49), channel_id=1, source_target_pairs={{0,1},{1,0},{2,3},{3,2},{4,5},{5,4},{6,7},{7,6},{8,9},{9,8},{10,11... | collective-permute-start | bytes 1179656 | tf_op jit(solution)/shard_map/ppermute | solution.py:170
  135.5 4.8 %collective-permute-start.7 = (bf16[32,24,256]{2,0,1:T(8,128)(2,1)}, bf16[32,24,256]{2,0,1:T(8,128)(2,1)}, u32[]{:S(2)}, u32[]{:S(2)}) collective-permute-start(bf16[32,24,256]{2,0,1:T(8,128)(2,1)} %collective-permute-done.6), channel_id=1, source_target_pairs={{0,1},{1,0},{2,3},{3,2},{4,5},{5,4},{6,7},{7,6},{8,9},{9,8},{10,11... | collective-permute-start | bytes 1179656 | tf_op jit(solution)/shard_map/ppermute | solution.py:170

commit v2 on v1

v2 whole, which is shorter than its diff:
```python
import jax
import jax.numpy as jnp
from jax import lax
from jax.experimental import pallas as pl
from jax.experimental.pallas import tpu as pltpu
from jax.sharding import PartitionSpec as P

HEADS = 8
HD = 32
K = 250
HALF = K // 2
D = 256
MP = 4
BF = jnp.bfloat16
F32 = jnp.float32
Q_SCALE = 1.4426950408889634 * HD ** (-0.5)
LOW = -1e30
VMEM_BYTES = 56 * 1024 * 1024


def params(**more):
    return pltpu.CompilerParams(vmem_limit_bytes=VMEM_BYTES, **more)


def dot(left, right, left_dim=1, right_dim=0):
    return lax.dot_general(
        left, right, (((left_dim,), (right_dim,)), ((), ())), preferred_element_type=F32
    )


def normed(values):
    centre = values - jnp.mean(values, axis=-1, keepdims=True)
    spread = jnp.mean(centre * centre, axis=-1, keepdims=True)
    return (centre * lax.rsqrt(spread + 1e-05)).astype(BF)


def pack_attention(qkv_ref, out_ref, packed_ref):
    for t in range(3):
        packed_ref[64 * t : 64 * t + 64, :] = qkv_ref[t].astype(F32).T.astype(BF)
    packed_ref[192:256, :] = out_ref[...]


def pack_rest(up1_ref, down1_ref, qkv_ref, out_ref, up2_ref, down2_ref, packed_ref):
    packed_ref[0:256, :] = up1_ref[...]
    packed_ref[256:512, :] = down1_ref[...]
    for t in range(3):
        packed_ref[512 + 64 * t : 576 + 64 * t, :] = qkv_ref[t].astype(F32).T.astype(BF)
    packed_ref[704:768, :] = out_ref[...]
    packed_ref[768:1024, :] = up2_ref[...]
    packed_ref[1024:1280, :] = down2_ref[...]


def put_attention_weights(shards, at, weights_ref):
    for k in range(MP):
        for t in range(4):
            weights_ref[t, 64 * k : 64 * k + 64, :] = shards[k][at + 64 * t : at + 64 * t + 64, :]


def project(rows, weights_ref, query_ref, key_ref, value_ref):
    query_ref[...] = (dot(weights_ref[0], rows, 1, 1) * Q_SCALE).astype(BF)
    keys = dot(rows, weights_ref[1], 1, 1).astype(BF)
    lane = lax.broadcasted_iota(jnp.int32, (rows.shape[0], 128), 1) // HD
    for h in range(HEADS):
        part = keys[:, 128 * (h // 4) : 128 * (h // 4) + 128]
        key_ref[h] = jnp.where(lane == h % 4, part, jnp.zeros_like(part))
    values = dot(weights_ref[2], rows, 1, 1).astype(BF)
    for h in range(HEADS):
        value_ref[h, 0:HD, :] = values[HD * h : HD * h + HD, :]
        value_ref[h, HD:48, :] = jnp.ones((48 - HD, rows.shape[0]), BF)


def attend(columns, query_ref, key_ref, value_ref, attended_ref):
    def scores(h):
        at = 128 * (h // 4)
        return dot(key_ref[h], query_ref[at : at + 128, columns])

    following = scores(0)
    for h in range(HEADS):
        current = following
        if h + 1 < HEADS:
            following = scores(h + 1)
        top = jnp.max(current, axis=0, keepdims=True)
        weights = jnp.exp2(current - top).astype(BF)
        mixed = dot(value_ref[h], weights)
        attended_ref[HD * h : HD * h + HD, columns] = mixed[0:HD] * (1.0 / mixed[HD : HD + 1])


def prepare(mine_ref, x_ref, n_ref, nq_ref, xq_ref, x_scratch, n_scratch):
    at = pl.multiple_of(mine_ref[0] * 32, 32)
    for u in range(x_ref.shape[0]):
        x = x_ref[u].astype(F32)
        centre = x - jnp.mean(x, axis=-1, keepdims=True)
        spread = jnp.mean(centre * centre, axis=-1, keepdims=True)
        for value, scratch in ((x, x_scratch), (centre * lax.rsqrt(spread + 1e-05), n_scratch)):
            scratch[u, 0:K, :] = value
            scratch[u, K:256, :] = jnp.zeros((256 - K, D), F32)
        late = n_scratch[u, HALF : HALF + 128, :]
        n_ref[u, 0:128, :] = n_scratch[u, 0:128, :].astype(BF)
        n_ref[u, 128:256, :] = late.astype(BF)
        for scratch, out_ref in ((x_scratch, xq_ref), (n_scratch, nq_ref)):
            out_ref[u, 0:32, :] = scratch[u, pl.ds(at, 32), :].astype(BF)
            late = scratch[u, HALF : HALF + 128, :]
            scratch[u, 0:128, :] = late
            out_ref[u, 32:64, :] = scratch[u, pl.ds(at, 32), :].astype(BF)


def intra_attention(n_ref, nq_ref, xq_ref, w0, w1, w2, w3, o_ref, weights_ref):
    @pl.when(pl.program_id(0) == 0)
    def _():
        put_attention_weights((w0, w1, w2, w3), 0, weights_ref)

    count = n_ref.shape[0]
    row = lax.broadcasted_iota(jnp.int32, (256, 256), 0)
    lane = lax.broadcasted_iota(jnp.int32, (256, 256), 1)
    valid = (row % 128) < HALF
    same = (row % 128) // HD == lane // 64
    keys, queries, values = [], [], []
    for u in range(count):
        rows = n_ref[u]
        few = nq_ref[u]
        keys.append(dot(rows, weights_ref[1], 1, 1).astype(BF))
        query = dot(weights_ref[0], jnp.concatenate([few] * 4, axis=0), 1, 1) * Q_SCALE
        queries.append(jnp.where(same, query, 0.0).astype(BF))
        values.append(dot(weights_ref[2], rows, 1, 1).astype(BF))
    parts = [(u, g) for u in range(count) for g in range(2)]

    def scores(u, g):
        part = slice(128 * g, 128 * g + 128)
        return jnp.where(valid, dot(keys[u][:, part], queries[u][part]), LOW)

    following = scores(*parts[0])
    found = []
    ones = jnp.ones((16, 256), BF)
    for at, (u, g) in enumerate(parts):
        current = following
        if at + 1 < len(parts):
            following = scores(*parts[at + 1])
        top = jnp.max(current, axis=0, keepdims=True)
        weights = jnp.exp2(current - top).astype(BF)
        mixed = dot(jnp.concatenate([values[u][128 * g : 128 * g + 128], ones], axis=0), weights)
        mixed = jnp.where(same[0:128], mixed[0:128] * (1.0 / mixed[128:129]), 0.0)
        mixed = (mixed[:, 0:128] + mixed[:, 128:256]).T
        found.append((mixed[0:64] + mixed[64:128]).astype(BF))
    attended = jnp.concatenate(
        [jnp.concatenate(found[2 * u : 2 * u + 2], axis=1) for u in range(count)], axis=0
    )
    branch = dot(attended, weights_ref[3])
    for u in range(count):
        o_ref[u] = (xq_ref[u].astype(F32) + branch[64 * u : 64 * u + 64]).astype(BF)


def feed_forward(middle, up, down):
    middle = middle.astype(F32)
    rows = normed(middle)
    total = middle
    for u, d in zip(up, down):
        hidden = jnp.maximum(dot(rows, u), 0.0).astype(BF)
        total = total + dot(hidden, d)
    return total.astype(BF)


def swapped(outer, inner):
    size = outer * inner
    to = lax.broadcasted_iota(jnp.int32, (size, size), 0)
    source = lax.broadcasted_iota(jnp.int32, (size, size), 1)
    return jnp.where(source % inner * outer + source // inner == to, 1.0, 0.0).astype(BF)


def intra_feed_forward(x_ref, w0, w1, w2, w3, o_ref, rows_ref):
    shards = (w0, w1, w2, w3)
    count = x_ref.shape[0]
    up = [w[0:256, :] for w in shards]
    down = [w[256:512, :] for w in shards]
    for at in range(0, count, 8):
        middle = x_ref[at : at + 8].reshape(512, D)
        rows_ref[64 * at : 64 * at + 512, :] = feed_forward(middle, up, down).astype(F32)
    turn = swapped(2 * count, 8)
    for part in range(4):
        taken = [
            rows_ref[64 * u + 32 * half + 8 * part : 64 * u + 32 * half + 8 * part + 8, :]
            for half in range(2)
            for u in range(count)
        ]
        size = 16 * count
        o_ref[size * part : size * part + size, :] = dot(
            turn, jnp.concatenate(taken, axis=0).astype(BF)
        ).astype(BF)


def inter_layer(x_ref, w0, w1, w2, w3, o_ref, weights_ref, query_ref, key_ref, value_ref, attended_ref, later_ref):
    shards = (w0, w1, w2, w3)
    step = pl.program_id(0)

    @pl.when(step == 0)
    def _():
        put_attention_weights(shards, 512, weights_ref)

    x = x_ref[:, 0].astype(F32).reshape(o_ref.shape)
    project(normed(x), weights_ref, query_ref, key_ref, value_ref)

    def block(i, carry):
        columns = pl.ds(pl.multiple_of(i * 256, 256), 256)
        attend(columns, query_ref, key_ref, value_ref, attended_ref)
        return carry

    lax.fori_loop(0, x.shape[0] // 256, block, 0)
    attended = attended_ref[...].T.astype(BF)
    middle = (x + dot(attended, weights_ref[3])).astype(BF)
    done = feed_forward(
        middle, [w[768:1024, :] for w in shards], [w[1024:1280, :] for w in shards]
    ).astype(F32)

    @pl.when(step == 0)
    def _():
        first = lax.broadcasted_iota(jnp.int32, done.shape, 0) == 0
        later_ref[...] = jnp.where(first, 0.0, pltpu.roll(done, 1, 0))

    @pl.when(step == 1)
    def _():
        o_ref[...] = (done + later_ref[...]).astype(BF)


def assemble(mine_ref, p0, p1, p2, p3, o_ref, rows_ref):
    turn = swapped(32, 8)
    for k, piece in enumerate((p0, p1, p2, p3)):
        at = pl.multiple_of((mine_ref[0] ^ k) * 32, 32)
        for part in range(3):
            taken = [piece[s, 8 * part : 8 * part + 8, :].astype(F32) for s in range(32)]
            rows = dot(turn, jnp.concatenate(taken, axis=0).astype(BF)).astype(BF)
            for u in range(8):
                rows_ref[8 * part + u, pl.ds(at, 32), :] = rows[32 * u : 32 * u + 32]
    to = lax.broadcasted_iota(jnp.int32, (128, 256), 0)
    source = lax.broadcasted_iota(jnp.int32, (128, 256), 1)
    for b in range(24):
        place = to + 3 * b
        place = jnp.where(place < HALF, place, place + 3)
        pick = jnp.where(place == source, 1.0, 0.0).astype(BF)
        rows = jnp.concatenate([rows_ref[b], rows_ref[min(b + 1, 23)]], axis=0)
        size = min(128, 3000 - 128 * b)
        o_ref[128 * b : 128 * b + size, :] = dot(pick, rows)[0:size].astype(BF)


def whole(shape):
    return pl.BlockSpec(shape, lambda i, *_: (0,) * len(shape))


def attention_scratch(length):
    return [
        pltpu.VMEM((4, D, D), BF),
        pltpu.VMEM((D, length), BF),
        pltpu.VMEM((HEADS, length, 128), BF),
        pltpu.VMEM((HEADS, 48, length), BF),
        pltpu.VMEM((D, length), F32),
    ]


def by(shard, k):
    return lax.ppermute(shard, "mp", [(i, i ^ k) for i in range(MP)])


def on_device(
    frames, intra_qkv, intra_out, intra_up, intra_down, inter_qkv, inter_out, inter_up, inter_down
):
    seq_count = lax.axis_size("seq")
    mine = lax.axis_index("mp").reshape(1)
    count = frames.shape[0]
    total = count * seq_count

    first = pl.pallas_call(
        pack_attention, out_shape=jax.ShapeDtypeStruct((256, D), BF), name="pack_first"
    )(jnp.transpose(intra_qkv, (1, 0, 2)), intra_out)
    across = by(first, 2)
    beside = by(first, 1)
    first = [first, beside, across, by(across, 1)]
    later = (intra_up, intra_down, jnp.transpose(inter_qkv, (1, 0, 2)), inter_out, inter_up, inter_down)
    *later, first[1] = lax.optimization_barrier((*later, beside))
    rest = pl.pallas_call(
        pack_rest, out_shape=jax.ShapeDtypeStruct((1280, D), BF), name="pack_rest"
    )(*later)
    across = by(rest, 2)
    rest = [rest, by(rest, 1), across, by(across, 1)]

    group = 4

    def blocks(rows):
        return pl.BlockSpec((group, rows, D), lambda i, *_: (i, 0, 0))

    few = jax.ShapeDtypeStruct((count, 64, D), BF)
    rows, few_rows, few_frames = pl.pallas_call(
        prepare,
        out_shape=(jax.ShapeDtypeStruct((count, 256, D), BF), few, few),
        grid_spec=pltpu.PrefetchScalarGridSpec(
            num_scalar_prefetch=1,
            grid=(count // group,),
            in_specs=[blocks(K)],
            out_specs=[blocks(256), blocks(64), blocks(64)],
            scratch_shapes=[pltpu.VMEM((group, 256, D), F32)] * 2,
        ),
        compiler_params=params(),
        cost_estimate=pl.CostEstimate(flops=10**7, bytes_accessed=8 * 10**6, transcendentals=10**4),
        name="prepare",
    )(mine, frames)
    middle = pl.pallas_call(
        intra_attention,
        out_shape=few,
        grid=(count // group,),
        in_specs=[blocks(256), blocks(64), blocks(64)] + [whole((256, D))] * 4,
        out_specs=blocks(64),
        scratch_shapes=[pltpu.VMEM((4, D, D), BF)],
        compiler_params=params(),
        cost_estimate=pl.CostEstimate(flops=10**10, bytes_accessed=4 * 10**6, transcendentals=3 * 10**6),
        name="intra_attention",
    )(rows, few_rows, few_frames, *first)
    send = pl.pallas_call(
        intra_feed_forward,
        out_shape=jax.ShapeDtypeStruct((64 * count, D), BF),
        grid=(1,),
        in_specs=[whole((count, 64, D))] + [whole((512, D))] * 4,
        out_specs=whole((64 * count, D)),
        scratch_shapes=[pltpu.VMEM((64 * count, D), F32)],
        compiler_params=params(),
        cost_estimate=pl.CostEstimate(flops=3 * 10**9, bytes_accessed=3 * 10**6, transcendentals=0),
        name="intra_feed_forward",
    )(middle, *rest)

    send = send.reshape(seq_count, 2 * count, D)
    got = lax.all_to_all(send, "seq", split_axis=0, concat_axis=0, tiled=True)
    got = got.reshape(seq_count, 2, count, D)

    summed = pl.pallas_call(
        inter_layer,
        out_shape=jax.ShapeDtypeStruct((total, D), BF),
        grid=(2,),
        in_specs=[pl.BlockSpec((seq_count, 1, count, D), lambda i: (0, 1 - i, 0, 0))]
        + [whole((1280, D))] * 4,
        out_specs=whole((total, D)),
        scratch_shapes=attention_scratch(total) + [pltpu.VMEM((total, D), F32)],
        compiler_params=params(),
        cost_estimate=pl.CostEstimate(flops=3 * 10**10, bytes_accessed=4 * 10**6, transcendentals=10**7),
        name="inter_layer",
    )(got, *rest)

    back = summed.reshape(seq_count, count, D)
    back = lax.all_to_all(back, "seq", split_axis=0, concat_axis=0, tiled=True)
    across = by(back, 2)
    pieces = [back, by(back, 1), across, by(across, 1)]
    return pl.pallas_call(
        assemble,
        out_shape=jax.ShapeDtypeStruct((HALF * count, D), BF),
        grid_spec=pltpu.PrefetchScalarGridSpec(
            num_scalar_prefetch=1,
            grid=(1,),
            in_specs=[whole(back.shape)] * 4,
            out_specs=whole((HALF * count, D)),
            scratch_shapes=[pltpu.VMEM((count, 128, D), BF)],
        ),
        compiler_params=params(),
        cost_estimate=pl.CostEstimate(flops=10**9, bytes_accessed=4 * 10**6, transcendentals=0),
        name="assemble",
    )(mine, *pieces)


def solution(mesh):
    return jax.shard_map(
        on_device,
        mesh=mesh,
        in_specs=(
            P("seq", None, None),
            P(None, None, "mp"),
            P("mp", None),
            P(None, "mp"),
            P("mp", None),
            P(None, None, "mp"),
            P("mp", None),
            P(None, "mp"),
            P("mp", None),
        ),
        out_specs=P("seq", None),
        check_vma=False,
    )
```

time: 146 us -> 142 us (0.973)
  Pallas kernels: 47.4 us -> 55.7 us
  local copies, waits for them, and re-layouts: 18.2 us -> 10.9 us
  blocking collectives: 41.4 us -> 35.3 us
  waiting for transfers between devices: 18.7 us -> 23.4 us
  other arithmetic: 2.76 us -> 0 us
  starting transfers between devices: 17.3 us -> 15.7 us
    reshape x8 -> x0, local copies, waits for them, and re-layouts: 10.7 us -> none  [the longest x2 3.84 us: on_device(): jnp.transpose(send, (3, 2, 1, 0, 4)).reshape(seq_count * MP, 2 * spans, D)]
    pallas_call x2 -> x4, Pallas kernels: 20.6 us -> 29.4 us  [the longest x1 13.5 us: on_device(): pl.pallas_call(intra_attention, out_shape=few, grid=(count // group,), in...]
    unnamed x14 -> x25, local copies, waits for them, and re-layouts: 4.28 us -> 10.9 us
    all_to_all x1, blocking collectives: 28.5 us -> 22.2 us  [on_device(): got = lax.all_to_all(send, 'seq', split_axis=0, concat_axis=0, tiled=True)]
    ppermute x9, waiting for transfers between devices: 18.7 us -> 23.4 us  [by(): return lax.ppermute(shard, 'mp', [(i, i ^ k) for i in range(MP)])]
    another operation x2 -> x0, other arithmetic: 2.76 us -> none  [on_device(): jnp.stack(pieces)]
    all_to_all x2 -> x0, local copies, waits for them, and re-layouts: 1.95 us -> none  [the longest x1 1.12 us: on_device(): lax.all_to_all(send, ('seq', 'mp'), split_axis=0, concat_axis=0, tiled=True)]
    ppermute x9, starting transfers between devices: 17.3 us -> 15.7 us  [by(): return lax.ppermute(shard, 'mp', [(i, i ^ k) for i in range(MP)])]
  transfers between devices with their start and end apart: 9 -> 9, of which waited for: 5 -> 3; matrix products, arithmetic and copies ran while one was open for 2% -> 4% of each run, Pallas kernels for 11% -> 15%
where the time goes in v2:
time: 142 us; the launch traced here: 141 us
  Pallas kernels  55.7 us (39%)
  blocking collectives  35.3 us (25%)
  waiting for transfers between devices  23.4 us (16%)
  starting transfers between devices  15.7 us (11%)
  local copies, waits for them, and re-layouts  10.9 us (8%)
    ppermute x9, waiting for transfers between devices, by(): return lax.ppermute(shard, 'mp', [(i, i ^ k) for i in range(MP)])  23.4 us
    pallas_call x1, Pallas kernels, on_device(): pl.pallas_call(inter_layer, out_shape=jax.ShapeDtypeStruct((total, D), BF...  22.3 us
    all_to_all x1, blocking collectives, on_device(): got = lax.all_to_all(send, 'seq', split_axis=0, concat_axis=0, tiled=True)  22.2 us
    ppermute x9, starting transfers between devices, by(): return lax.ppermute(shard, 'mp', [(i, i ^ k) for i in range(MP)])  15.7 us
    pallas_call x1, Pallas kernels, on_device(): pl.pallas_call(intra_attention, out_shape=few, grid=(count // group,), in...  13.5 us
    all_to_all x1, blocking collectives, on_device(): back = lax.all_to_all(back, 'seq', split_axis=0, concat_axis=0, tiled=True)  13.1 us
    unnamed x25, local copies, waits for them, and re-layouts  10.9 us
    pallas_call x1, Pallas kernels, on_device(): pl.pallas_call(prepare, out_shape=(jax.ShapeDtypeStruct((count, 256, D),...  7.23 us
  transfers between devices with their start and end apart: 9, of which 3 were waited for; matrix products, arithmetic and copies ran while one was open for 4% of the time, Pallas kernels for 15%

profile of v2, /device:TPU:1, one launch (start us, length us, event | category | flops | bytes accessed | tf_op | source)
XLA Modules:
  0.0 141.1 jit_solution(8360411414928972535)
XLA Ops:
  0.0 1.7 %copy.11 = bf16[256,3,64]{2,0,1:T(8,128)(2,1)} copy(bf16[256,3,64]{0,2,1:T(8,128)(2,1)} %param.10) | data formatting | bytes 196608 | tf_op args[1]
  1.7 1.7 %pack_first.1.w0 = bf16[256,256]{1,0:T(8,128)(2,1)} custom-call(bf16[3,256,64]{2,1,0:T(8,128)(2,1)} %bitcast.8, bf16[64,256]{1,0:T(8,128)(2,1)} %out_ref.1), custom_call_target="tpu_custom_call" | custom-call | tf_op jit(solution)/shard_map/pack_first/pallas_call | solution.py:269
  3.4 1.4 %collective-permute-start = (bf16[256,256]{1,0:T(8,128)(2,1)}, bf16[256,256]{1,0:T(8,128)(2,1)S(1)}, u32[]{:S(2)}, u32[]{:S(2)}) collective-permute-start(bf16[256,256]{1,0:T(8,128)(2,1)} %pack_first.1.w0), channel_id=1, source_target_pairs={{0,1},{1,0},{2,3},{3,2},{4,5},{5,4},{6,7},{7,6},{8,9},{9,8},{10,11... | collective-permute-start | bytes 393224 | tf_op jit(solution)/shard_map/ppermute | solution.py:258
  4.8 1.7 %copy.12 = bf16[256,3,64]{2,0,1:T(8,128)(2,1)} copy(bf16[256,3,64]{0,2,1:T(8,128)(2,1)} %param.14) | data formatting | bytes 196608 | tf_op args[5]
  6.5 0.0 collective-permute-done.w1
  6.5 0.0 copy-start.8
  6.5 2.2 %pack_rest.1.w0 = bf16[1280,256]{1,0:T(8,128)(2,1)} custom-call(bf16[256,256]{1,0:T(8,128)(2,1)} %up1_ref, bf16[256,256]{1,0:T(8,128)(2,1)} %down1_ref, bf16[3,256,64]{2,1,0:T(8,128)(2,1)} %bitcast.9, bf16[64,256]{1,0:T(8,128)(2,1)} %out_ref.2, bf16[256,256]{1,0:T(8,128)(2,1)} %up2_ref, bf16[256,256]{1,0:T(8,128)(2,1)} %down2_ref), custom_call_target="tpu_custom_call" | custom-call | tf_op jit(solution)/shard_map/pack_rest/pallas_call | solution.py:277
  8.8 3.7 %collective-permute-start.4 = (bf16[1280,256]{1,0:T(8,128)(2,1)}, bf16[1280,256]{1,0:T(8,128)(2,1)S(1)}, u32[]{:S(2)}, u32[]{:S(2)}) collective-permute-start(bf16[1280,256]{1,0:T(8,128)(2,1)} %pack_rest.1.w0), channel_id=1, source_target_pairs={{0,2},{1,3},{2,0},{3,1},{4,6},{5,7},{6,4},{7,5},{8,10},{9,11},{10,... | collective-permute-start | bytes 1966088 | tf_op jit(solution)/shard_map/ppermute | solution.py:258
  12.4 0.0 collective-permute-start.1
  12.5 18.1 %collective-permute-done.1.w2 = bf16[256,256]{1,0:T(8,128)(2,1)S(1)} collective-permute-done((bf16[256,256]{1,0:T(8,128)(2,1)}, bf16[256,256]{1,0:T(8,128)(2,1)S(1)}, u32[]{:S(2)}, u32[]{:S(2)}) %collective-permute-start.1) | collective-permute-done | bytes 131104 | tf_op jit(solution)/shard_map/ppermute | solution.py:258
  30.6 0.0 copy-start.9
  30.6 0.6 collective-permute-start.2
  31.1 0.0 copy-start
  31.1 4.3 %copy.10.x_ref = bf16[24,250,256]{2,1,0:T(8,128)(2,1)} copy(bf16[24,250,256]{2,0,1:T(8,128)(2,1)} %param.9) | data formatting | bytes 6144000 | tf_op args[0]
  35.5 0.0 copy-done.8
  35.5 7.2 %prepare.1 = (bf16[24,256,256]{2,1,0:T(8,128)(2,1)}, bf16[24,64,256]{2,1,0:T(8,128)(2,1)}, bf16[24,64,256]{2,1,0:T(8,128)(2,1)}) custom-call(s32[1]{0:T(128)} %bitcast.mine_ref, bf16[24,250,256]{2,1,0:T(8,128)(2,1)} %copy.10.x_ref), custom_call_target="tpu_custom_call" | custom-call | flops 10000000 | bytes 8000000 | tf_op jit(solution)/shard_map/prepare/pallas_call | solution.py:289
  42.7 0.0 copy-done.9
  42.7 0.0 copy-done
  42.7 0.1 collective-permute-start.3
  42.8 0.0 collective-permute-done.4.w2
  42.8 0.0 copy-start.2
  42.8 0.5 collective-permute-start.5
  43.3 0.0 collective-permute-done.2.w3
  43.3 0.0 copy-start.10
  43.3 0.7 copy-done.10
  44.0 13.5 %intra_attention.1.x_ref = bf16[24,64,256]{2,1,0:T(8,128)(2,1)} custom-call(bf16[24,256,256]{2,1,0:T(8,128)(2,1)} %get-tuple-element.15.n_ref, bf16[24,64,256]{2,1,0:T(8,128)(2,1)} %get-tuple-element.16.nq_ref, bf16[24,64,256]{2,1,0:T(8,128)(2,1)} %get-tuple-element.17.xq_ref, bf16[256,256]{1,0:T(8,128)(2,1)} %pack_first.1.w0, bf16[256,256]{1,0:T(8,128)(2,1)} %copy-done.8, ...), custom_call_target="tpu_custom_call" | custom-call | flops 10000000000 | bytes 4000000 | tf_op jit(solution)/shard_map/intra_attention/pallas_call | solution.py:303
  57.5 0.0 copy-done.2
  57.5 0.0 collective-permute-done.3.w1
  57.5 0.0 copy-start.3
  57.5 0.0 collective-permute-done.5.w3
  57.5 0.8 copy-done.3
  58.4 0.0 copy-start.4
  58.4 0.9 copy-done.4
  59.3 5.0 %intra_feed_forward.1 = bf16[1536,256]{1,0:T(8,128)(2,1)} custom-call(bf16[24,64,256]{2,1,0:T(8,128)(2,1)} %intra_attention.1.x_ref, bf16[1280,256]{1,0:T(8,128)(2,1)} %pack_rest.1.w0, bf16[1280,256]{1,0:T(8,128)(2,1)} %copy-done.3, bf16[1280,256]{1,0:T(8,128)(2,1)} %copy-done.2, bf16[1280,256]{1,0:T(8,128)(2,1)} %copy-done.4), custom_call_target="tpu_custom_call" | custom-call | flops 3000000000 | bytes 3000000 | tf_op jit(solution)/shard_map/intra_feed_forward/pallas_call | solution.py:314
  64.2 22.2 %all_to_all.10 = bf16[32,48,256]{2,1,0:T(8,128)(2,1)} all-to-all(bf16[32,48,256]{2,1,0:T(8,128)(2,1)} %bitcast.7), channel_id=1, replica_groups=mesh['seq'=32,'mp'=4] {'seq'}, dimensions={0} | all-to-all | bytes 1572864 | tf_op jit(solution)/shard_map/all_to_all | solution.py:327
  86.4 22.3 %inter_layer.1 = bf16[768,256]{1,0:T(8,128)(2,1)} custom-call(bf16[32,2,24,256]{3,2,1,0:T(8,128)(2,1)} %bitcast.6, bf16[1280,256]{1,0:T(8,128)(2,1)} %pack_rest.1.w0, bf16[1280,256]{1,0:T(8,128)(2,1)} %copy-done.3, bf16[1280,256]{1,0:T(8,128)(2,1)} %copy-done.2, bf16[1280,256]{1,0:T(8,128)(2,1)} %copy-done.4), custom_call_target="tpu_custom_call" | custom-call | flops 30000001024 | bytes 4000000 | tf_op jit(solution)/shard_map/inter_layer/pallas_call | solution.py:330
  108.8 13.1 %all_to_all.11.p0 = bf16[32,24,256]{2,1,0:T(8,128)(2,1)S(1)} all-to-all(bf16[32,24,256]{2,1,0:T(8,128)(2,1)} %bitcast.10), channel_id=1, replica_groups=mesh['seq'=32,'mp'=4] {'seq'}, dimensions={0} | all-to-all | bytes 786432 | tf_op jit(solution)/shard_map/all_to_all | solution.py:344
  121.9 0.0 copy-start.1
  121.9 3.3 %collective-permute-start.7 = (bf16[32,24,256]{2,1,0:T(8,128)(2,1)S(1)}, bf16[32,24,256]{2,1,0:T(8,128)(2,1)S(1)}, u32[]{:S(2)}, u32[]{:S(2)}) collective-permute-start(bf16[32,24,256]{2,1,0:T(8,128)(2,1)S(1)} %all_to_all.11.p0), channel_id=1, source_target_pairs={{0,2},{1,3},{2,0},{3,1},{4,6},{5,7},{6,4},{7,5},{8,10},{9,11},{10,... | collective-permute-start | bytes 1179656 | tf_op jit(solution)/shard_map/ppermute | solution.py:258
  125.2 2.9 %collective-permute-start.6 = (bf16[32,24,256]{2,1,0:T(8,128)(2,1)S(1)}, bf16[32,24,256]{2,1,0:T(8,128)(2,1)S(1)}, u32[]{:S(2)}, u32[]{:S(2)}) collective-permute-start(bf16[32,24,256]{2,1,0:T(8,128)(2,1)S(1)} %all_to_all.11.p0), channel_id=1, source_target_pairs={{0,1},{1,0},{2,3},{3,2},{4,5},{5,4},{6,7},{7,6},{8,9},{9,8},{10,11... | collective-permute-start | bytes 1179656 | tf_op jit(solution)/shard_map/ppermute | solution.py:258
  128.1 3.9 %collective-permute-done.7.p2 = bf16[32,24,256]{2,1,0:T(8,128)(2,1)S(1)} collective-permute-done((bf16[32,24,256]{2,1,0:T(8,128)(2,1)S(1)}, bf16[32,24,256]{2,1,0:T(8,128)(2,1)S(1)}, u32[]{:S(2)}, u32[]{:S(2)}) %collective-permute-start.7) | collective-permute-done | bytes 393248 | tf_op jit(solution)/shard_map/ppermute | solution.py:258
  132.1 0.0 copy-start.5
  132.1 3.2 %collective-permute-start.8 = (bf16[32,24,256]{2,1,0:T(8,128)(2,1)S(1)}, bf16[32,24,256]{2,1,0:T(8,128)(2,1)S(1)}, u32[]{:S(2)}, u32[]{:S(2)}) collective-permute-start(bf16[32,24,256]{2,1,0:T(8,128)(2,1)S(1)} %collective-permute-done.7.p2), channel_id=1, source_target_pairs={{0,1},{1,0},{2,3},{3,2},{4,5},{5,4},{6,7},{7,6},{8,9},{9,8},{10,11... | collective-permute-start | bytes 1179656 | tf_op jit(solution)/shard_map/ppermute | solution.py:258
  135.3 0.0 collective-permute-done.6.p1
  135.3 0.0 copy-start.6
  135.3 1.3 collective-permute-done.8.p3
  136.7 0.0 copy-done.1
  136.7 0.0 copy-done.5
  136.7 0.0 copy-done.6
  136.7 0.0 copy-start.7
  136.7 0.7 copy-done.7
  137.4 3.6 %assemble.1 = bf16[3000,256]{1,0:T(8,128)(2,1)} custom-call(s32[1]{0:T(128)} %bitcast.mine_ref, bf16[32,24,256]{2,1,0:T(8,128)(2,1)} %copy-done.1, bf16[32,24,256]{2,1,0:T(8,128)(2,1)} %copy-done.6, bf16[32,24,256]{2,1,0:T(8,128)(2,1)} %copy-done.5, bf16[32,24,256]{2,1,0:T(8,128)(2,1)} %copy-done.7), custom_call_target="tpu_custom_call" | custom-call | flops 1000000000 | bytes 4000000 | tf_op jit(solution)/shard_map/assemble/pallas_call | solution.py:347
Async XLA Ops:
  3.4 3.1 %collective-permute-start = (bf16[256,256]{1,0:T(8,128)(2,1)}, bf16[256,256]{1,0:T(8,128)(2,1)S(1)}, u32[]{:S(2)}, u32[]{:S(2)}) collective-permute-start(bf16[256,256]{1,0:T(8,128)(2,1)} %pack_first.1.w0), channel_id=1, source_target_pairs={{0,1},{1,0},{2,3},{3,2},{4,5},{5,4},{6,7},{7,6},{8,9},{9,8},{10,11... | collective-permute-start | bytes 393224 | tf_op jit(solution)/shard_map/ppermute | solution.py:258
  6.5 28.9 %copy-start.8 = (bf16[256,256]{1,0:T(8,128)(2,1)}, bf16[256,256]{1,0:T(8,128)(2,1)S(1)}, u32[]{:S(2)}) copy-start(bf16[256,256]{1,0:T(8,128)(2,1)S(1)} %collective-permute-done.w1) | copy-start | bytes 393220
  8.8 34.0 %collective-permute-start.4 = (bf16[1280,256]{1,0:T(8,128)(2,1)}, bf16[1280,256]{1,0:T(8,128)(2,1)S(1)}, u32[]{:S(2)}, u32[]{:S(2)}) collective-permute-start(bf16[1280,256]{1,0:T(8,128)(2,1)} %pack_rest.1.w0), channel_id=1, source_target_pairs={{0,2},{1,3},{2,0},{3,1},{4,6},{5,7},{6,4},{7,5},{8,10},{9,11},{10,... | collective-permute-start | bytes 1966088 | tf_op jit(solution)/shard_map/ppermute | solution.py:258
  12.4 18.1 %collective-permute-start.1 = (bf16[256,256]{1,0:T(8,128)(2,1)}, bf16[256,256]{1,0:T(8,128)(2,1)S(1)}, u32[]{:S(2)}, u32[]{:S(2)}) collective-permute-start(bf16[256,256]{1,0:T(8,128)(2,1)} %pack_first.1.w0), channel_id=1, source_target_pairs={{0,2},{1,3},{2,0},{3,1},{4,6},{5,7},{6,4},{7,5},{8,10},{9,11},{10,... | collective-permute-start | bytes 393224 | tf_op jit(solution)/shard_map/ppermute | solution.py:258
  30.6 12.1 %copy-start.9 = (bf16[256,256]{1,0:T(8,128)(2,1)}, bf16[256,256]{1,0:T(8,128)(2,1)S(1)}, u32[]{:S(2)}) copy-start(bf16[256,256]{1,0:T(8,128)(2,1)S(1)} %collective-permute-done.1.w2) | copy-start | bytes 393220
  30.6 12.7 %collective-permute-start.2 = (bf16[256,256]{1,0:T(8,128)(2,1)S(1)}, bf16[256,256]{1,0:T(8,128)(2,1)S(1)}, u32[]{:S(2)}, u32[]{:S(2)}) collective-permute-start(bf16[256,256]{1,0:T(8,128)(2,1)S(1)} %collective-permute-done.1.w2), channel_id=1, source_target_pairs={{0,1},{1,0},{2,3},{3,2},{4,5},{5,4},{6,7},{7,6},{8,9},{9,8},{10,11... | collective-permute-start | bytes 393224 | tf_op jit(solution)/shard_map/ppermute | solution.py:258
  31.1 11.6 %copy-start = (bf16[1280,256]{1,0:T(8,128)(2,1)S(1)}, bf16[1280,256]{1,0:T(8,128)(2,1)}, u32[]{:S(2)}) copy-start(bf16[1280,256]{1,0:T(8,128)(2,1)} %pack_rest.1.w0) | copy-start | bytes 1966084
  42.7 14.8 %collective-permute-start.3 = (bf16[1280,256]{1,0:T(8,128)(2,1)S(1)}, bf16[1280,256]{1,0:T(8,128)(2,1)S(1)}, u32[]{:S(2)}, u32[]{:S(2)}) collective-permute-start(bf16[1280,256]{1,0:T(8,128)(2,1)S(1)} %copy-done), channel_id=1, source_target_pairs={{0,1},{1,0},{2,3},{3,2},{4,5},{5,4},{6,7},{7,6},{8,9},{9,8},{10,11... | collective-permute-start | bytes 1966088 | tf_op jit(solution)/shard_map/ppermute | solution.py:258
  42.8 14.7 %copy-start.2 = (bf16[1280,256]{1,0:T(8,128)(2,1)}, bf16[1280,256]{1,0:T(8,128)(2,1)S(1)}, u32[]{:S(2)}) copy-start(bf16[1280,256]{1,0:T(8,128)(2,1)S(1)} %collective-permute-done.4.w2) | copy-start | bytes 1966084
  42.8 14.7 %collective-permute-start.5 = (bf16[1280,256]{1,0:T(8,128)(2,1)S(1)}, bf16[1280,256]{1,0:T(8,128)(2,1)S(1)}, u32[]{:S(2)}, u32[]{:S(2)}) collective-permute-start(bf16[1280,256]{1,0:T(8,128)(2,1)S(1)} %collective-permute-done.4.w2), channel_id=1, source_target_pairs={{0,1},{1,0},{2,3},{3,2},{4,5},{5,4},{6,7},{7,6},{8,9},{9,8},{10,11... | collective-permute-start | bytes 1966088 | tf_op jit(solution)/shard_map/ppermute | solution.py:258
  43.3 0.7 copy-start.10
  57.5 0.9 copy-start.3
  58.4 0.9 copy-start.4
  121.9 14.7 %copy-start.1 = (bf16[32,24,256]{2,1,0:T(8,128)(2,1)}, bf16[32,24,256]{2,1,0:T(8,128)(2,1)S(1)}, u32[]{:S(2)}) copy-start(bf16[32,24,256]{2,1,0:T(8,128)(2,1)S(1)} %all_to_all.11.p0) | copy-start | bytes 1179652
  121.9 10.1 %collective-permute-start.7 = (bf16[32,24,256]{2,1,0:T(8,128)(2,1)S(1)}, bf16[32,24,256]{2,1,0:T(8,128)(2,1)S(1)}, u32[]{:S(2)}, u32[]{:S(2)}) collective-permute-start(bf16[32,24,256]{2,1,0:T(8,128)(2,1)S(1)} %all_to_all.11.p0), channel_id=1, source_target_pairs={{0,2},{1,3},{2,0},{3,1},{4,6},{5,7},{6,4},{7,5},{8,10},{9,11},{10,... | collective-permute-start | bytes 1179656 | tf_op jit(solution)/shard_map/ppermute | solution.py:258
  125.2 10.1 %collective-permute-start.6 = (bf16[32,24,256]{2,1,0:T(8,128)(2,1)S(1)}, bf16[32,24,256]{2,1,0:T(8,128)(2,1)S(1)}, u32[]{:S(2)}, u32[]{:S(2)}) collective-permute-start(bf16[32,24,256]{2,1,0:T(8,128)(2,1)S(1)} %all_to_all.11.p0), channel_id=1, source_target_pairs={{0,1},{1,0},{2,3},{3,2},{4,5},{5,4},{6,7},{7,6},{8,9},{9,8},{10,11... | collective-permute-start | bytes 1179656 | tf_op jit(solution)/shard_map/ppermute | solution.py:258
  132.1 4.6 %copy-start.5 = (bf16[32,24,256]{2,1,0:T(8,128)(2,1)}, bf16[32,24,256]{2,1,0:T(8,128)(2,1)S(1)}, u32[]{:S(2)}) copy-start(bf16[32,24,256]{2,1,0:T(8,128)(2,1)S(1)} %collective-permute-done.7.p2) | copy-start | bytes 1179652
  132.1 4.6 %collective-permute-start.8 = (bf16[32,24,256]{2,1,0:T(8,128)(2,1)S(1)}, bf16[32,24,256]{2,1,0:T(8,128)(2,1)S(1)}, u32[]{:S(2)}, u32[]{:S(2)}) collective-permute-start(bf16[32,24,256]{2,1,0:T(8,128)(2,1)S(1)} %collective-permute-done.7.p2), channel_id=1, source_target_pairs={{0,1},{1,0},{2,3},{3,2},{4,5},{5,4},{6,7},{7,6},{8,9},{9,8},{10,11... | collective-permute-start | bytes 1179656 | tf_op jit(solution)/shard_map/ppermute | solution.py:258
  135.3 1.4 copy-start.6
  136.7 0.7 copy-start.7

commit v3 on v2

v3 whole, which is shorter than its diff:
```python
import functools

import jax
import jax.numpy as jnp
from jax import lax
from jax.experimental import pallas as pl
from jax.experimental.pallas import tpu as pltpu
from jax.sharding import PartitionSpec as P

HEADS = 8
HD = 32
K = 250
HALF = K // 2
D = 256
MP = 4
BF = jnp.bfloat16
F32 = jnp.float32
Q_SCALE = 1.4426950408889634 * HD ** (-0.5)
LOW = -1e30
IN_VMEM = pl.BlockSpec(memory_space=pltpu.VMEM)


def params(mebibytes):
    return pltpu.CompilerParams(vmem_limit_bytes=mebibytes * 1024 * 1024)


def dot(left, right, left_dim=1, right_dim=0):
    return lax.dot_general(
        left, right, (((left_dim,), (right_dim,)), ((), ())), preferred_element_type=F32
    )


def normed(values):
    centre = values - jnp.mean(values, axis=-1, keepdims=True)
    spread = jnp.mean(centre * centre, axis=-1, keepdims=True)
    return (centre * lax.rsqrt(spread + 1e-05)).astype(BF)


def put_attention_weights(shards, weights_ref):
    for k in range(MP):
        for t in range(weights_ref.shape[0]):
            weights_ref[t, 64 * k : 64 * k + 64, :] = shards[k][64 * t : 64 * t + 64, :]


def project(rows, weights_ref, query_ref, key_ref, value_ref):
    query_ref[...] = (dot(weights_ref[0], rows, 1, 1) * Q_SCALE).astype(BF)
    keys = dot(rows, weights_ref[1], 1, 1).astype(BF)
    lane = lax.broadcasted_iota(jnp.int32, (rows.shape[0], 128), 1) // HD
    for h in range(HEADS):
        part = keys[:, 128 * (h // 4) : 128 * (h // 4) + 128]
        key_ref[h] = jnp.where(lane == h % 4, part, jnp.zeros_like(part))
    values = dot(weights_ref[2], rows, 1, 1).astype(BF)
    for h in range(HEADS):
        value_ref[h, 0:HD, :] = values[HD * h : HD * h + HD, :]
        value_ref[h, HD:48, :] = jnp.ones((48 - HD, rows.shape[0]), BF)


def attend(columns, query_ref, key_ref, value_ref, attended_ref):
    def scores(h):
        at = 128 * (h // 4)
        return dot(key_ref[h], query_ref[at : at + 128, columns])

    following = scores(0)
    for h in range(HEADS):
        current = following
        if h + 1 < HEADS:
            following = scores(h + 1)
        top = jnp.max(current, axis=0, keepdims=True)
        weights = jnp.exp2(current - top).astype(BF)
        mixed = dot(value_ref[h], weights)
        attended_ref[HD * h : HD * h + HD, columns] = mixed[0:HD] * (1.0 / mixed[HD : HD + 1])


def swapped(outer, bits):
    inner = 1 << bits
    size = outer * inner
    to = lax.broadcasted_iota(jnp.int32, (size, size), 0)
    source = lax.broadcasted_iota(jnp.int32, (size, size), 1)
    return jnp.where((source & (inner - 1)) * outer + (source >> bits) == to, 1.0, 0.0).astype(BF)


def pack(*refs):
    sources, packed_ref = refs[:-1], refs[-1]
    at = 0
    for source in sources:
        packed_ref[at : at + source.shape[0], :] = source[...]
        at += source.shape[0]


def prepare(mine_ref, x_ref, n_ref, xq_ref, turn_ref):
    count = x_ref.shape[1]
    turn_ref[...] = swapped(count, 4).T

    def put(to, x):
        rows = normed(x.astype(F32).reshape(16 * count, D))
        rows = dot(turn_ref[...], rows).astype(BF)
        for u in range(count):
            n_ref[u, pl.ds(to, 16), :] = rows[16 * u : 16 * u + 16]

    def early(b, carry):
        at = pl.multiple_of(b * 16, 16)
        put(at, x_ref[pl.ds(at, 16)])
        return carry

    def late(b, carry):
        at = pl.multiple_of(b * 16, 16)
        put(128 + at, x_ref[pl.ds(HALF + at, 16)])
        return carry

    lax.fori_loop(0, 8, early, 0)
    lax.fori_loop(0, 7, late, 0)
    put(240, jnp.concatenate([x_ref[HALF + 112 : K], x_ref[K - 3 : K]], axis=0))

    def residual(j, carry):
        r = mine_ref[0] * 32 + j
        xq_ref[0, j] = x_ref[r]
        xq_ref[1, j] = x_ref[jnp.minimum(HALF + r, K - 1)]
        return carry

    lax.fori_loop(0, 32, residual, 0)


def intra_attention(mine_ref, n_ref, w0, w1, w2, w3, o_ref, weights_ref):
    @pl.when(pl.program_id(0) == 0)
    def _():
        put_attention_weights((w0, w1, w2, w3), weights_ref)

    own = pl.multiple_of(mine_ref[0] * 32, 32)
    count = n_ref.shape[0]
    row = lax.broadcasted_iota(jnp.int32, (256, 256), 0)
    lane = lax.broadcasted_iota(jnp.int32, (256, 256), 1)
    valid = (row % 128) < HALF
    same = (row % 128) // HD == lane // 64
    keys, queries, values = [], [], []
    for u in range(count):
        rows = n_ref[u]
        few = jnp.concatenate(
            [n_ref[u, pl.ds(own, 32), :], n_ref[u, pl.ds(128 + own, 32), :]], axis=0
        )
        keys.append(dot(rows, weights_ref[1], 1, 1).astype(BF))
        query = dot(weights_ref[0], jnp.concatenate([few] * 4, axis=0), 1, 1) * Q_SCALE
        queries.append(jnp.where(same, query, 0.0).astype(BF))
        values.append(dot(weights_ref[2], rows, 1, 1).astype(BF))
    parts = [(u, g) for u in range(count) for g in range(2)]

    def scores(u, g):
        part = slice(128 * g, 128 * g + 128)
        return jnp.where(valid, dot(keys[u][:, part], queries[u][part]), LOW)

    following = scores(*parts[0])
    found = []
    ones = jnp.ones((16, 256), BF)
    for at, (u, g) in enumerate(parts):
        current = following
        if at + 1 < len(parts):
            following = scores(*parts[at + 1])
        top = jnp.max(current, axis=0, keepdims=True)
        weights = jnp.exp2(current - top).astype(BF)
        mixed = dot(jnp.concatenate([values[u][128 * g : 128 * g + 128], ones], axis=0), weights)
        mixed = jnp.where(same[0:128], mixed[0:128] * (1.0 / mixed[128:129]), 0.0)
        mixed = (mixed[:, 0:128] + mixed[:, 128:256]).T
        found.append((mixed[0:64] + mixed[64:128]).astype(BF))
    for u in range(count):
        o_ref[u] = jnp.concatenate(found[2 * u : 2 * u + 2], axis=1)


def feed_forward(middle, up, down):
    middle = middle.astype(F32)
    rows = normed(middle)
    total = middle
    for u, d in zip(up, down):
        hidden = jnp.maximum(dot(rows, u), 0.0).astype(BF)
        total = total + dot(hidden, d)
    return total.astype(BF)


def intra_feed_forward(a0_ref, a1_ref, xq_ref, w0, w1, w2, w3, o_ref):
    shards = (w0, w1, w2, w3)
    count = 2 * a0_ref.shape[0]
    out = jnp.concatenate([w[768:832, :] for w in shards], axis=0)
    up = [w[832:1088, :] for w in shards]
    down = [w[1088:1344, :] for w in shards]
    turn = swapped(count, 3)
    for half in range(2):
        for pair in range(2):
            rows = []
            for at in (32 * half + 16 * pair, 32 * half + 16 * pair + 8):
                taken = [
                    ref[u, at : at + 8, :].astype(F32)
                    for ref in (a0_ref, a1_ref)
                    for u in range(count // 2)
                ]
                rows.append(dot(turn, jnp.concatenate(taken, axis=0).astype(BF)).astype(BF))
            attended = jnp.concatenate(rows, axis=0)
            part = slice(16 * pair, 16 * pair + 16)
            x = xq_ref[half, part].astype(F32).reshape(16 * count, D)
            middle = (x + dot(attended, out)).astype(BF)
            done = feed_forward(middle, up, down).astype(F32)
            o_ref[part, half] = done.reshape(16, count, D).astype(BF)


def inter_layer(x_ref, w0, w1, w2, w3, o_ref, weights_ref, query_ref, key_ref, value_ref, attended_ref):
    shards = (w0, w1, w2, w3)
    put_attention_weights(shards, weights_ref)
    for half in (1, 0):
        x = x_ref[:, half].astype(F32).reshape(o_ref.shape)
        project(normed(x), weights_ref, query_ref, key_ref, value_ref)

        def block(i, carry):
            columns = pl.ds(pl.multiple_of(i * 256, 256), 256)
            attend(columns, query_ref, key_ref, value_ref, attended_ref)
            return carry

        lax.fori_loop(0, x.shape[0] // 256, block, 0)
        attended = attended_ref[...].T.astype(BF)
        middle = (x + dot(attended, weights_ref[3])).astype(BF)
        done = feed_forward(
            middle, [w[256:512, :] for w in shards], [w[512:768, :] for w in shards]
        )
        if half == 1:
            first = lax.broadcasted_iota(jnp.int32, done.shape, 0) == 0
            o_ref[...] = jnp.where(first, 0.0, pltpu.roll(done.astype(F32), 1, 0)).astype(BF)
        else:
            o_ref[...] = (done.astype(F32) + o_ref[...].astype(F32)).astype(BF)


def assemble(mine_ref, p0, p1, p2, p3, o_ref, rows_ref):
    turn = swapped(32, 3)
    for k, piece in enumerate((p0, p1, p2, p3)):
        at = pl.multiple_of((mine_ref[0] ^ k) * 32, 32)
        for part in range(3):
            taken = [piece[s, 8 * part : 8 * part + 8, :].astype(F32) for s in range(32)]
            rows = dot(turn, jnp.concatenate(taken, axis=0).astype(BF)).astype(BF)
            for u in range(8):
                rows_ref[8 * part + u, pl.ds(at, 32), :] = rows[32 * u : 32 * u + 32]
    to = lax.broadcasted_iota(jnp.int32, (128, 256), 0)
    source = lax.broadcasted_iota(jnp.int32, (128, 256), 1)
    for b in range(24):
        place = to + 3 * b
        place = jnp.where(place < HALF, place, place + 3)
        pick = jnp.where(place == source, 1.0, 0.0).astype(BF)
        rows = jnp.concatenate([rows_ref[b], rows_ref[min(b + 1, 23)]], axis=0)
        size = min(128, 3000 - 128 * b)
        o_ref[128 * b : 128 * b + size, :] = dot(pick, rows)[0:size].astype(BF)


def whole(shape):
    return pl.BlockSpec(shape, lambda i, *_: (0,) * len(shape))


def attention_scratch(length):
    return [
        pltpu.VMEM((4, D, D), BF),
        pltpu.VMEM((D, length), BF),
        pltpu.VMEM((HEADS, length, 128), BF),
        pltpu.VMEM((HEADS, 48, length), BF),
        pltpu.VMEM((D, length), F32),
    ]


def by(shard, k):
    return lax.ppermute(shard, "mp", [(i, i ^ k) for i in range(MP)])


def on_device(
    frames, intra_qkv, intra_out, intra_up, intra_down, inter_qkv, inter_out, inter_up, inter_down
):
    seq_count = lax.axis_size("seq")
    mine = lax.axis_index("mp").reshape(1)
    count = frames.shape[0]
    total = count * seq_count

    first = jnp.transpose(intra_qkv, (1, 2, 0)).reshape(-1, D)
    across = by(first, 2)
    first = [first, by(first, 1), across, by(across, 1)]
    rest = (
        jnp.transpose(inter_qkv, (1, 2, 0)).reshape(-1, D),
        inter_out,
        inter_up,
        inter_down,
        intra_out,
        intra_up,
        intra_down,
    )
    rest = pl.pallas_call(
        pack,
        out_shape=jax.ShapeDtypeStruct((1344, D), BF),
        in_specs=[IN_VMEM] * len(rest),
        out_specs=IN_VMEM,
        compiler_params=params(4),
        name="pack",
    )(*rest)
    rest, first[2] = lax.optimization_barrier((rest, across))
    rest = [rest, by(rest, 1), by(rest, 2)]

    rows, own_frames = pl.pallas_call(
        prepare,
        out_shape=(
            jax.ShapeDtypeStruct((count, 256, D), BF),
            jax.ShapeDtypeStruct((2, 32, count, D), BF),
        ),
        grid_spec=pltpu.PrefetchScalarGridSpec(
            num_scalar_prefetch=1,
            in_specs=[IN_VMEM],
            out_specs=[IN_VMEM] * 2,
            scratch_shapes=[pltpu.VMEM((16 * count, 16 * count), BF)],
        ),
        compiler_params=params(24),
        cost_estimate=pl.CostEstimate(flops=4 * 10**9, bytes_accessed=8 * 10**6, transcendentals=10**4),
        name="prepare",
    )(mine, jnp.transpose(frames, (1, 0, 2)))

    group = 4
    steps = count // group // 2
    attended = []
    for part in range(2):
        found = pl.pallas_call(
            intra_attention,
            out_shape=jax.ShapeDtypeStruct((count // 2, 64, D), BF),
            grid_spec=pltpu.PrefetchScalarGridSpec(
                num_scalar_prefetch=1,
                grid=(steps,),
                in_specs=[
                    pl.BlockSpec((group, 256, D), lambda i, *_, part=part: (i + steps * part, 0, 0))
                ]
                + [whole((192, D))] * 4,
                out_specs=pl.BlockSpec((group, 64, D), lambda i, *_: (i, 0, 0)),
                scratch_shapes=[pltpu.VMEM((3, D, D), BF)],
            ),
            compiler_params=params(20),
            cost_estimate=pl.CostEstimate(
                flops=5 * 10**9, bytes_accessed=2 * 10**6, transcendentals=15 * 10**5
            ),
            name="intra_attention",
        )(mine, rows, *first)
        if part == 0:
            rest[2], found = lax.optimization_barrier((rest[2], found))
            rest.append(by(rest[2], 1))
        attended.append(found)

    sent = pl.pallas_call(
        intra_feed_forward,
        out_shape=jax.ShapeDtypeStruct((seq_count, 2, count, D), BF),
        in_specs=[IN_VMEM] * 7,
        out_specs=IN_VMEM,
        compiler_params=params(24),
        cost_estimate=pl.CostEstimate(flops=3 * 10**9, bytes_accessed=3 * 10**6, transcendentals=0),
        name="intra_feed_forward",
    )(*attended, own_frames, *rest)
    sent = sent.reshape(seq_count, 2 * count, D)
    got = lax.all_to_all(sent, "seq", split_axis=0, concat_axis=0, tiled=True)
    summed = pl.pallas_call(
        inter_layer,
        out_shape=jax.ShapeDtypeStruct((total, D), BF),
        in_specs=[IN_VMEM] * 5,
        out_specs=IN_VMEM,
        scratch_shapes=attention_scratch(total),
        compiler_params=params(32),
        cost_estimate=pl.CostEstimate(flops=3 * 10**10, bytes_accessed=4 * 10**6, transcendentals=10**7),
        name="inter_layer",
    )(got.reshape(seq_count, 2, count, D), *rest)

    back = summed.reshape(seq_count, count, D)
    back = lax.all_to_all(back, "seq", split_axis=0, concat_axis=0, tiled=True)
    across = by(back, 2)
    pieces = [back, by(back, 1), across, by(across, 1)]
    return pl.pallas_call(
        assemble,
        out_shape=jax.ShapeDtypeStruct((HALF * count, D), BF),
        grid_spec=pltpu.PrefetchScalarGridSpec(
            num_scalar_prefetch=1,
            in_specs=[IN_VMEM] * 4,
            out_specs=IN_VMEM,
            scratch_shapes=[pltpu.VMEM((count, 128, D), BF)],
        ),
        compiler_params=params(12),
        cost_estimate=pl.CostEstimate(flops=10**9, bytes_accessed=4 * 10**6, transcendentals=0),
        name="assemble",
    )(mine, *pieces)


def solution(mesh):
    return jax.shard_map(
        on_device,
        mesh=mesh,
        in_specs=(
            P("seq", None, None),
            P(None, None, "mp"),
            P("mp", None),
            P(None, "mp"),
            P("mp", None),
            P(None, None, "mp"),
            P("mp", None),
            P(None, "mp"),
            P("mp", None),
        ),
        out_specs=P("seq", None),
        check_vma=False,
    )
```

time: 142 us -> 111 us (0.78)
  waiting for transfers between devices: 23.4 us -> 10.2 us
  Pallas kernels: 55.7 us -> 43.7 us
  local copies, waits for them, and re-layouts: 10.9 us -> 7.89 us
  starting transfers between devices: 15.7 us -> 14.1 us
    ppermute x9, waiting for transfers between devices: 23.4 us -> 10.2 us  [by(): return lax.ppermute(shard, 'mp', [(i, i ^ k) for i in range(MP)])]
    pallas_call x4, Pallas kernels: 22.4 us -> 14.7 us  [the longest x2 10.8 us: on_device(): pl.pallas_call(intra_attention, out_shape=jax.ShapeDtypeStruct((count //...]
    pallas_call x1, Pallas kernels: 22.3 us -> 19.1 us  [on_device(): pl.pallas_call(inter_layer, out_shape=jax.ShapeDtypeStruct((total, D), BF...]
    unnamed x25 -> x18, local copies, waits for them, and re-layouts: 10.9 us -> 7.89 us
    ppermute x9, starting transfers between devices: 15.7 us -> 14.1 us  [by(): return lax.ppermute(shard, 'mp', [(i, i ^ k) for i in range(MP)])]
  transfers between devices with their start and end apart: 9 -> 9, of which waited for: 3 -> 3; matrix products, arithmetic and copies ran while one was open for 4% -> 0% of each run, Pallas kernels for 15% -> 17%
where the time goes in v3:
time: 111 us; the launch traced here: 110 us
  Pallas kernels  43.7 us (39%)
  blocking collectives  34.4 us (31%)
  starting transfers between devices  14.1 us (13%)
  waiting for transfers between devices  10.2 us (9%)
  local copies, waits for them, and re-layouts  7.89 us (7%)
    all_to_all x1, blocking collectives, on_device(): got = lax.all_to_all(sent, 'seq', split_axis=0, concat_axis=0, tiled=True)  21.9 us
    pallas_call x1, Pallas kernels, on_device(): pl.pallas_call(inter_layer, out_shape=jax.ShapeDtypeStruct((total, D), BF...  19.1 us
    ppermute x9, starting transfers between devices, by(): return lax.ppermute(shard, 'mp', [(i, i ^ k) for i in range(MP)])  14.1 us
    all_to_all x1, blocking collectives, on_device(): back = lax.all_to_all(back, 'seq', split_axis=0, concat_axis=0, tiled=True)  12.5 us
    pallas_call x2, Pallas kernels, on_device(): pl.pallas_call(intra_attention, out_shape=jax.ShapeDtypeStruct((count //...  10.8 us
    ppermute x9, waiting for transfers between devices, by(): return lax.ppermute(shard, 'mp', [(i, i ^ k) for i in range(MP)])  10.2 us
    unnamed x18, local copies, waits for them, and re-layouts  7.89 us
    pallas_call x1, Pallas kernels, on_device(): pl.pallas_call(prepare, out_shape=(jax.ShapeDtypeStruct((count, 256, D),...  7.64 us
  transfers between devices with their start and end apart: 9, of which 3 were waited for; matrix products, arithmetic and copies ran while one was open for 0% of the time, Pallas kernels for 17%

profile of v3, /device:TPU:1, one launch (start us, length us, event | category | flops | bytes accessed | tf_op | source)
XLA Modules:
  0.0 110.4 jit_solution(17254190843573614481)
XLA Ops:
  0.0 4.4 %collective-permute-start = (bf16[192,256]{1,0:T(8,128)(2,1)}, bf16[192,256]{1,0:T(8,128)(2,1)S(1)}, u32[]{:S(2)}, u32[]{:S(2)}) collective-permute-start(bf16[192,256]{1,0:T(8,128)(2,1)} %bitcast.16), channel_id=1, source_target_pairs={{0,2},{1,3},{2,0},{3,1},{4,6},{5,7},{6,4},{7,5},{8,10},{9,11},{10,... | collective-permute-start | bytes 294920 | tf_op jit(solution)/shard_map/ppermute | solution.py:262
  4.4 1.0 collective-permute-start.2
  5.4 0.0 copy-start
  5.4 0.9 copy-done
  6.3 0.0 copy-start.1
  6.3 0.9 copy-done.1
  7.2 0.0 copy-start.2
  7.2 0.9 copy-done.2
  8.1 0.0 copy-start.3
  8.1 0.9 copy-done.3
  9.0 0.0 copy-start.4
  9.0 0.9 copy-done.4
  9.9 0.0 copy-start.5
  9.9 0.8 copy-done.5
  10.7 0.0 copy-start.6
  10.7 0.8 copy-done.6
  11.5 0.0 collective-permute-done.w2
  11.5 0.1 collective-permute-start.1
  11.6 0.1 collective-permute-start.3
  11.7 0.0 copy-start.7
  11.7 1.9 %copy-done.7 = bf16[24,250,256]{2,0,1:T(8,128)(2,1)S(1)} copy-done((bf16[24,250,256]{2,0,1:T(8,128)(2,1)S(1)}, bf16[24,250,256]{2,0,1:T(8,128)(2,1)}, u32[]{:S(2)}) %copy-start.7) | copy-done | bytes 3072024
  13.6 0.0 copy-start.8
  13.6 7.6 %prepare.1 = (bf16[24,256,256]{2,1,0:T(8,128)(2,1)S(1)}, bf16[2,32,24,256]{3,2,1,0:T(8,128)(2,1)S(1)}) custom-call(s32[1]{0:T(128)} %bitcast.mine_ref, bf16[250,24,256]{2,1,0:T(8,128)(2,1)S(1)} %bitcast.15), custom_call_target="tpu_custom_call" | custom-call | flops 4000000000 | bytes 8000000 | tf_op jit(solution)/shard_map/prepare/pallas_call | solution.py:296
  21.2 0.5 collective-permute-start.4
  21.7 0.0 collective-permute-done.2.w1
  21.8 0.0 collective-permute-done.3.w3
  21.8 0.0 copy-done.8
  21.8 5.4 %intra_attention.2.a0_ref = bf16[12,64,256]{2,1,0:T(8,128)(2,1)S(1)} custom-call(s32[1]{0:T(128)} %bitcast.mine_ref, bf16[24,256,256]{2,1,0:T(8,128)(2,1)S(1)} %get-tuple-element.12.n_ref, bf16[192,256]{1,0:T(8,128)(2,1)S(1)} %bitcast.18, bf16[192,256]{1,0:T(8,128)(2,1)S(1)} %collective-permute-done.2.w1, bf16[192,256]{1,0:T(8,128)(2,1)S(1)} %collective-permute-done.w2, ...), custom_call_target="tpu_custom_call" | custom-call | flops 5000000000 | bytes 2000000 | tf_op jit(solution)/shard_map/intra_attention/pallas_call | solution.py:317
  27.2 2.9 %collective-permute-done.1.w2 = bf16[1344,256]{1,0:T(8,128)(2,1)S(1)} collective-permute-done((bf16[1344,256]{1,0:T(8,128)(2,1)S(1)}, bf16[1344,256]{1,0:T(8,128)(2,1)S(1)}, u32[]{:S(2)}, u32[]{:S(2)}) %collective-permute-start.1) | collective-permute-done | bytes 688160 | tf_op jit(solution)/shard_map/ppermute | solution.py:262
  30.1 0.8 collective-permute-start.5
  30.9 5.4 %intra_attention.3.a1_ref = bf16[12,64,256]{2,1,0:T(8,128)(2,1)S(1)} custom-call(s32[1]{0:T(128)} %bitcast.mine_ref, bf16[24,256,256]{2,1,0:T(8,128)(2,1)S(1)} %get-tuple-element.12.n_ref, bf16[192,256]{1,0:T(8,128)(2,1)S(1)} %bitcast.19, bf16[192,256]{1,0:T(8,128)(2,1)S(1)} %collective-permute-done.2.w1, bf16[192,256]{1,0:T(8,128)(2,1)S(1)} %collective-permute-done.w2, ...), custom_call_target="tpu_custom_call" | custom-call | flops 5000000000 | bytes 2000000 | tf_op jit(solution)/shard_map/intra_attention/pallas_call | solution.py:317
  36.3 0.0 collective-permute-done.4.w1
  36.3 0.0 collective-permute-done.5.w3
  36.3 3.9 %intra_feed_forward.1 = bf16[32,2,24,256]{3,2,1,0:T(8,128)(2,1)S(1)} custom-call(bf16[12,64,256]{2,1,0:T(8,128)(2,1)S(1)} %intra_attention.2.a0_ref, bf16[12,64,256]{2,1,0:T(8,128)(2,1)S(1)} %intra_attention.3.a1_ref, bf16[2,32,24,256]{3,2,1,0:T(8,128)(2,1)S(1)} %get-tuple-element.15.xq_ref, bf16[1344,256]{1,0:T(8,128)(2,1)S(1)} %pack.1.w0, ...), custom_call_target="tpu_custom_call" | custom-call | flops 3000000000 | bytes 3000000 | tf_op jit(solution)/shard_map/intra_feed_forward/pallas_call | solution.py:341
  40.2 21.9 %all_to_all.10 = bf16[32,48,256]{2,1,0:T(8,128)(2,1)S(1)} all-to-all(bf16[32,48,256]{2,1,0:T(8,128)(2,1)S(1)} %bitcast.12), channel_id=1, replica_groups=mesh['seq'=32,'mp'=4] {'seq'}, dimensions={0} | all-to-all | bytes 1572864 | tf_op jit(solution)/shard_map/all_to_all | solution.py:351
  62.1 19.1 %inter_layer.1 = bf16[768,256]{1,0:T(8,128)(2,1)S(1)} custom-call(bf16[32,2,24,256]{3,2,1,0:T(8,128)(2,1)S(1)} %bitcast.11, bf16[1344,256]{1,0:T(8,128)(2,1)S(1)} %pack.1.w0, bf16[1344,256]{1,0:T(8,128)(2,1)S(1)} %collective-permute-done.4.w1, bf16[1344,256]{1,0:T(8,128)(2,1)S(1)} %collective-permute-done.1.w2, bf16[1344,256]{1,0:T(8,128)(2,1)S(1)} %collective-permute-done.5.w3), custom_call_target="tpu_custom_call" | custom-call | flops 30000001024 | bytes 4000000 | tf_op jit(solution)/shard_map/inter_layer/pallas_call | solution.py:352
  81.2 12.5 %all_to_all.11.p0 = bf16[32,24,256]{2,1,0:T(8,128)(2,1)S(1)} all-to-all(bf16[32,24,256]{2,1,0:T(8,128)(2,1)S(1)} %bitcast.13), channel_id=1, replica_groups=mesh['seq'=32,'mp'=4] {'seq'}, dimensions={0} | all-to-all | bytes 786432 | tf_op jit(solution)/shard_map/all_to_all | solution.py:364
  93.7 0.9 collective-permute-start.7
  94.6 2.8 %collective-permute-start.6 = (bf16[32,24,256]{2,1,0:T(8,128)(2,1)S(1)}, bf16[32,24,256]{2,1,0:T(8,128)(2,1)S(1)}, u32[]{:S(2)}, u32[]{:S(2)}) collective-permute-start(bf16[32,24,256]{2,1,0:T(8,128)(2,1)S(1)} %all_to_all.11.p0), channel_id=1, source_target_pairs={{0,1},{1,0},{2,3},{3,2},{4,5},{5,4},{6,7},{7,6},{8,9},{9,8},{10,11... | collective-permute-start | bytes 1179656 | tf_op jit(solution)/shard_map/ppermute | solution.py:262
  97.4 5.8 %collective-permute-done.7.p2 = bf16[32,24,256]{2,1,0:T(8,128)(2,1)S(1)} collective-permute-done((bf16[32,24,256]{2,1,0:T(8,128)(2,1)S(1)}, bf16[32,24,256]{2,1,0:T(8,128)(2,1)S(1)}, u32[]{:S(2)}, u32[]{:S(2)}) %collective-permute-start.7) | collective-permute-done | bytes 393248 | tf_op jit(solution)/shard_map/ppermute | solution.py:262
  103.2 3.5 %collective-permute-start.8 = (bf16[32,24,256]{2,1,0:T(8,128)(2,1)S(1)}, bf16[32,24,256]{2,1,0:T(8,128)(2,1)S(1)}, u32[]{:S(2)}, u32[]{:S(2)}) collective-permute-start(bf16[32,24,256]{2,1,0:T(8,128)(2,1)S(1)} %collective-permute-done.7.p2), channel_id=1, source_target_pairs={{0,1},{1,0},{2,3},{3,2},{4,5},{5,4},{6,7},{7,6},{8,9},{9,8},{10,11... | collective-permute-start | bytes 1179656 | tf_op jit(solution)/shard_map/ppermute | solution.py:262
  106.7 0.0 collective-permute-done.6.p1
  106.7 1.3 %collective-permute-done.8.p3 = bf16[32,24,256]{2,1,0:T(8,128)(2,1)S(1)} collective-permute-done((bf16[32,24,256]{2,1,0:T(8,128)(2,1)S(1)}, bf16[32,24,256]{2,1,0:T(8,128)(2,1)S(1)}, u32[]{:S(2)}, u32[]{:S(2)}) %collective-permute-start.8) | collective-permute-done | bytes 393248 | tf_op jit(solution)/shard_map/ppermute | solution.py:262
  108.1 2.3 %assemble.1 = bf16[3000,256]{1,0:T(8,128)(2,1)} custom-call(s32[1]{0:T(128)} %bitcast.mine_ref, bf16[32,24,256]{2,1,0:T(8,128)(2,1)S(1)} %all_to_all.11.p0, bf16[32,24,256]{2,1,0:T(8,128)(2,1)S(1)} %collective-permute-done.6.p1, bf16[32,24,256]{2,1,0:T(8,128)(2,1)S(1)} %collective-permute-done.7.p2, bf16[32,24,256]{2,1,0:T(8,128)(2,1)S(1)} %collective-permute-done.8.p3), custom_call_target="tpu_custom_call" | custom-call | flops 1000000000 | bytes 4000000 | tf_op jit(solution)/shard_map/assemble/pallas_call | solution.py:367
  (1 shorter events, 0.0 us)
Async XLA Ops:
  0.0 11.5 %collective-permute-start = (bf16[192,256]{1,0:T(8,128)(2,1)}, bf16[192,256]{1,0:T(8,128)(2,1)S(1)}, u32[]{:S(2)}, u32[]{:S(2)}) collective-permute-start(bf16[192,256]{1,0:T(8,128)(2,1)} %bitcast.16), channel_id=1, source_target_pairs={{0,2},{1,3},{2,0},{3,1},{4,6},{5,7},{6,4},{7,5},{8,10},{9,11},{10,... | collective-permute-start | bytes 294920 | tf_op jit(solution)/shard_map/ppermute | solution.py:262
  4.4 17.3 %collective-permute-start.2 = (bf16[192,256]{1,0:T(8,128)(2,1)}, bf16[192,256]{1,0:T(8,128)(2,1)S(1)}, u32[]{:S(2)}, u32[]{:S(2)}) collective-permute-start(bf16[192,256]{1,0:T(8,128)(2,1)} %bitcast.17), channel_id=1, source_target_pairs={{0,1},{1,0},{2,3},{3,2},{4,5},{5,4},{6,7},{7,6},{8,9},{9,8},{10,11... | collective-permute-start | bytes 294920 | tf_op jit(solution)/shard_map/ppermute | solution.py:262
  5.4 0.9 copy-start
  6.3 0.9 copy-start.1
  7.2 0.9 copy-start.2
  8.1 0.9 copy-start.3
  9.0 0.9 copy-start.4
  9.9 0.8 copy-start.5
  10.7 0.8 copy-start.6
  11.5 18.6 %collective-permute-start.1 = (bf16[1344,256]{1,0:T(8,128)(2,1)S(1)}, bf16[1344,256]{1,0:T(8,128)(2,1)S(1)}, u32[]{:S(2)}, u32[]{:S(2)}) collective-permute-start(bf16[1344,256]{1,0:T(8,128)(2,1)S(1)} %pack.1.w0), channel_id=1, source_target_pairs={{0,2},{1,3},{2,0},{3,1},{4,6},{5,7},{6,4},{7,5},{8,10},{9,11},{10,... | collective-permute-start | bytes 2064392 | tf_op jit(solution)/shard_map/ppermute | solution.py:262
  11.6 10.2 %collective-permute-start.3 = (bf16[192,256]{1,0:T(8,128)(2,1)S(1)}, bf16[192,256]{1,0:T(8,128)(2,1)S(1)}, u32[]{:S(2)}, u32[]{:S(2)}) collective-permute-start(bf16[192,256]{1,0:T(8,128)(2,1)S(1)} %collective-permute-done.w2), channel_id=1, source_target_pairs={{0,1},{1,0},{2,3},{3,2},{4,5},{5,4},{6,7},{7,6},{8,9},{9,8},{10,11... | collective-permute-start | bytes 294920 | tf_op jit(solution)/shard_map/ppermute | solution.py:262
  11.7 1.9 %copy-start.7 = (bf16[24,250,256]{2,0,1:T(8,128)(2,1)S(1)}, bf16[24,250,256]{2,0,1:T(8,128)(2,1)}, u32[]{:S(2)}) copy-start(bf16[24,250,256]{2,0,1:T(8,128)(2,1)} %param.9) | copy-start | bytes 9216004
  13.6 8.2 %copy-start.8 = (bf16[256,3,64]{0,2,1:T(8,128)(2,1)S(1)}, bf16[256,3,64]{0,2,1:T(8,128)(2,1)}, u32[]{:S(2)}) copy-start(bf16[256,3,64]{0,2,1:T(8,128)(2,1)} %param.10) | copy-start | bytes 294916
  21.2 15.1 %collective-permute-start.4 = (bf16[1344,256]{1,0:T(8,128)(2,1)S(1)}, bf16[1344,256]{1,0:T(8,128)(2,1)S(1)}, u32[]{:S(2)}, u32[]{:S(2)}) collective-permute-start(bf16[1344,256]{1,0:T(8,128)(2,1)S(1)} %pack.1.w0), channel_id=1, source_target_pairs={{0,1},{1,0},{2,3},{3,2},{4,5},{5,4},{6,7},{7,6},{8,9},{9,8},{10,11... | collective-permute-start | bytes 2064392 | tf_op jit(solution)/shard_map/ppermute | solution.py:262
  30.1 6.2 %collective-permute-start.5 = (bf16[1344,256]{1,0:T(8,128)(2,1)S(1)}, bf16[1344,256]{1,0:T(8,128)(2,1)S(1)}, u32[]{:S(2)}, u32[]{:S(2)}) collective-permute-start(bf16[1344,256]{1,0:T(8,128)(2,1)S(1)} %collective-permute-done.1.w2), channel_id=1, source_target_pairs={{0,1},{1,0},{2,3},{3,2},{4,5},{5,4},{6,7},{7,6},{8,9},{9,8},{10,11... | collective-permute-start | bytes 2064392 | tf_op jit(solution)/shard_map/ppermute | solution.py:262
  93.7 9.5 %collective-permute-start.7 = (bf16[32,24,256]{2,1,0:T(8,128)(2,1)S(1)}, bf16[32,24,256]{2,1,0:T(8,128)(2,1)S(1)}, u32[]{:S(2)}, u32[]{:S(2)}) collective-permute-start(bf16[32,24,256]{2,1,0:T(8,128)(2,1)S(1)} %all_to_all.11.p0), channel_id=1, source_target_pairs={{0,2},{1,3},{2,0},{3,1},{4,6},{5,7},{6,4},{7,5},{8,10},{9,11},{10,... | collective-permute-start | bytes 1179656 | tf_op jit(solution)/shard_map/ppermute | solution.py:262
  94.6 12.2 %collective-permute-start.6 = (bf16[32,24,256]{2,1,0:T(8,128)(2,1)S(1)}, bf16[32,24,256]{2,1,0:T(8,128)(2,1)S(1)}, u32[]{:S(2)}, u32[]{:S(2)}) collective-permute-start(bf16[32,24,256]{2,1,0:T(8,128)(2,1)S(1)} %all_to_all.11.p0), channel_id=1, source_target_pairs={{0,1},{1,0},{2,3},{3,2},{4,5},{5,4},{6,7},{7,6},{8,9},{9,8},{10,11... | collective-permute-start | bytes 1179656 | tf_op jit(solution)/shard_map/ppermute | solution.py:262
  103.2 4.9 %collective-permute-start.8 = (bf16[32,24,256]{2,1,0:T(8,128)(2,1)S(1)}, bf16[32,24,256]{2,1,0:T(8,128)(2,1)S(1)}, u32[]{:S(2)}, u32[]{:S(2)}) collective-permute-start(bf16[32,24,256]{2,1,0:T(8,128)(2,1)S(1)} %collective-permute-done.7.p2), channel_id=1, source_target_pairs={{0,1},{1,0},{2,3},{3,2},{4,5},{5,4},{6,7},{7,6},{8,9},{9,8},{10,11... | collective-permute-start | bytes 1179656 | tf_op jit(solution)/shard_map/ppermute | solution.py:262

commit v4 on v3

--- a/solution.py
+++ b/solution.py
@@ -17,6 +17,7 @@
 F32 = jnp.float32
 Q_SCALE = 1.4426950408889634 * HD ** (-0.5)
 LOW = -1e30
+IN_HBM = pl.BlockSpec(memory_space=pltpu.HBM)
 IN_VMEM = pl.BlockSpec(memory_space=pltpu.VMEM)
 
 
@@ -80,15 +81,24 @@
 
 
 def pack(*refs):
-    sources, packed_ref = refs[:-1], refs[-1]
-    at = 0
-    for source in sources:
-        packed_ref[at : at + source.shape[0], :] = source[...]
+    sources, packed_ref, sems = refs[:-2], refs[-2], refs[-1]
+    copies, at = [], 0
+    for k, source in enumerate(sources):
+        into = packed_ref.at[pl.ds(at, source.shape[0])]
+        copies.append(pltpu.make_async_copy(source, into, sems.at[k]))
+        copies[-1].start()
         at += source.shape[0]
-
-
-def prepare(mine_ref, x_ref, n_ref, xq_ref, turn_ref):
+    for copy in copies:
+        copy.wait()
+
+
+def prepare(mine_ref, frames_ref, n_ref, xq_ref, x_ref, turn_ref, sems):
     count = x_ref.shape[1]
+    copies = []
+    for k, (at, to) in enumerate(((0, 64), (64, HALF), (HALF, 189), (189, K))):
+        part = pl.ds(at, to - at)
+        copies.append(pltpu.make_async_copy(frames_ref.at[part], x_ref.at[part], sems.at[k]))
+        copies[-1].start()
     turn_ref[...] = swapped(count, 4).T
 
     def put(to, x):
@@ -107,8 +117,14 @@
         put(128 + at, x_ref[pl.ds(HALF + at, 16)])
         return carry
 
-    lax.fori_loop(0, 8, early, 0)
-    lax.fori_loop(0, 7, late, 0)
+    copies[0].wait()
+    lax.fori_loop(0, 4, early, 0, unroll=True)
+    copies[1].wait()
+    copies[2].wait()
+    lax.fori_loop(4, 8, early, 0, unroll=True)
+    lax.fori_loop(0, 4, late, 0, unroll=True)
+    copies[3].wait()
+    lax.fori_loop(4, 7, late, 0, unroll=True)
     put(240, jnp.concatenate([x_ref[HALF + 112 : K], x_ref[K - 3 : K]], axis=0))
 
     def residual(j, carry):
@@ -176,7 +192,7 @@
 
 def intra_feed_forward(a0_ref, a1_ref, xq_ref, w0, w1, w2, w3, o_ref):
     shards = (w0, w1, w2, w3)
-    count = 2 * a0_ref.shape[0]
+    count = xq_ref.shape[2]
     out = jnp.concatenate([w[768:832, :] for w in shards], axis=0)
     up = [w[832:1088, :] for w in shards]
     down = [w[1088:1344, :] for w in shards]
@@ -188,7 +204,7 @@
                 taken = [
                     ref[u, at : at + 8, :].astype(F32)
                     for ref in (a0_ref, a1_ref)
-                    for u in range(count // 2)
+                    for u in range(ref.shape[0])
                 ]
                 rows.append(dot(turn, jnp.concatenate(taken, axis=0).astype(BF)).astype(BF))
             attended = jnp.concatenate(rows, axis=0)
@@ -199,11 +215,11 @@
             o_ref[part, half] = done.reshape(16, count, D).astype(BF)
 
 
-def inter_layer(x_ref, w0, w1, w2, w3, o_ref, weights_ref, query_ref, key_ref, value_ref, attended_ref):
+def inter_layer(x_ref, w0, w1, w2, w3, o_ref, weights_ref, query_ref, key_ref, value_ref, attended_ref, later_ref):
     shards = (w0, w1, w2, w3)
     put_attention_weights(shards, weights_ref)
     for half in (1, 0):
-        x = x_ref[:, half].astype(F32).reshape(o_ref.shape)
+        x = x_ref[:, half].astype(F32).reshape(later_ref.shape)
         project(normed(x), weights_ref, query_ref, key_ref, value_ref)
 
         def block(i, carry):
@@ -219,17 +235,19 @@
         )
         if half == 1:
             first = lax.broadcasted_iota(jnp.int32, done.shape, 0) == 0
-            o_ref[...] = jnp.where(first, 0.0, pltpu.roll(done.astype(F32), 1, 0)).astype(BF)
+            later_ref[...] = jnp.where(first, 0.0, pltpu.roll(done.astype(F32), 1, 0))
         else:
-            o_ref[...] = (done.astype(F32) + o_ref[...].astype(F32)).astype(BF)
-
-
-def assemble(mine_ref, p0, p1, p2, p3, o_ref, rows_ref):
+            summed = (done.astype(F32) + later_ref[...]).reshape(x_ref.shape[0], *x_ref.shape[2:])
+            for copy in range(2):
+                o_ref[:, copy] = summed.astype(BF)
+
+
+def assemble(mine_ref, p0, p1, o_ref, rows_ref):
     turn = swapped(32, 3)
-    for k, piece in enumerate((p0, p1, p2, p3)):
-        at = pl.multiple_of((mine_ref[0] ^ k) * 32, 32)
+    for piece, core, z in ((p, core, z) for core, p in enumerate((p0, p1)) for z in range(2)):
+        at = pl.multiple_of((2 * z + ((mine_ref[0] & 1) ^ core)) * 32, 32)
         for part in range(3):
-            taken = [piece[s, 8 * part : 8 * part + 8, :].astype(F32) for s in range(32)]
+            taken = [piece[2 * s + z, 8 * part : 8 * part + 8, :].astype(F32) for s in range(32)]
             rows = dot(turn, jnp.concatenate(taken, axis=0).astype(BF)).astype(BF)
             for u in range(8):
                 rows_ref[8 * part + u, pl.ds(at, 32), :] = rows[32 * u : 32 * u + 32]
@@ -285,11 +303,12 @@
     rest = pl.pallas_call(
         pack,
         out_shape=jax.ShapeDtypeStruct((1344, D), BF),
-        in_specs=[IN_VMEM] * len(rest),
+        in_specs=[IN_HBM] * len(rest),
         out_specs=IN_VMEM,
+        scratch_shapes=[pltpu.SemaphoreType.DMA((len(rest),))],
         compiler_params=params(4),
         name="pack",
-    )(*rest)
+    )(*[pltpu.with_memory_space_constraint(a, pltpu.HBM) for a in rest])
     rest, first[2] = lax.optimization_barrier((rest, across))
     rest = [rest, by(rest, 1), by(rest, 2)]
 
@@ -301,27 +320,30 @@
         ),
         grid_spec=pltpu.PrefetchScalarGridSpec(
             num_scalar_prefetch=1,
-            in_specs=[IN_VMEM],
+            in_specs=[IN_HBM],
             out_specs=[IN_VMEM] * 2,
-            scratch_shapes=[pltpu.VMEM((16 * count, 16 * count), BF)],
+            scratch_shapes=[
+                pltpu.VMEM((K, count, D), BF),
+                pltpu.VMEM((16 * count, 16 * count), BF),
+                pltpu.SemaphoreType.DMA((4,)),
+            ],
         ),
         compiler_params=params(24),
         cost_estimate=pl.CostEstimate(flops=4 * 10**9, bytes_accessed=8 * 10**6, transcendentals=10**4),
         name="prepare",
-    )(mine, jnp.transpose(frames, (1, 0, 2)))
+    )(mine, pltpu.with_memory_space_constraint(jnp.transpose(frames, (1, 0, 2)), pltpu.HBM))
 
     group = 4
-    steps = count // group // 2
     attended = []
-    for part in range(2):
+    for start, steps in ((0, 4), (4, 2)):
         found = pl.pallas_call(
             intra_attention,
-            out_shape=jax.ShapeDtypeStruct((count // 2, 64, D), BF),
+            out_shape=jax.ShapeDtypeStruct((group * steps, 64, D), BF),
             grid_spec=pltpu.PrefetchScalarGridSpec(
                 num_scalar_prefetch=1,
                 grid=(steps,),
                 in_specs=[
-                    pl.BlockSpec((group, 256, D), lambda i, *_, part=part: (i + steps * part, 0, 0))
+                    pl.BlockSpec((group, 256, D), lambda i, *_, start=start: (i + start, 0, 0))
                 ]
                 + [whole((192, D))] * 4,
                 out_specs=pl.BlockSpec((group, 64, D), lambda i, *_: (i, 0, 0)),
@@ -333,7 +355,7 @@
             ),
             name="intra_attention",
         )(mine, rows, *first)
-        if part == 0:
+        if start == 0:
             rest[2], found = lax.optimization_barrier((rest[2], found))
             rest.append(by(rest[2], 1))
         attended.append(found)
@@ -351,25 +373,28 @@
     got = lax.all_to_all(sent, "seq", split_axis=0, concat_axis=0, tiled=True)
     summed = pl.pallas_call(
         inter_layer,
-        out_shape=jax.ShapeDtypeStruct((total, D), BF),
+        out_shape=jax.ShapeDtypeStruct((seq_count, 2, count, D), BF),
         in_specs=[IN_VMEM] * 5,
         out_specs=IN_VMEM,
-        scratch_shapes=attention_scratch(total),
+        scratch_shapes=attention_scratch(total) + [pltpu.VMEM((total, D), F32)],
         compiler_params=params(32),
         cost_estimate=pl.CostEstimate(flops=3 * 10**10, bytes_accessed=4 * 10**6, transcendentals=10**7),
         name="inter_layer",
     )(got.reshape(seq_count, 2, count, D), *rest)
 
-    back = summed.reshape(seq_count, count, D)
-    back = lax.all_to_all(back, "seq", split_axis=0, concat_axis=0, tiled=True)
-    across = by(back, 2)
-    pieces = [back, by(back, 1), across, by(across, 1)]
+    back = summed.reshape(2 * seq_count, count, D)
+    chips = [(s, z) for s in range(seq_count) for z in range(2)]
+    groups = [[MP * s + 2 * z + core for s, z in chips] for core in range(2)]
+    back = lax.all_to_all(
+        back, ("seq", "mp"), split_axis=0, concat_axis=0, tiled=True, axis_index_groups=groups
+    )
+    pieces = [back, by(back, 1)]
     return pl.pallas_call(
         assemble,
         out_shape=jax.ShapeDtypeStruct((HALF * count, D), BF),
         grid_spec=pltpu.PrefetchScalarGridSpec(
             num_scalar_prefetch=1,
-            in_specs=[IN_VMEM] * 4,
+            in_specs=[IN_VMEM] * 2,
             out_specs=IN_VMEM,
             scratch_shapes=[pltpu.VMEM((count, 128, D), BF)],
         ),

time: 111 us -> 103 us (0.928)
  blocking collectives: 34.4 us -> 42.7 us
  local copies, waits for them, and re-layouts: 7.89 us -> 0.01 us
  waiting for transfers between devices: 10.2 us -> 2.91 us
  Pallas kernels: 43.7 us -> 42.1 us
    all_to_all x1, blocking collectives: 12.5 us -> 21 us  [on_device(): lax.all_to_all(back, ('seq', 'mp'), split_axis=0, concat_axis=0, tiled=Tr...]
    unnamed x18 -> x2, local copies, waits for them, and re-layouts: 7.89 us -> 0.01 us
    ppermute x9 -> x7, waiting for transfers between devices: 10.2 us -> 2.91 us  [by(): return lax.ppermute(shard, 'mp', [(i, i ^ k) for i in range(MP)])]
    pallas_call x1, Pallas kernels: 7.64 us -> 4.84 us  [on_device(): pl.pallas_call(prepare, out_shape=(jax.ShapeDtypeStruct((count, 256, D),...]
    pallas_call x1, Pallas kernels: 0.05 us -> 1.24 us  [on_device(): pl.pallas_call(pack, out_shape=jax.ShapeDtypeStruct((1344, D), BF), in_sp...]
    ppermute x9 -> x7, starting transfers between devices: 14.1 us -> 14.8 us  [by(): return lax.ppermute(shard, 'mp', [(i, i ^ k) for i in range(MP)])]
  transfers between devices with their start and end apart: 9 -> 7, of which waited for: 3 -> 3; matrix products, arithmetic and copies ran while one was open for 0% -> 0% of each run, Pallas kernels for 17% -> 16%
where the time goes in v4:
time: 103 us
  blocking collectives  42.7 us (41%)
  Pallas kernels  42.1 us (41%)
  starting transfers between devices  14.8 us (14%)
  waiting for transfers between devices  2.91 us (3%)
    all_to_all x1, blocking collectives, on_device(): got = lax.all_to_all(sent, 'seq', split_axis=0, concat_axis=0, tiled=True)  21.6 us
    all_to_all x1, blocking collectives, on_device(): lax.all_to_all(back, ('seq', 'mp'), split_axis=0, concat_axis=0, tiled=Tr...  21 us
    pallas_call x1, Pallas kernels, on_device(): pl.pallas_call(inter_layer, out_shape=jax.ShapeDtypeStruct((seq_count, 2,...  19.1 us
    ppermute x7, starting transfers between devices, by(): return lax.ppermute(shard, 'mp', [(i, i ^ k) for i in range(MP)])  14.8 us
    pallas_call x2, Pallas kernels, on_device(): pl.pallas_call(intra_attention, out_shape=jax.ShapeDtypeStruct((group * s...  10.8 us
    pallas_call x1, Pallas kernels, on_device(): pl.pallas_call(prepare, out_shape=(jax.ShapeDtypeStruct((count, 256, D),...  4.84 us
    pallas_call x1, Pallas kernels, on_device(): pl.pallas_call(intra_feed_forward, out_shape=jax.ShapeDtypeStruct((seq_co...  3.87 us
    ppermute x7, waiting for transfers between devices, by(): return lax.ppermute(shard, 'mp', [(i, i ^ k) for i in range(MP)])  2.91 us
  transfers between devices with their start and end apart: 7, of which 3 were waited for; matrix products, arithmetic and copies ran while one was open for 0% of the time, Pallas kernels for 16%

profile of v4, /device:TPU:1, one launch (start us, length us, event | category | flops | bytes accessed | tf_op | source)
XLA Modules:
  0.0 102.6 jit_solution(9265249268118993899)
XLA Ops:
  0.0 4.4 %collective-permute-start = (bf16[192,256]{1,0:T(8,128)(2,1)}, bf16[192,256]{1,0:T(8,128)(2,1)S(1)}, u32[]{:S(2)}, u32[]{:S(2)}) collective-permute-start(bf16[192,256]{1,0:T(8,128)(2,1)} %bitcast.14), channel_id=1, source_target_pairs={{0,2},{1,3},{2,0},{3,1},{4,6},{5,7},{6,4},{7,5},{8,10},{9,11},{10,... | collective-permute-start | bytes 294920 | tf_op jit(solution)/shard_map/ppermute | solution.py:280
  4.4 1.0 collective-permute-start.2
  5.4 1.2 %pack.1.w0 = bf16[1344,256]{1,0:T(8,128)(2,1)S(1)} custom-call(bf16[192,256]{1,0:T(8,128)(2,1)} %bitcast.18, bf16[64,256]{1,0:T(8,128)(2,1)} %refs_1_.1, bf16[256,256]{1,0:T(8,128)(2,1)} %refs_2_.1, bf16[256,256]{1,0:T(8,128)(2,1)} %refs_3_.1, bf16[64,256]{1,0:T(8,128)(2,1)} %refs_4_.1, bf16[256,256]{1,0:T(8,128)(2,1)} %refs_5_.1, bf16[256,256]{1,0:T(8,128)(2,1)} %refs_6_.1), custom_call_target="tpu_custom_call" | custom-call | tf_op jit(solution)/shard_map/pack/pallas_call | solution.py:303
  6.6 0.5 collective-permute-done.w2
  7.2 2.5 %collective-permute-start.1 = (bf16[1344,256]{1,0:T(8,128)(2,1)S(1)}, bf16[1344,256]{1,0:T(8,128)(2,1)S(1)}, u32[]{:S(2)}, u32[]{:S(2)}) collective-permute-start(bf16[1344,256]{1,0:T(8,128)(2,1)S(1)} %pack.1.w0), channel_id=1, source_target_pairs={{0,2},{1,3},{2,0},{3,1},{4,6},{5,7},{6,4},{7,5},{8,10},{9,11},{10,... | collective-permute-start | bytes 2064392 | tf_op jit(solution)/shard_map/ppermute | solution.py:280
  9.6 2.1 %collective-permute-start.3 = (bf16[192,256]{1,0:T(8,128)(2,1)S(1)}, bf16[192,256]{1,0:T(8,128)(2,1)S(1)}, u32[]{:S(2)}, u32[]{:S(2)}) collective-permute-start(bf16[192,256]{1,0:T(8,128)(2,1)S(1)} %collective-permute-done.w2), channel_id=1, source_target_pairs={{0,1},{1,0},{2,3},{3,2},{4,5},{5,4},{6,7},{7,6},{8,9},{9,8},{10,11... | collective-permute-start | bytes 294920 | tf_op jit(solution)/shard_map/ppermute | solution.py:280
  11.7 0.0 copy-start
  11.7 4.8 %prepare.1 = (bf16[24,256,256]{2,1,0:T(8,128)(2,1)S(1)}, bf16[2,32,24,256]{3,2,1,0:T(8,128)(2,1)S(1)}) custom-call(s32[1]{0:T(128)} %bitcast.mine_ref, bf16[250,24,256]{2,1,0:T(8,128)(2,1)} %bitcast.19), custom_call_target="tpu_custom_call" | custom-call | flops 4000000000 | bytes 8000000 | tf_op jit(solution)/shard_map/prepare/pallas_call | solution.py:315
  16.6 0.1 collective-permute-start.4
  16.7 0.0 collective-permute-done.2.w1
  16.7 0.0 collective-permute-done.3.w3
  16.7 0.0 copy-done
  16.7 7.2 %intra_attention.2.a0_ref = bf16[16,64,256]{2,1,0:T(8,128)(2,1)S(1)} custom-call(s32[1]{0:T(128)} %bitcast.mine_ref, bf16[24,256,256]{2,1,0:T(8,128)(2,1)S(1)} %get-tuple-element.12.n_ref, bf16[192,256]{1,0:T(8,128)(2,1)S(1)} %bitcast.16, bf16[192,256]{1,0:T(8,128)(2,1)S(1)} %collective-permute-done.2.w1, bf16[192,256]{1,0:T(8,128)(2,1)S(1)} %collective-permute-done.w2, ...), custom_call_target="tpu_custom_call" | custom-call | flops 5000000000 | bytes 2000000 | tf_op jit(solution)/shard_map/intra_attention/pallas_call | solution.py:339
  23.9 0.5 collective-permute-done.1.w2
  24.4 2.2 %collective-permute-start.5 = (bf16[1344,256]{1,0:T(8,128)(2,1)S(1)}, bf16[1344,256]{1,0:T(8,128)(2,1)S(1)}, u32[]{:S(2)}, u32[]{:S(2)}) collective-permute-start(bf16[1344,256]{1,0:T(8,128)(2,1)S(1)} %collective-permute-done.1.w2), channel_id=1, source_target_pairs={{0,1},{1,0},{2,3},{3,2},{4,5},{5,4},{6,7},{7,6},{8,9},{9,8},{10,11... | collective-permute-start | bytes 2064392 | tf_op jit(solution)/shard_map/ppermute | solution.py:280
  26.5 3.6 %intra_attention.3.a1_ref = bf16[8,64,256]{2,1,0:T(8,128)(2,1)S(1)} custom-call(s32[1]{0:T(128)} %bitcast.mine_ref, bf16[24,256,256]{2,1,0:T(8,128)(2,1)S(1)} %get-tuple-element.12.n_ref, bf16[192,256]{1,0:T(8,128)(2,1)S(1)} %bitcast.17, bf16[192,256]{1,0:T(8,128)(2,1)S(1)} %collective-permute-done.2.w1, bf16[192,256]{1,0:T(8,128)(2,1)S(1)} %collective-permute-done.w2, ...), custom_call_target="tpu_custom_call" | custom-call | flops 5000000000 | bytes 2000000 | tf_op jit(solution)/shard_map/intra_attention/pallas_call | solution.py:339
  30.1 0.0 collective-permute-done.4.w1
  30.1 0.0 collective-permute-done.5.w3
  30.1 3.9 %intra_feed_forward.1 = bf16[32,2,24,256]{3,2,1,0:T(8,128)(2,1)S(1)} custom-call(bf16[16,64,256]{2,1,0:T(8,128)(2,1)S(1)} %intra_attention.2.a0_ref, bf16[8,64,256]{2,1,0:T(8,128)(2,1)S(1)} %intra_attention.3.a1_ref, bf16[2,32,24,256]{3,2,1,0:T(8,128)(2,1)S(1)} %get-tuple-element.15.xq_ref, bf16[1344,256]{1,0:T(8,128)(2,1)S(1)} %pack.1.w0, ...), custom_call_target="tpu_custom_call" | custom-call | flops 3000000000 | bytes 3000000 | tf_op jit(solution)/shard_map/intra_feed_forward/pallas_call | solution.py:363
  34.0 21.6 %all_to_all.10 = bf16[32,48,256]{2,1,0:T(8,128)(2,1)S(1)} all-to-all(bf16[32,48,256]{2,1,0:T(8,128)(2,1)S(1)} %bitcast.13), channel_id=1, replica_groups=mesh['seq'=32,'mp'=4] {'seq'}, dimensions={0} | all-to-all | bytes 1572864 | tf_op jit(solution)/shard_map/all_to_all | solution.py:373
  55.7 19.1 %inter_layer.1 = bf16[32,2,24,256]{3,2,1,0:T(8,128)(2,1)S(1)} custom-call(bf16[32,2,24,256]{3,2,1,0:T(8,128)(2,1)S(1)} %bitcast.11, bf16[1344,256]{1,0:T(8,128)(2,1)S(1)} %pack.1.w0, bf16[1344,256]{1,0:T(8,128)(2,1)S(1)} %collective-permute-done.4.w1, bf16[1344,256]{1,0:T(8,128)(2,1)S(1)} %collective-permute-done.1.w2, ...), custom_call_target="tpu_custom_call" | custom-call | flops 30000001024 | bytes 4000000 | tf_op jit(solution)/shard_map/inter_layer/pallas_call | solution.py:374
  74.8 21.0 %all_to_all.11.p0 = bf16[64,24,256]{2,1,0:T(8,128)(2,1)S(1)} all-to-all(bf16[64,24,256]{2,1,0:T(8,128)(2,1)S(1)} %bitcast.12), channel_id=1, replica_groups={{0,2,4,6,8,10,12,14,16,18,20,22,24,26,28,30,32,34,36,38,40,42,44,46,48,..., dimensions={0} | all-to-all | bytes 1572864 | tf_op jit(solution)/shard_map/all_to_all | solution.py:388
  95.8 2.6 %collective-permute-start.6 = (bf16[64,24,256]{2,1,0:T(8,128)(2,1)S(1)}, bf16[64,24,256]{2,1,0:T(8,128)(2,1)S(1)}, u32[]{:S(2)}, u32[]{:S(2)}) collective-permute-start(bf16[64,24,256]{2,1,0:T(8,128)(2,1)S(1)} %all_to_all.11.p0), channel_id=1, source_target_pairs={{0,1},{1,0},{2,3},{3,2},{4,5},{5,4},{6,7},{7,6},{8,9},{9,8},{10,11... | collective-permute-start | bytes 2359304 | tf_op jit(solution)/shard_map/ppermute | solution.py:280
  98.4 1.9 %collective-permute-done.6.p1 = bf16[64,24,256]{2,1,0:T(8,128)(2,1)S(1)} collective-permute-done((bf16[64,24,256]{2,1,0:T(8,128)(2,1)S(1)}, bf16[64,24,256]{2,1,0:T(8,128)(2,1)S(1)}, u32[]{:S(2)}, u32[]{:S(2)}) %collective-permute-start.6) | collective-permute-done | bytes 786464 | tf_op jit(solution)/shard_map/ppermute | solution.py:280
  100.3 2.3 %assemble.1 = bf16[3000,256]{1,0:T(8,128)(2,1)} custom-call(s32[1]{0:T(128)} %bitcast.mine_ref, bf16[64,24,256]{2,1,0:T(8,128)(2,1)S(1)} %all_to_all.11.p0, bf16[64,24,256]{2,1,0:T(8,128)(2,1)S(1)} %collective-permute-done.6.p1), custom_call_target="tpu_custom_call" | custom-call | flops 1000000000 | bytes 4000000 | tf_op jit(solution)/shard_map/assemble/pallas_call | solution.py:392
Async XLA Ops:
  0.0 7.2 %collective-permute-start = (bf16[192,256]{1,0:T(8,128)(2,1)}, bf16[192,256]{1,0:T(8,128)(2,1)S(1)}, u32[]{:S(2)}, u32[]{:S(2)}) collective-permute-start(bf16[192,256]{1,0:T(8,128)(2,1)} %bitcast.14), channel_id=1, source_target_pairs={{0,2},{1,3},{2,0},{3,1},{4,6},{5,7},{6,4},{7,5},{8,10},{9,11},{10,... | collective-permute-start | bytes 294920 | tf_op jit(solution)/shard_map/ppermute | solution.py:280
  4.4 12.2 %collective-permute-start.2 = (bf16[192,256]{1,0:T(8,128)(2,1)}, bf16[192,256]{1,0:T(8,128)(2,1)S(1)}, u32[]{:S(2)}, u32[]{:S(2)}) collective-permute-start(bf16[192,256]{1,0:T(8,128)(2,1)} %bitcast.15), channel_id=1, source_target_pairs={{0,1},{1,0},{2,3},{3,2},{4,5},{5,4},{6,7},{7,6},{8,9},{9,8},{10,11... | collective-permute-start | bytes 294920 | tf_op jit(solution)/shard_map/ppermute | solution.py:280
  7.2 17.2 %collective-permute-start.1 = (bf16[1344,256]{1,0:T(8,128)(2,1)S(1)}, bf16[1344,256]{1,0:T(8,128)(2,1)S(1)}, u32[]{:S(2)}, u32[]{:S(2)}) collective-permute-start(bf16[1344,256]{1,0:T(8,128)(2,1)S(1)} %pack.1.w0), channel_id=1, source_target_pairs={{0,2},{1,3},{2,0},{3,1},{4,6},{5,7},{6,4},{7,5},{8,10},{9,11},{10,... | collective-permute-start | bytes 2064392 | tf_op jit(solution)/shard_map/ppermute | solution.py:280
  9.6 7.1 %collective-permute-start.3 = (bf16[192,256]{1,0:T(8,128)(2,1)S(1)}, bf16[192,256]{1,0:T(8,128)(2,1)S(1)}, u32[]{:S(2)}, u32[]{:S(2)}) collective-permute-start(bf16[192,256]{1,0:T(8,128)(2,1)S(1)} %collective-permute-done.w2), channel_id=1, source_target_pairs={{0,1},{1,0},{2,3},{3,2},{4,5},{5,4},{6,7},{7,6},{8,9},{9,8},{10,11... | collective-permute-start | bytes 294920 | tf_op jit(solution)/shard_map/ppermute | solution.py:280
  11.7 5.0 %copy-start = (bf16[256,3,64]{0,2,1:T(8,128)(2,1)S(1)}, bf16[256,3,64]{0,2,1:T(8,128)(2,1)}, u32[]{:S(2)}) copy-start(bf16[256,3,64]{0,2,1:T(8,128)(2,1)} %param.10) | copy-start | bytes 294916
  16.6 13.6 %collective-permute-start.4 = (bf16[1344,256]{1,0:T(8,128)(2,1)S(1)}, bf16[1344,256]{1,0:T(8,128)(2,1)S(1)}, u32[]{:S(2)}, u32[]{:S(2)}) collective-permute-start(bf16[1344,256]{1,0:T(8,128)(2,1)S(1)} %pack.1.w0), channel_id=1, source_target_pairs={{0,1},{1,0},{2,3},{3,2},{4,5},{5,4},{6,7},{7,6},{8,9},{9,8},{10,11... | collective-permute-start | bytes 2064392 | tf_op jit(solution)/shard_map/ppermute | solution.py:280
  24.4 5.8 %collective-permute-start.5 = (bf16[1344,256]{1,0:T(8,128)(2,1)S(1)}, bf16[1344,256]{1,0:T(8,128)(2,1)S(1)}, u32[]{:S(2)}, u32[]{:S(2)}) collective-permute-start(bf16[1344,256]{1,0:T(8,128)(2,1)S(1)} %collective-permute-done.1.w2), channel_id=1, source_target_pairs={{0,1},{1,0},{2,3},{3,2},{4,5},{5,4},{6,7},{7,6},{8,9},{9,8},{10,11... | collective-permute-start | bytes 2064392 | tf_op jit(solution)/shard_map/ppermute | solution.py:280
  95.8 4.6 %collective-permute-start.6 = (bf16[64,24,256]{2,1,0:T(8,128)(2,1)S(1)}, bf16[64,24,256]{2,1,0:T(8,128)(2,1)S(1)}, u32[]{:S(2)}, u32[]{:S(2)}) collective-permute-start(bf16[64,24,256]{2,1,0:T(8,128)(2,1)S(1)} %all_to_all.11.p0), channel_id=1, source_target_pairs={{0,1},{1,0},{2,3},{3,2},{4,5},{5,4},{6,7},{7,6},{8,9},{9,8},{10,11... | collective-permute-start | bytes 2359304 | tf_op jit(solution)/shard_map/ppermute | solution.py:280

commit v5 on v4

v5 whole, which is shorter than its diff:
```python
import functools

import jax
import jax.numpy as jnp
from jax import lax
from jax.experimental import pallas as pl
from jax.experimental.pallas import tpu as pltpu
from jax.sharding import PartitionSpec as P

HEADS = 8
HD = 32
K = 250
HALF = K // 2
D = 256
MP = 4
BF = jnp.bfloat16
F32 = jnp.float32
Q_SCALE = 1.4426950408889634 * HD ** (-0.5)
LOW = -1e30
IN_HBM = pl.BlockSpec(memory_space=pltpu.HBM)
IN_VMEM = pl.BlockSpec(memory_space=pltpu.VMEM)


def params(mebibytes):
    return pltpu.CompilerParams(vmem_limit_bytes=mebibytes * 1024 * 1024)


def dot(left, right, left_dim=1, right_dim=0):
    return lax.dot_general(
        left, right, (((left_dim,), (right_dim,)), ((), ())), preferred_element_type=F32
    )


def normed(values):
    centre = values - jnp.mean(values, axis=-1, keepdims=True)
    spread = jnp.mean(centre * centre, axis=-1, keepdims=True)
    return (centre * lax.rsqrt(spread + 1e-05)).astype(BF)


def put_attention_weights(shards, weights_ref):
    for k in range(MP):
        for t in range(weights_ref.shape[0]):
            weights_ref[t, 64 * k : 64 * k + 64, :] = shards[k][64 * t : 64 * t + 64, :]


def project(rows, weights_ref, query_ref, key_ref, value_ref):
    query_ref[...] = (dot(weights_ref[0], rows, 1, 1) * Q_SCALE).astype(BF)
    keys = dot(rows, weights_ref[1], 1, 1).astype(BF)
    lane = lax.broadcasted_iota(jnp.int32, (rows.shape[0], 128), 1) // HD
    for h in range(HEADS):
        part = keys[:, 128 * (h // 4) : 128 * (h // 4) + 128]
        key_ref[h] = jnp.where(lane == h % 4, part, jnp.zeros_like(part))
    values = dot(weights_ref[2], rows, 1, 1).astype(BF)
    for h in range(HEADS):
        value_ref[h, 0:HD, :] = values[HD * h : HD * h + HD, :]
        value_ref[h, HD:48, :] = jnp.ones((48 - HD, rows.shape[0]), BF)


def attend(query_ref, key_ref, value_ref, attended_ref):
    def scores(h):
        half = 128 * (h // 4)
        return dot(key_ref[h], query_ref[half : half + 128, :])

    following = scores(0)
    for h in range(HEADS):
        current = following
        if h + 1 < HEADS:
            following = scores(h + 1)
        top = jnp.max(current, axis=0, keepdims=True)
        weights = jnp.exp2(current - top).astype(BF)
        mixed = dot(value_ref[h], weights)
        attended_ref[HD * h : HD * h + HD, :] = mixed[0:HD] * (1.0 / mixed[HD : HD + 1])


def swapped(outer, bits):
    inner = 1 << bits
    size = outer * inner
    to = lax.broadcasted_iota(jnp.int32, (size, size), 0)
    source = lax.broadcasted_iota(jnp.int32, (size, size), 1)
    return jnp.where((source & (inner - 1)) * outer + (source >> bits) == to, 1.0, 0.0).astype(BF)


def pack(early, *refs):
    sources, (first_ref, rest_ref, sems) = refs[:-3], refs[-3:]
    copies = []
    for some, into in ((range(early), first_ref), (range(early, len(sources)), rest_ref)):
        at = 0
        for k in some:
            size = sources[k].shape[0]
            copies.append(pltpu.make_async_copy(sources[k], into.at[pl.ds(at, size)], sems.at[k]))
            copies[-1].start()
            at += size
    for copy in copies:
        copy.wait()


def prepare(half, mine_ref, frames_ref, n_ref, xq_ref, x_ref, turn_ref, sems):
    count = x_ref.shape[1]
    length = 128 if half == 0 else K - HALF
    copies = []
    for k, (at, to) in enumerate(((0, 64), (64, length))):
        copies.append(
            pltpu.make_async_copy(
                frames_ref.at[pl.ds(half * HALF + at, to - at)],
                x_ref.at[pl.ds(at, to - at)],
                sems.at[k],
            )
        )
        copies[-1].start()
    to = lax.broadcasted_iota(jnp.int32, turn_ref.shape, 0)
    source = lax.broadcasted_iota(jnp.int32, turn_ref.shape, 1)
    turn_ref[...] = jnp.where((to & 15) * count + (to >> 4) == source, 1.0, 0.0).astype(BF)
    for b in range(8):
        if b == 0:
            copies[0].wait()
        if b == 4:
            copies[1].wait()
            if length < 128:
                x_ref[length:128] = x_ref[length - (128 - length) : length]
        rows = normed(x_ref[16 * b : 16 * b + 16].astype(F32).reshape(16 * count, D))
        rows = dot(turn_ref[...], rows).astype(BF)
        for u in range(count):
            n_ref[u, 16 * b : 16 * b + 16, :] = rows[16 * u : 16 * u + 16]
    xq_ref[...] = x_ref[pl.ds(mine_ref[0] * 32, 32)]


def intra_attention(mine_ref, early_ref, late_ref, w0, w1, w2, w3, o_ref, weights_ref):
    @pl.when(pl.program_id(0) == 0)
    def _():
        put_attention_weights((w0, w1, w2, w3), weights_ref)

    own = pl.multiple_of(mine_ref[0] * 32, 32)
    count = early_ref.shape[0]
    row = lax.broadcasted_iota(jnp.int32, (256, 256), 0)
    lane = lax.broadcasted_iota(jnp.int32, (256, 256), 1)
    same = (row & 127) >> 5 == lane >> 6
    valid = jnp.concatenate([row[0:8] < 5] * 2, axis=1)
    rows, few = [], []
    for u in range(count):
        rows += [early_ref[u], late_ref[u]]
        few += [early_ref[u, pl.ds(own, 32), :], late_ref[u, pl.ds(own, 32), :]] * 4
    rows = jnp.concatenate(rows, axis=0)
    keys = dot(rows, weights_ref[1], 1, 1).astype(BF)
    query = dot(weights_ref[0], jnp.concatenate(few, axis=0), 1, 1) * Q_SCALE
    values = dot(weights_ref[2], rows, 1, 1).astype(BF)
    ones = jnp.ones((16, 256), BF)

    def scores(u):
        at = slice(256 * u, 256 * u + 256)
        own_query = query[:, at]
        low = jnp.where(same & (row < 128), own_query, 0.0)
        high = jnp.where(same & (row >= 128), own_query, 0.0)
        score = dot(keys[at], jnp.concatenate([low, high], axis=1).astype(BF))
        pieces = []
        for at in (0, 128):
            pieces += [score[at : at + 120], jnp.where(valid, score[at + 120 : at + 128], LOW)]
        return jnp.concatenate(pieces, axis=0)

    following = scores(0)
    found = []
    for u in range(count):
        current = following
        if u + 1 < count:
            following = scores(u + 1)
        top = jnp.max(current, axis=0, keepdims=True)
        weights = jnp.exp2(current - top).astype(BF)
        for g in range(2):
            value = values[128 * g : 128 * g + 128, 256 * u : 256 * u + 256]
            mixed = dot(
                jnp.concatenate([value, ones], axis=0), weights[:, 256 * g : 256 * g + 256]
            )
            mixed = jnp.where(same[0:128], mixed[0:128] * (1.0 / mixed[128:129]), 0.0)
            mixed = (mixed[:, 0:128] + mixed[:, 128:256]).T
            found.append((mixed[0:64] + mixed[64:128]).astype(BF))
    for u in range(count):
        o_ref[u] = jnp.concatenate(found[2 * u : 2 * u + 2], axis=1)


def add_hidden(rows, total, up, down):
    hidden = jnp.maximum(dot(rows, up[0]), 0.0).astype(BF)
    for k in range(len(up)):
        ready = hidden
        if k + 1 < len(up):
            hidden = jnp.maximum(dot(rows, up[k + 1]), 0.0).astype(BF)
        total = total + dot(ready, down[k])
    return total


def feed_forward(middles, up, down):
    done = []
    following = normed(middles[0].astype(F32))
    for at, middle in enumerate(middles):
        rows = following
        if at + 1 < len(middles):
            following = normed(middles[at + 1].astype(F32))
        done.append((rows, add_hidden(rows, middle.astype(F32), up, down)))
    return done


def intra_feed_forward(a_ref, xq0_ref, xq1_ref, f0, f1, f2, f3, w0, w1, w2, rows_ref, total_ref):
    shards = (w0, w1, w2)
    count = xq0_ref.shape[1]
    out = jnp.concatenate([w[192:256, :] for w in (f0, f1, f2, f3)], axis=0)
    up = [w[768:1024, :] for w in shards]
    down = [w[1024:1280, :] for w in shards]
    turn = swapped(count, 3)
    middles = []
    for half in range(2):
        for pair in range(2):
            rows = []
            for at in (32 * half + 16 * pair, 32 * half + 16 * pair + 8):
                taken = [a_ref[u, at : at + 8, :].astype(F32) for u in range(count)]
                rows.append(dot(turn, jnp.concatenate(taken, axis=0).astype(BF)).astype(BF))
            x = (xq0_ref, xq1_ref)[half][16 * pair : 16 * pair + 16].astype(F32).reshape(16 * count, D)
            middles.append((x + dot(jnp.concatenate(rows, axis=0), out)).astype(BF))
    size = 16 * count
    for at, (rows, total) in enumerate(feed_forward(middles, up, down)):
        rows_ref[size * at : size * at + size, :] = rows
        total_ref[size * at : size * at + size, :] = total


def intra_last_hidden(rows_ref, total_ref, w3, o_ref):
    count = o_ref.shape[2]
    size = 16 * count
    for half in range(2):
        for pair in range(2):
            at = slice(size * (2 * half + pair), size * (2 * half + pair + 1))
            total = add_hidden(rows_ref[at], total_ref[at], [w3[768:1024, :]], [w3[1024:1280, :]])
            total = total.astype(BF).astype(F32).reshape(16, count, D)
            o_ref[16 * pair : 16 * pair + 16, half] = total.astype(BF)


def inter_layer(x_ref, w0, w1, w2, w3, o_ref, weights_ref, query_ref, key_ref, value_ref, attended_ref, later_ref):
    shards = (w0, w1, w2, w3)
    put_attention_weights(shards, weights_ref)
    for half in (1, 0):
        x = x_ref[:, half].astype(F32).reshape(later_ref.shape)
        project(normed(x), weights_ref, query_ref, key_ref, value_ref)
        attend(query_ref, key_ref, value_ref, attended_ref)
        attended = attended_ref[...].T.astype(BF)
        middle = (x + dot(attended, weights_ref[3])).astype(BF)
        done = feed_forward(
            [middle[at : at + 256] for at in range(0, x.shape[0], 256)],
            [w[256:512, :] for w in shards],
            [w[512:768, :] for w in shards],
        )
        done = jnp.concatenate([total.astype(BF) for _, total in done], axis=0)
        if half == 1:
            first = lax.broadcasted_iota(jnp.int32, done.shape, 0) == 0
            later_ref[...] = jnp.where(first, 0.0, pltpu.roll(done.astype(F32), 1, 0))
        else:
            summed = (done.astype(F32) + later_ref[...]).reshape(x_ref.shape[0], *x_ref.shape[2:])
            for copy in range(2):
                o_ref[:, copy] = summed.astype(BF)


def assemble(mine_ref, p0, p1, o_ref, rows_ref):
    turn = swapped(32, 3)
    for piece, core, z in ((p, core, z) for core, p in enumerate((p0, p1)) for z in range(2)):
        at = pl.multiple_of((2 * z + ((mine_ref[0] & 1) ^ core)) * 32, 32)
        for part in range(3):
            taken = [piece[2 * s + z, 8 * part : 8 * part + 8, :].astype(F32) for s in range(32)]
            rows = dot(turn, jnp.concatenate(taken, axis=0).astype(BF)).astype(BF)
            for u in range(8):
                rows_ref[8 * part + u, pl.ds(at, 32), :] = rows[32 * u : 32 * u + 32]
    to = lax.broadcasted_iota(jnp.int32, (128, 256), 0)
    source = lax.broadcasted_iota(jnp.int32, (128, 256), 1)
    for b in range(24):
        place = to + 3 * b
        place = jnp.where(place < HALF, place, place + 3)
        pick = jnp.where(place == source, 1.0, 0.0).astype(BF)
        rows = jnp.concatenate([rows_ref[b], rows_ref[min(b + 1, 23)]], axis=0)
        size = min(128, 3000 - 128 * b)
        o_ref[128 * b : 128 * b + size, :] = dot(pick, rows)[0:size].astype(BF)


def whole(shape):
    return pl.BlockSpec(shape, lambda i, *_: (0,) * len(shape))


def attention_scratch(length):
    return [
        pltpu.VMEM((4, D, D), BF),
        pltpu.VMEM((D, length), BF),
        pltpu.VMEM((HEADS, length, 128), BF),
        pltpu.VMEM((HEADS, 48, length), BF),
        pltpu.VMEM((D, length), F32),
    ]


def by(shard, k):
    return lax.ppermute(shard, "mp", [(i, i ^ k) for i in range(MP)])


def on_device(
    frames, intra_qkv, intra_out, intra_up, intra_down, inter_qkv, inter_out, inter_up, inter_down
):
    seq_count = lax.axis_size("seq")
    mine = lax.axis_index("mp").reshape(1)
    count = frames.shape[0]
    total = count * seq_count

    weights = (
        jnp.transpose(intra_qkv, (1, 2, 0)).reshape(-1, D),
        intra_out,
        jnp.transpose(inter_qkv, (1, 2, 0)).reshape(-1, D),
        inter_out,
        inter_up,
        inter_down,
        intra_up,
        intra_down,
    )
    first, rest = pl.pallas_call(
        functools.partial(pack, 2),
        out_shape=(jax.ShapeDtypeStruct((256, D), BF), jax.ShapeDtypeStruct((1280, D), BF)),
        in_specs=[IN_HBM] * len(weights),
        out_specs=[IN_VMEM] * 2,
        scratch_shapes=[pltpu.SemaphoreType.DMA((len(weights),))],
        compiler_params=params(4),
        name="pack",
    )(*[pltpu.with_memory_space_constraint(a, pltpu.HBM) for a in weights])
    across = by(first, 2)
    first = [first, by(first, 1), across, by(across, 1)]

    rows, own_frames = [], []
    stored = pltpu.with_memory_space_constraint(jnp.transpose(frames, (1, 0, 2)), pltpu.HBM)
    for half in range(2):
        found = pl.pallas_call(
            functools.partial(prepare, half),
            out_shape=(
                jax.ShapeDtypeStruct((count, 128, D), BF),
                jax.ShapeDtypeStruct((32, count, D), BF),
            ),
            grid_spec=pltpu.PrefetchScalarGridSpec(
                num_scalar_prefetch=1,
                in_specs=[IN_HBM],
                out_specs=[IN_VMEM] * 2,
                scratch_shapes=[
                    pltpu.VMEM((128, count, D), BF),
                    pltpu.VMEM((16 * count, 16 * count), BF),
                    pltpu.SemaphoreType.DMA((2,)),
                ],
            ),
            compiler_params=params(16),
            cost_estimate=pl.CostEstimate(flops=10**9, bytes_accessed=4 * 10**6, transcendentals=10**4),
            name="prepare",
        )(mine, stored)
        rows.append(found[0])
        own_frames.append(found[1])
        if half == 0:
            rest, first[2], rows[0] = lax.optimization_barrier((rest, across, rows[0]))
            rest = [rest, by(rest, 1), by(rest, 2)]

    group = 8
    attended = pl.pallas_call(
        intra_attention,
        out_shape=jax.ShapeDtypeStruct((count, 64, D), BF),
        grid_spec=pltpu.PrefetchScalarGridSpec(
            num_scalar_prefetch=1,
            grid=(count // group,),
            in_specs=[pl.BlockSpec((group, 128, D), lambda i, *_: (i, 0, 0))] * 2
            + [whole((192, D))] * 4,
            out_specs=pl.BlockSpec((group, 64, D), lambda i, *_: (i, 0, 0)),
            scratch_shapes=[pltpu.VMEM((3, D, D), BF)],
        ),
        compiler_params=params(20),
        cost_estimate=pl.CostEstimate(flops=2 * 10**9, bytes_accessed=4 * 10**6, transcendentals=3 * 10**6),
        name="intra_attention",
    )(mine, *rows, *first)
    rest[2], attended = lax.optimization_barrier((rest[2], attended))
    rest.append(by(rest[2], 1))

    normed_rows, partial_sums = pl.pallas_call(
        intra_feed_forward,
        out_shape=(
            jax.ShapeDtypeStruct((64 * count, D), BF),
            jax.ShapeDtypeStruct((64 * count, D), F32),
        ),
        in_specs=[IN_VMEM] * 10,
        out_specs=[IN_VMEM] * 2,
        compiler_params=params(24),
        cost_estimate=pl.CostEstimate(flops=3 * 10**9, bytes_accessed=3 * 10**6, transcendentals=0),
        name="intra_feed_forward",
    )(attended, *own_frames, *first, *rest[:3])
    sent = pl.pallas_call(
        intra_last_hidden,
        out_shape=jax.ShapeDtypeStruct((seq_count, 2, count, D), BF),
        in_specs=[IN_VMEM] * 3,
        out_specs=IN_VMEM,
        compiler_params=params(16),
        cost_estimate=pl.CostEstimate(flops=10**9, bytes_accessed=3 * 10**6, transcendentals=0),
        name="intra_last_hidden",
    )(normed_rows, partial_sums, rest[3])
    sent = sent.reshape(seq_count, 2 * count, D)
    got = lax.all_to_all(sent, "seq", split_axis=0, concat_axis=0, tiled=True)
    summed = pl.pallas_call(
        inter_layer,
        out_shape=jax.ShapeDtypeStruct((seq_count, 2, count, D), BF),
        in_specs=[IN_VMEM] * 5,
        out_specs=IN_VMEM,
        scratch_shapes=attention_scratch(total) + [pltpu.VMEM((total, D), F32)],
        compiler_params=params(32),
        cost_estimate=pl.CostEstimate(flops=3 * 10**10, bytes_accessed=4 * 10**6, transcendentals=10**7),
        name="inter_layer",
    )(got.reshape(seq_count, 2, count, D), *rest)

    back = summed.reshape(2 * seq_count, count, D)
    chips = [(s, z) for s in range(seq_count) for z in range(2)]
    groups = [[MP * s + 2 * z + core for s, z in chips] for core in range(2)]
    back = lax.all_to_all(
        back, ("seq", "mp"), split_axis=0, concat_axis=0, tiled=True, axis_index_groups=groups
    )
    pieces = [back, by(back, 1)]
    return pl.pallas_call(
        assemble,
        out_shape=jax.ShapeDtypeStruct((HALF * count, D), BF),
        grid_spec=pltpu.PrefetchScalarGridSpec(
            num_scalar_prefetch=1,
            in_specs=[IN_VMEM] * 2,
            out_specs=IN_VMEM,
            scratch_shapes=[pltpu.VMEM((count, 128, D), BF)],
        ),
        compiler_params=params(12),
        cost_estimate=pl.CostEstimate(flops=10**9, bytes_accessed=4 * 10**6, transcendentals=0),
        name="assemble",
    )(mine, *pieces)


def solution(mesh):
    return jax.shard_map(
        on_device,
        mesh=mesh,
        in_specs=(
            P("seq", None, None),
            P(None, None, "mp"),
            P("mp", None),
            P(None, "mp"),
            P("mp", None),
            P(None, None, "mp"),
            P("mp", None),
            P(None, "mp"),
            P("mp", None),
        ),
        out_specs=P("seq", None),
        check_vma=False,
    )
```

time: 103 us -> 93.4 us (0.907)
  Pallas kernels: 42.1 us -> 33.2 us
    pallas_call x1, Pallas kernels: 19.1 us -> 13.1 us  [on_device(): pl.pallas_call(inter_layer, out_shape=jax.ShapeDtypeStruct((seq_count, 2,...]
    pallas_call x5 -> x6, Pallas kernels: 20.7 us -> 17.8 us  [the longest x1 7.88 us: on_device(): pl.pallas_call(intra_attention, out_shape=jax.ShapeDtypeStruct((count, 64...]
  transfers between devices with their start and end apart: 7 -> 7, of which waited for: 3 -> 3; matrix products, arithmetic and copies ran while one was open for 0% -> 0% of each run, Pallas kernels for 16% -> 17%
where the time goes in v5:
time: 93.4 us; the launch traced here: 93.2 us
  blocking collectives  42.8 us (46%)
  Pallas kernels  33.2 us (36%)
  starting transfers between devices  14.3 us (15%)
  waiting for transfers between devices  2.76 us (3%)
    all_to_all x1, blocking collectives, on_device(): got = lax.all_to_all(sent, 'seq', split_axis=0, concat_axis=0, tiled=True)  21.8 us
    all_to_all x1, blocking collectives, on_device(): lax.all_to_all(back, ('seq', 'mp'), split_axis=0, concat_axis=0, tiled=Tr...  21.1 us
    ppermute x7, starting transfers between devices, by(): return lax.ppermute(shard, 'mp', [(i, i ^ k) for i in range(MP)])  14.3 us
    pallas_call x1, Pallas kernels, on_device(): pl.pallas_call(inter_layer, out_shape=jax.ShapeDtypeStruct((seq_count, 2,...  13.1 us
    pallas_call x1, Pallas kernels, on_device(): pl.pallas_call(intra_attention, out_shape=jax.ShapeDtypeStruct((count, 64...  7.88 us
    pallas_call x2, Pallas kernels, on_device(): pl.pallas_call(functools.partial(prepare, half), out_shape=(jax.ShapeDtyp...  5.97 us
    ppermute x7, waiting for transfers between devices, by(): return lax.ppermute(shard, 'mp', [(i, i ^ k) for i in range(MP)])  2.76 us
    pallas_call x1, Pallas kernels, on_device(): pl.pallas_call(assemble, out_shape=jax.ShapeDtypeStruct((HALF * count, D)...  2.29 us
  transfers between devices with their start and end apart: 7, of which 3 were waited for; matrix products, arithmetic and copies ran while one was open for 0% of the time, Pallas kernels for 17%

profile of v5, /device:TPU:1, one launch (start us, length us, event | category | flops | bytes accessed | tf_op | source)
XLA Modules:
  0.0 93.2 jit_solution(4309216045389411053)
XLA Ops:
  0.0 1.3 %pack.1 = (bf16[256,256]{1,0:T(8,128)(2,1)S(1)}, bf16[1280,256]{1,0:T(8,128)(2,1)S(1)}) custom-call(bf16[192,256]{1,0:T(8,128)(2,1)} %bitcast.14, bf16[64,256]{1,0:T(8,128)(2,1)} %refs_1_.1, bf16[192,256]{1,0:T(8,128)(2,1)} %bitcast.15, bf16[64,256]{1,0:T(8,128)(2,1)} %refs_3_.1, bf16[256,256]{1,0:T(8,128)(2,1)} %refs_4_.1, bf16[256,256]{1,0:T(8,128)(2,1)} %refs_5_.1, ...), custom_call_target="tpu_custom_call" | custom-call | tf_op jit(solution)/shard_map/pack/pallas_call | solution.py:313
  1.3 4.5 %collective-permute-start = (bf16[256,256]{1,0:T(8,128)(2,1)S(1)}, bf16[256,256]{1,0:T(8,128)(2,1)S(1)}, u32[]{:S(2)}, u32[]{:S(2)}) collective-permute-start(bf16[256,256]{1,0:T(8,128)(2,1)S(1)} %get-tuple-element.19.w0.f0), channel_id=1, source_target_pairs={{0,2},{1,3},{2,0},{3,1},{4,6},{5,7},{6,4},{7,5},{8,10},{9,11},{10,... | collective-permute-start | bytes 393224 | tf_op jit(solution)/shard_map/ppermute | solution.py:292
  5.8 3.0 %prepare.2 = (bf16[24,128,256]{2,1,0:T(8,128)(2,1)S(1)}, bf16[32,24,256]{2,1,0:T(8,128)(2,1)S(1)}) custom-call(s32[1]{0:T(128)} %bitcast.mine_ref, bf16[250,24,256]{2,1,0:T(8,128)(2,1)} %bitcast.16), custom_call_target="tpu_custom_call" | custom-call | flops 1000000000 | bytes 4000000 | tf_op jit(solution)/shard_map/prepare/pallas_call | solution.py:328
  8.8 0.2 collective-permute-done.w2.f2
  9.0 2.6 %collective-permute-start.1 = (bf16[1280,256]{1,0:T(8,128)(2,1)S(1)}, bf16[1280,256]{1,0:T(8,128)(2,1)S(1)}, u32[]{:S(2)}, u32[]{:S(2)}) collective-permute-start(bf16[1280,256]{1,0:T(8,128)(2,1)S(1)} %get-tuple-element.21.w0), channel_id=1, source_target_pairs={{0,2},{1,3},{2,0},{3,1},{4,6},{5,7},{6,4},{7,5},{8,10},{9,11},{10,... | collective-permute-start | bytes 1966088 | tf_op jit(solution)/shard_map/ppermute | solution.py:292
  11.7 1.8 %collective-permute-start.2 = (bf16[256,256]{1,0:T(8,128)(2,1)S(1)}, bf16[256,256]{1,0:T(8,128)(2,1)S(1)}, u32[]{:S(2)}, u32[]{:S(2)}) collective-permute-start(bf16[256,256]{1,0:T(8,128)(2,1)S(1)} %get-tuple-element.19.w0.f0), channel_id=1, source_target_pairs={{0,1},{1,0},{2,3},{3,2},{4,5},{5,4},{6,7},{7,6},{8,9},{9,8},{10,11... | collective-permute-start | bytes 393224 | tf_op jit(solution)/shard_map/ppermute | solution.py:292
  13.5 0.0 collective-permute-start.3
  13.5 0.5 collective-permute-start.4
  14.0 3.0 %prepare.3 = (bf16[24,128,256]{2,1,0:T(8,128)(2,1)S(1)}, bf16[32,24,256]{2,1,0:T(8,128)(2,1)S(1)}) custom-call(s32[1]{0:T(128)} %bitcast.mine_ref, bf16[250,24,256]{2,1,0:T(8,128)(2,1)} %bitcast.17), custom_call_target="tpu_custom_call" | custom-call | flops 1000000000 | bytes 4000000 | tf_op jit(solution)/shard_map/prepare/pallas_call | solution.py:328
  17.0 0.0 collective-permute-done.2.w1.f1
  17.0 0.0 collective-permute-done.3.w3.f3
  17.0 7.9 %intra_attention.1.a_ref = bf16[24,64,256]{2,1,0:T(8,128)(2,1)S(1)} custom-call(s32[1]{0:T(128)} %bitcast.mine_ref, bf16[24,128,256]{2,1,0:T(8,128)(2,1)S(1)} %get-tuple-element.22.early_ref, bf16[24,128,256]{2,1,0:T(8,128)(2,1)S(1)} %get-tuple-element.23.late_ref, bf16[256,256]{1,0:T(8,128)(2,1)S(1)} %get-tuple-element.19.w0.f0, ...), custom_call_target="tpu_custom_call" | custom-call | flops 2000000000 | bytes 4000000 | tf_op jit(solution)/shard_map/intra_attention/pallas_call | solution.py:355
  24.9 0.6 collective-permute-done.1.w2
  25.5 2.2 %collective-permute-start.5 = (bf16[1280,256]{1,0:T(8,128)(2,1)S(1)}, bf16[1280,256]{1,0:T(8,128)(2,1)S(1)}, u32[]{:S(2)}, u32[]{:S(2)}) collective-permute-start(bf16[1280,256]{1,0:T(8,128)(2,1)S(1)} %collective-permute-done.1.w2), channel_id=1, source_target_pairs={{0,1},{1,0},{2,3},{3,2},{4,5},{5,4},{6,7},{7,6},{8,9},{9,8},{10,11... | collective-permute-start | bytes 1966088 | tf_op jit(solution)/shard_map/ppermute | solution.py:292
  27.7 0.0 collective-permute-done.4.w1
  27.7 2.0 %intra_feed_forward.1 = (bf16[1536,256]{1,0:T(8,128)(2,1)S(1)}, f32[1536,256]{1,0:T(8,128)S(1)}) custom-call(bf16[24,64,256]{2,1,0:T(8,128)(2,1)S(1)} %intra_attention.1.a_ref, bf16[32,24,256]{2,1,0:T(8,128)(2,1)S(1)} %get-tuple-element.26.xq0_ref, bf16[32,24,256]{2,1,0:T(8,128)(2,1)S(1)} %get-tuple-element.27.xq1_ref, ...), custom_call_target="tpu_custom_call" | custom-call | flops 3000000000 | bytes 3000000 | tf_op jit(solution)/shard_map/intra_feed_forward/pallas_call | solution.py:373
  29.7 0.0 collective-permute-done.5.w3
  29.7 0.7 intra_last_hidden.1
  30.4 21.8 %all_to_all.10 = bf16[32,48,256]{2,1,0:T(8,128)(2,1)S(1)} all-to-all(bf16[32,48,256]{2,1,0:T(8,128)(2,1)S(1)} %bitcast.11), channel_id=1, replica_groups=mesh['seq'=32,'mp'=4] {'seq'}, dimensions={0} | all-to-all | bytes 1572864 | tf_op jit(solution)/shard_map/all_to_all | solution.py:395
  52.1 13.1 %inter_layer.1 = bf16[32,2,24,256]{3,2,1,0:T(8,128)(2,1)S(1)} custom-call(bf16[32,2,24,256]{3,2,1,0:T(8,128)(2,1)S(1)} %bitcast.12, bf16[1280,256]{1,0:T(8,128)(2,1)S(1)} %get-tuple-element.21.w0, bf16[1280,256]{1,0:T(8,128)(2,1)S(1)} %collective-permute-done.4.w1, bf16[1280,256]{1,0:T(8,128)(2,1)S(1)} %collective-permute-done.1.w2, ...), custom_call_target="tpu_custom_call" | custom-call | flops 30000001024 | bytes 4000000 | tf_op jit(solution)/shard_map/inter_layer/pallas_call | solution.py:396
  65.2 21.1 %all_to_all.11.p0 = bf16[64,24,256]{2,1,0:T(8,128)(2,1)S(1)} all-to-all(bf16[64,24,256]{2,1,0:T(8,128)(2,1)S(1)} %bitcast.13), channel_id=1, replica_groups={{0,2,4,6,8,10,12,14,16,18,20,22,24,26,28,30,32,34,36,38,40,42,44,46,48,..., dimensions={0} | all-to-all | bytes 1572864 | tf_op jit(solution)/shard_map/all_to_all | solution.py:410
  86.3 2.7 %collective-permute-start.6 = (bf16[64,24,256]{2,1,0:T(8,128)(2,1)S(1)}, bf16[64,24,256]{2,1,0:T(8,128)(2,1)S(1)}, u32[]{:S(2)}, u32[]{:S(2)}) collective-permute-start(bf16[64,24,256]{2,1,0:T(8,128)(2,1)S(1)} %all_to_all.11.p0), channel_id=1, source_target_pairs={{0,1},{1,0},{2,3},{3,2},{4,5},{5,4},{6,7},{7,6},{8,9},{9,8},{10,11... | collective-permute-start | bytes 2359304 | tf_op jit(solution)/shard_map/ppermute | solution.py:292
  89.0 1.9 %collective-permute-done.6.p1 = bf16[64,24,256]{2,1,0:T(8,128)(2,1)S(1)} collective-permute-done((bf16[64,24,256]{2,1,0:T(8,128)(2,1)S(1)}, bf16[64,24,256]{2,1,0:T(8,128)(2,1)S(1)}, u32[]{:S(2)}, u32[]{:S(2)}) %collective-permute-start.6) | collective-permute-done | bytes 786464 | tf_op jit(solution)/shard_map/ppermute | solution.py:292
  90.9 2.3 %assemble.1 = bf16[3000,256]{1,0:T(8,128)(2,1)} custom-call(s32[1]{0:T(128)} %bitcast.mine_ref, bf16[64,24,256]{2,1,0:T(8,128)(2,1)S(1)} %all_to_all.11.p0, bf16[64,24,256]{2,1,0:T(8,128)(2,1)S(1)} %collective-permute-done.6.p1), custom_call_target="tpu_custom_call" | custom-call | flops 1000000000 | bytes 4000000 | tf_op jit(solution)/shard_map/assemble/pallas_call | solution.py:414
Async XLA Ops:
  1.3 7.7 %collective-permute-start = (bf16[256,256]{1,0:T(8,128)(2,1)S(1)}, bf16[256,256]{1,0:T(8,128)(2,1)S(1)}, u32[]{:S(2)}, u32[]{:S(2)}) collective-permute-start(bf16[256,256]{1,0:T(8,128)(2,1)S(1)} %get-tuple-element.19.w0.f0), channel_id=1, source_target_pairs={{0,2},{1,3},{2,0},{3,1},{4,6},{5,7},{6,4},{7,5},{8,10},{9,11},{10,... | collective-permute-start | bytes 393224 | tf_op jit(solution)/shard_map/ppermute | solution.py:292
  9.0 16.5 %collective-permute-start.1 = (bf16[1280,256]{1,0:T(8,128)(2,1)S(1)}, bf16[1280,256]{1,0:T(8,128)(2,1)S(1)}, u32[]{:S(2)}, u32[]{:S(2)}) collective-permute-start(bf16[1280,256]{1,0:T(8,128)(2,1)S(1)} %get-tuple-element.21.w0), channel_id=1, source_target_pairs={{0,2},{1,3},{2,0},{3,1},{4,6},{5,7},{6,4},{7,5},{8,10},{9,11},{10,... | collective-permute-start | bytes 1966088 | tf_op jit(solution)/shard_map/ppermute | solution.py:292
  11.7 5.3 %collective-permute-start.2 = (bf16[256,256]{1,0:T(8,128)(2,1)S(1)}, bf16[256,256]{1,0:T(8,128)(2,1)S(1)}, u32[]{:S(2)}, u32[]{:S(2)}) collective-permute-start(bf16[256,256]{1,0:T(8,128)(2,1)S(1)} %get-tuple-element.19.w0.f0), channel_id=1, source_target_pairs={{0,1},{1,0},{2,3},{3,2},{4,5},{5,4},{6,7},{7,6},{8,9},{9,8},{10,11... | collective-permute-start | bytes 393224 | tf_op jit(solution)/shard_map/ppermute | solution.py:292
  13.5 3.5 %collective-permute-start.3 = (bf16[256,256]{1,0:T(8,128)(2,1)S(1)}, bf16[256,256]{1,0:T(8,128)(2,1)S(1)}, u32[]{:S(2)}, u32[]{:S(2)}) collective-permute-start(bf16[256,256]{1,0:T(8,128)(2,1)S(1)} %collective-permute-done.w2.f2), channel_id=1, source_target_pairs={{0,1},{1,0},{2,3},{3,2},{4,5},{5,4},{6,7},{7,6},{8,9},{9,8},{10,11... | collective-permute-start | bytes 393224 | tf_op jit(solution)/shard_map/ppermute | solution.py:292
  13.5 14.2 %collective-permute-start.4 = (bf16[1280,256]{1,0:T(8,128)(2,1)S(1)}, bf16[1280,256]{1,0:T(8,128)(2,1)S(1)}, u32[]{:S(2)}, u32[]{:S(2)}) collective-permute-start(bf16[1280,256]{1,0:T(8,128)(2,1)S(1)} %get-tuple-element.21.w0), channel_id=1, source_target_pairs={{0,1},{1,0},{2,3},{3,2},{4,5},{5,4},{6,7},{7,6},{8,9},{9,8},{10,11... | collective-permute-start | bytes 1966088 | tf_op jit(solution)/shard_map/ppermute | solution.py:292
  25.5 4.2 %collective-permute-start.5 = (bf16[1280,256]{1,0:T(8,128)(2,1)S(1)}, bf16[1280,256]{1,0:T(8,128)(2,1)S(1)}, u32[]{:S(2)}, u32[]{:S(2)}) collective-permute-start(bf16[1280,256]{1,0:T(8,128)(2,1)S(1)} %collective-permute-done.1.w2), channel_id=1, source_target_pairs={{0,1},{1,0},{2,3},{3,2},{4,5},{5,4},{6,7},{7,6},{8,9},{9,8},{10,11... | collective-permute-start | bytes 1966088 | tf_op jit(solution)/shard_map/ppermute | solution.py:292
  86.3 4.6 %collective-permute-start.6 = (bf16[64,24,256]{2,1,0:T(8,128)(2,1)S(1)}, bf16[64,24,256]{2,1,0:T(8,128)(2,1)S(1)}, u32[]{:S(2)}, u32[]{:S(2)}) collective-permute-start(bf16[64,24,256]{2,1,0:T(8,128)(2,1)S(1)} %all_to_all.11.p0), channel_id=1, source_target_pairs={{0,1},{1,0},{2,3},{3,2},{4,5},{5,4},{6,7},{7,6},{8,9},{9,8},{10,11... | collective-permute-start | bytes 2359304 | tf_op jit(solution)/shard_map/ppermute | solution.py:292

commit v6 on v5

--- a/solution.py
+++ b/solution.py
@@ -94,34 +94,39 @@
         copy.wait()
 
 
-def prepare(half, mine_ref, frames_ref, n_ref, xq_ref, x_ref, turn_ref, sems):
+def norm_rows(mine_ref, x_ref, n_ref, xq_ref, turn_ref, arrived):
     count = x_ref.shape[1]
-    length = 128 if half == 0 else K - HALF
-    copies = []
-    for k, (at, to) in enumerate(((0, 64), (64, length))):
-        copies.append(
-            pltpu.make_async_copy(
-                frames_ref.at[pl.ds(half * HALF + at, to - at)],
-                x_ref.at[pl.ds(at, to - at)],
-                sems.at[k],
-            )
-        )
-        copies[-1].start()
     to = lax.broadcasted_iota(jnp.int32, turn_ref.shape, 0)
     source = lax.broadcasted_iota(jnp.int32, turn_ref.shape, 1)
     turn_ref[...] = jnp.where((to & 15) * count + (to >> 4) == source, 1.0, 0.0).astype(BF)
     for b in range(8):
-        if b == 0:
-            copies[0].wait()
-        if b == 4:
-            copies[1].wait()
-            if length < 128:
-                x_ref[length:128] = x_ref[length - (128 - length) : length]
+        if 16 * b in arrived:
+            arrived[16 * b].wait()
         rows = normed(x_ref[16 * b : 16 * b + 16].astype(F32).reshape(16 * count, D))
         rows = dot(turn_ref[...], rows).astype(BF)
         for u in range(count):
             n_ref[u, 16 * b : 16 * b + 16, :] = rows[16 * u : 16 * u + 16]
     xq_ref[...] = x_ref[pl.ds(mine_ref[0] * 32, 32)]
+
+
+def prepare_early(mine_ref, frames_ref, n_ref, xq_ref, late_ref, x_ref, turn_ref, sems):
+    arrived = {}
+    for k, (at, to) in enumerate(((0, 16), (16, 48), (48, 128))):
+        part = pl.ds(at, to - at)
+        arrived[at] = pltpu.make_async_copy(frames_ref.at[part], x_ref.at[part], sems.at[k])
+        arrived[at].start()
+    length = K - HALF
+    late = pltpu.make_async_copy(
+        frames_ref.at[pl.ds(HALF, length)], late_ref.at[pl.ds(0, length)], sems.at[3]
+    )
+    late.start()
+    norm_rows(mine_ref, x_ref, n_ref, xq_ref, turn_ref, arrived)
+    late.wait()
+    late_ref[length:128] = late_ref[length - (128 - length) : length]
+
+
+def prepare_late(mine_ref, x_ref, n_ref, xq_ref, turn_ref):
+    norm_rows(mine_ref, x_ref, n_ref, xq_ref, turn_ref, {})
 
 
 def intra_attention(mine_ref, early_ref, late_ref, w0, w1, w2, w3, o_ref, weights_ref):
@@ -197,8 +202,8 @@
     return done
 
 
-def intra_feed_forward(a_ref, xq0_ref, xq1_ref, f0, f1, f2, f3, w0, w1, w2, rows_ref, total_ref):
-    shards = (w0, w1, w2)
+def intra_feed_forward(a_ref, xq0_ref, xq1_ref, f0, f1, f2, f3, w0, rows_ref, total_ref):
+    shards = (w0,)
     count = xq0_ref.shape[1]
     out = jnp.concatenate([w[192:256, :] for w in (f0, f1, f2, f3)], axis=0)
     up = [w[768:1024, :] for w in shards]
@@ -219,13 +224,23 @@
         total_ref[size * at : size * at + size, :] = total
 
 
-def intra_last_hidden(rows_ref, total_ref, w3, o_ref):
+def intra_more_hidden(rows_ref, total_ref, w1, w2, o_ref):
+    size = rows_ref.shape[0] // 4
+    up = [w[768:1024, :] for w in (w1, w2)]
+    down = [w[1024:1280, :] for w in (w1, w2)]
+    for at in (slice(size * k, size * k + size) for k in range(4)):
+        o_ref[at] = add_hidden(rows_ref[at], total_ref[at], up, down)
+
+
+def intra_last_hidden(rows_ref, total_ref, w_ref, o_ref):
     count = o_ref.shape[2]
     size = 16 * count
     for half in range(2):
         for pair in range(2):
             at = slice(size * (2 * half + pair), size * (2 * half + pair + 1))
-            total = add_hidden(rows_ref[at], total_ref[at], [w3[768:1024, :]], [w3[1024:1280, :]])
+            total = add_hidden(
+                rows_ref[at], total_ref[at], [w_ref[768:1024, :]], [w_ref[1024:1280, :]]
+            )
             total = total.astype(BF).astype(F32).reshape(16, count, D)
             o_ref[16 * pair : 16 * pair + 16, half] = total.astype(BF)
 
@@ -254,7 +269,7 @@
                 o_ref[:, copy] = summed.astype(BF)
 
 
-def assemble(mine_ref, p0, p1, o_ref, rows_ref):
+def assemble(mine_ref, p0, p1, o_ref, rows_ref, done_ref, sems):
     turn = swapped(32, 3)
     for piece, core, z in ((p, core, z) for core, p in enumerate((p0, p1)) for z in range(2)):
         at = pl.multiple_of((2 * z + ((mine_ref[0] & 1) ^ core)) * 32, 32)
@@ -265,13 +280,22 @@
                 rows_ref[8 * part + u, pl.ds(at, 32), :] = rows[32 * u : 32 * u + 32]
     to = lax.broadcasted_iota(jnp.int32, (128, 256), 0)
     source = lax.broadcasted_iota(jnp.int32, (128, 256), 1)
+    copies = []
     for b in range(24):
         place = to + 3 * b
         place = jnp.where(place < HALF, place, place + 3)
         pick = jnp.where(place == source, 1.0, 0.0).astype(BF)
         rows = jnp.concatenate([rows_ref[b], rows_ref[min(b + 1, 23)]], axis=0)
         size = min(128, 3000 - 128 * b)
-        o_ref[128 * b : 128 * b + size, :] = dot(pick, rows)[0:size].astype(BF)
+        done_ref[128 * b : 128 * b + size, :] = dot(pick, rows)[0:size].astype(BF)
+        if b % 4 == 3:
+            part = pl.ds(128 * (b - 3), 384 + size)
+            copies.append(
+                pltpu.make_async_copy(done_ref.at[part], o_ref.at[part], sems.at[b // 4])
+            )
+            copies[-1].start()
+    for copy in copies:
+        copy.wait()
 
 
 def whole(shape):
@@ -322,36 +346,47 @@
     across = by(first, 2)
     first = [first, by(first, 1), across, by(across, 1)]
 
-    rows, own_frames = [], []
-    stored = pltpu.with_memory_space_constraint(jnp.transpose(frames, (1, 0, 2)), pltpu.HBM)
-    for half in range(2):
-        found = pl.pallas_call(
-            functools.partial(prepare, half),
-            out_shape=(
-                jax.ShapeDtypeStruct((count, 128, D), BF),
-                jax.ShapeDtypeStruct((32, count, D), BF),
-            ),
-            grid_spec=pltpu.PrefetchScalarGridSpec(
-                num_scalar_prefetch=1,
-                in_specs=[IN_HBM],
-                out_specs=[IN_VMEM] * 2,
-                scratch_shapes=[
-                    pltpu.VMEM((128, count, D), BF),
-                    pltpu.VMEM((16 * count, 16 * count), BF),
-                    pltpu.SemaphoreType.DMA((2,)),
-                ],
-            ),
-            compiler_params=params(16),
-            cost_estimate=pl.CostEstimate(flops=10**9, bytes_accessed=4 * 10**6, transcendentals=10**4),
-            name="prepare",
-        )(mine, stored)
-        rows.append(found[0])
-        own_frames.append(found[1])
-        if half == 0:
-            rest, first[2], rows[0] = lax.optimization_barrier((rest, across, rows[0]))
-            rest = [rest, by(rest, 1), by(rest, 2)]
-
-    group = 8
+    halves = (
+        jax.ShapeDtypeStruct((count, 128, D), BF),
+        jax.ShapeDtypeStruct((32, count, D), BF),
+        jax.ShapeDtypeStruct((128, count, D), BF),
+    )
+    turn = pltpu.VMEM((16 * count, 16 * count), BF)
+    early, early_frames, late_stored = pl.pallas_call(
+        prepare_early,
+        out_shape=halves,
+        grid_spec=pltpu.PrefetchScalarGridSpec(
+            num_scalar_prefetch=1,
+            in_specs=[IN_HBM],
+            out_specs=[IN_VMEM] * 3,
+            scratch_shapes=[
+                pltpu.VMEM((128, count, D), BF),
+                turn,
+                pltpu.SemaphoreType.DMA((4,)),
+            ],
+        ),
+        compiler_params=params(16),
+        cost_estimate=pl.CostEstimate(flops=10**9, bytes_accessed=4 * 10**6, transcendentals=10**4),
+        name="prepare_early",
+    )(mine, pltpu.with_memory_space_constraint(jnp.transpose(frames, (1, 0, 2)), pltpu.HBM))
+    rest, first[2], early = lax.optimization_barrier((rest, across, early))
+    rest = [rest, None, by(rest, 2)]
+    late, late_frames = pl.pallas_call(
+        prepare_late,
+        out_shape=halves[:2],
+        grid_spec=pltpu.PrefetchScalarGridSpec(
+            num_scalar_prefetch=1,
+            in_specs=[IN_VMEM],
+            out_specs=[IN_VMEM] * 2,
+            scratch_shapes=[turn],
+        ),
+        compiler_params=params(16),
+        cost_estimate=pl.CostEstimate(flops=10**8, bytes_accessed=10**5, transcendentals=10**4),
+        name="prepare_late",
+    )(mine, late_stored)
+    rows, own_frames = (early, late), (early_frames, late_frames)
+
+    group = 12
     attended = pl.pallas_call(
         intra_attention,
         out_shape=jax.ShapeDtypeStruct((count, 64, D), BF),
@@ -364,11 +399,12 @@
             scratch_shapes=[pltpu.VMEM((3, D, D), BF)],
         ),
         compiler_params=params(20),
-        cost_estimate=pl.CostEstimate(flops=2 * 10**9, bytes_accessed=4 * 10**6, transcendentals=3 * 10**6),
+        cost_estimate=pl.CostEstimate(flops=10**9, bytes_accessed=10**6, transcendentals=10**6),
         name="intra_attention",
     )(mine, *rows, *first)
-    rest[2], attended = lax.optimization_barrier((rest[2], attended))
-    rest.append(by(rest[2], 1))
+
+    beside, attended = lax.optimization_barrier((rest[0], attended))
+    rest[1] = by(beside, 1)
 
     normed_rows, partial_sums = pl.pallas_call(
         intra_feed_forward,
@@ -376,12 +412,24 @@
             jax.ShapeDtypeStruct((64 * count, D), BF),
             jax.ShapeDtypeStruct((64 * count, D), F32),
         ),
-        in_specs=[IN_VMEM] * 10,
+        in_specs=[IN_VMEM] * 8,
         out_specs=[IN_VMEM] * 2,
         compiler_params=params(24),
-        cost_estimate=pl.CostEstimate(flops=3 * 10**9, bytes_accessed=3 * 10**6, transcendentals=0),
+        cost_estimate=pl.CostEstimate(flops=10**8, bytes_accessed=10**5, transcendentals=0),
         name="intra_feed_forward",
-    )(attended, *own_frames, *first, *rest[:3])
+    )(attended, *own_frames, *first, rest[0])
+    rest[2], partial_sums = lax.optimization_barrier((rest[2], partial_sums))
+    rest.append(by(rest[2], 1))
+    partial_sums = pl.pallas_call(
+        intra_more_hidden,
+        out_shape=jax.ShapeDtypeStruct((64 * count, D), F32),
+        in_specs=[IN_VMEM] * 4,
+        out_specs=IN_VMEM,
+        input_output_aliases={1: 0},
+        compiler_params=params(16),
+        cost_estimate=pl.CostEstimate(flops=10**9, bytes_accessed=3 * 10**6, transcendentals=0),
+        name="intra_more_hidden",
+    )(normed_rows, partial_sums, *rest[1:3])
     sent = pl.pallas_call(
         intra_last_hidden,
         out_shape=jax.ShapeDtypeStruct((seq_count, 2, count, D), BF),
@@ -417,8 +465,12 @@
         grid_spec=pltpu.PrefetchScalarGridSpec(
             num_scalar_prefetch=1,
             in_specs=[IN_VMEM] * 2,
-            out_specs=IN_VMEM,
-            scratch_shapes=[pltpu.VMEM((count, 128, D), BF)],
+            out_specs=IN_HBM,
+            scratch_shapes=[
+                pltpu.VMEM((count, 128, D), BF),
+                pltpu.VMEM((HALF * count, D), BF),
+                pltpu.SemaphoreType.DMA((6,)),
+            ],
         ),
         compiler_params=params(12),
         cost_estimate=pl.CostEstimate(flops=10**9, bytes_accessed=4 * 10**6, transcendentals=0),

time: 93.4 us -> 92.4 us (0.989)
  Pallas kernels: 33.2 us -> 31.8 us
    pallas_call x2 -> x3, Pallas kernels: 5.97 us -> 5.9 us  [the longest x1 3.22 us: on_device(): pl.pallas_call(prepare_early, out_shape=halves, grid_spec=pltpu.PrefetchS...]
  transfers between devices with their start and end apart: 7 -> 7, of which waited for: 3 -> 3; matrix products, arithmetic and copies ran while one was open for 0% -> 0% of each run, Pallas kernels for 17% -> 16%
where the time goes in v6:
time: 92.4 us; the launch traced here: 92.2 us
  blocking collectives  42 us (45%)
  Pallas kernels  31.8 us (34%)
  starting transfers between devices  14.5 us (16%)
  waiting for transfers between devices  3.69 us (4%)
    all_to_all x1, blocking collectives, on_device(): got = lax.all_to_all(sent, 'seq', split_axis=0, concat_axis=0, tiled=True)  21.5 us
    all_to_all x1, blocking collectives, on_device(): lax.all_to_all(back, ('seq', 'mp'), split_axis=0, concat_axis=0, tiled=Tr...  20.5 us
    ppermute x7, starting transfers between devices, by(): return lax.ppermute(shard, 'mp', [(i, i ^ k) for i in range(MP)])  14.5 us
    pallas_call x1, Pallas kernels, on_device(): pl.pallas_call(inter_layer, out_shape=jax.ShapeDtypeStruct((seq_count, 2,...  13.1 us
    pallas_call x1, Pallas kernels, on_device(): pl.pallas_call(intra_attention, out_shape=jax.ShapeDtypeStruct((count, 64...  7.44 us
    ppermute x7, waiting for transfers between devices, by(): return lax.ppermute(shard, 'mp', [(i, i ^ k) for i in range(MP)])  3.69 us
    pallas_call x1, Pallas kernels, on_device(): pl.pallas_call(prepare_early, out_shape=halves, grid_spec=pltpu.PrefetchS...  3.22 us
    pallas_call x1, Pallas kernels, on_device(): pl.pallas_call(assemble, out_shape=jax.ShapeDtypeStruct((HALF * count, D)...  1.99 us
  transfers between devices with their start and end apart: 7, of which 3 were waited for; matrix products, arithmetic and copies ran while one was open for 0% of the time, Pallas kernels for 16%

profile of v6, /device:TPU:1, one launch (start us, length us, event | category | flops | bytes accessed | tf_op | source)
XLA Modules:
  0.0 92.2 jit_solution(1335127126396374307)
XLA Ops:
  0.0 1.3 %pack.1 = (bf16[256,256]{1,0:T(8,128)(2,1)S(1)}, bf16[1280,256]{1,0:T(8,128)(2,1)S(1)}) custom-call(bf16[192,256]{1,0:T(8,128)(2,1)} %bitcast.14, bf16[64,256]{1,0:T(8,128)(2,1)} %refs_1_.1, bf16[192,256]{1,0:T(8,128)(2,1)} %bitcast.15, bf16[64,256]{1,0:T(8,128)(2,1)} %refs_3_.1, bf16[256,256]{1,0:T(8,128)(2,1)} %refs_4_.1, bf16[256,256]{1,0:T(8,128)(2,1)} %refs_5_.1, ...), custom_call_target="tpu_custom_call" | custom-call | tf_op jit(solution)/shard_map/pack/pallas_call | solution.py:337
  1.3 4.5 %collective-permute-start = (bf16[256,256]{1,0:T(8,128)(2,1)S(1)}, bf16[256,256]{1,0:T(8,128)(2,1)S(1)}, u32[]{:S(2)}, u32[]{:S(2)}) collective-permute-start(bf16[256,256]{1,0:T(8,128)(2,1)S(1)} %get-tuple-element.22.w0.f0), channel_id=1, source_target_pairs={{0,2},{1,3},{2,0},{3,1},{4,6},{5,7},{6,4},{7,5},{8,10},{9,11},{10,... | collective-permute-start | bytes 393224 | tf_op jit(solution)/shard_map/ppermute | solution.py:316
  5.8 3.2 %prepare_early.1 = (bf16[24,128,256]{2,1,0:T(8,128)(2,1)S(1)}, bf16[32,24,256]{2,1,0:T(8,128)(2,1)S(1)}, bf16[128,24,256]{2,1,0:T(8,128)(2,1)S(1)}) custom-call(s32[1]{0:T(128)} %bitcast.mine_ref, bf16[250,24,256]{2,1,0:T(8,128)(2,1)} %bitcast.16), custom_call_target="tpu_custom_call" | custom-call | flops 1000000000 | bytes 4000000 | tf_op jit(solution)/shard_map/prepare_early/pallas_call | solution.py:355
  9.0 0.0 collective-permute-done.w2.f2
  9.0 2.6 %collective-permute-start.3 = (bf16[1280,256]{1,0:T(8,128)(2,1)S(1)}, bf16[1280,256]{1,0:T(8,128)(2,1)S(1)}, u32[]{:S(2)}, u32[]{:S(2)}) collective-permute-start(bf16[1280,256]{1,0:T(8,128)(2,1)S(1)} %get-tuple-element.35.w0), channel_id=1, source_target_pairs={{0,2},{1,3},{2,0},{3,1},{4,6},{5,7},{6,4},{7,5},{8,10},{9,11},{10,... | collective-permute-start | bytes 1966088 | tf_op jit(solution)/shard_map/ppermute | solution.py:316
  11.7 1.8 %collective-permute-start.1 = (bf16[256,256]{1,0:T(8,128)(2,1)S(1)}, bf16[256,256]{1,0:T(8,128)(2,1)S(1)}, u32[]{:S(2)}, u32[]{:S(2)}) collective-permute-start(bf16[256,256]{1,0:T(8,128)(2,1)S(1)} %get-tuple-element.22.w0.f0), channel_id=1, source_target_pairs={{0,1},{1,0},{2,3},{3,2},{4,5},{5,4},{6,7},{7,6},{8,9},{9,8},{10,11... | collective-permute-start | bytes 393224 | tf_op jit(solution)/shard_map/ppermute | solution.py:316
  13.5 0.0 collective-permute-start.2
  13.5 1.5 %prepare_late.1 = (bf16[24,128,256]{2,1,0:T(8,128)(2,1)S(1)}, bf16[32,24,256]{2,1,0:T(8,128)(2,1)S(1)}) custom-call(s32[1]{0:T(128)} %bitcast.mine_ref, bf16[128,24,256]{2,1,0:T(8,128)(2,1)S(1)} %get-tuple-element.26.x_ref), custom_call_target="tpu_custom_call" | custom-call | flops 100000000 | bytes 100000 | tf_op jit(solution)/shard_map/prepare_late/pallas_call | solution.py:374
  15.0 0.0 collective-permute-done.1.w1.f1
  15.0 0.0 collective-permute-done.2.w3.f3
  15.0 7.4 %intra_attention.1.a_ref = bf16[24,64,256]{2,1,0:T(8,128)(2,1)S(1)} custom-call(s32[1]{0:T(128)} %bitcast.mine_ref, bf16[24,128,256]{2,1,0:T(8,128)(2,1)S(1)} %get-tuple-element.25.early_ref, bf16[24,128,256]{2,1,0:T(8,128)(2,1)S(1)} %get-tuple-element.27.late_ref, bf16[256,256]{1,0:T(8,128)(2,1)S(1)} %get-tuple-element.22.w0.f0, ...), custom_call_target="tpu_custom_call" | custom-call | flops 1000000000 | bytes 1000000 | tf_op jit(solution)/shard_map/intra_attention/pallas_call | solution.py:390
  22.5 0.6 collective-permute-start.4
  23.1 1.4 %intra_feed_forward.1 = (bf16[1536,256]{1,0:T(8,128)(2,1)S(1)}, f32[1536,256]{1,0:T(8,128)S(1)}) custom-call(bf16[24,64,256]{2,1,0:T(8,128)(2,1)S(1)} %intra_attention.1.a_ref, bf16[32,24,256]{2,1,0:T(8,128)(2,1)S(1)} %get-tuple-element.30.xq0_ref, bf16[32,24,256]{2,1,0:T(8,128)(2,1)S(1)} %get-tuple-element.31.xq1_ref, ...), custom_call_target="tpu_custom_call" | custom-call | flops 100000000 | bytes 100000 | tf_op jit(solution)/shard_map/intra_feed_forward/pallas_call | solution.py:409
  24.5 1.2 %collective-permute-done.3.w2 = bf16[1280,256]{1,0:T(8,128)(2,1)S(1)} collective-permute-done((bf16[1280,256]{1,0:T(8,128)(2,1)S(1)}, bf16[1280,256]{1,0:T(8,128)(2,1)S(1)}, u32[]{:S(2)}, u32[]{:S(2)}) %collective-permute-start.3) | collective-permute-done | bytes 655392 | tf_op jit(solution)/shard_map/ppermute | solution.py:316
  25.7 2.1 %collective-permute-start.5 = (bf16[1280,256]{1,0:T(8,128)(2,1)S(1)}, bf16[1280,256]{1,0:T(8,128)(2,1)S(1)}, u32[]{:S(2)}, u32[]{:S(2)}) collective-permute-start(bf16[1280,256]{1,0:T(8,128)(2,1)S(1)} %collective-permute-done.3.w2), channel_id=1, source_target_pairs={{0,1},{1,0},{2,3},{3,2},{4,5},{5,4},{6,7},{7,6},{8,9},{9,8},{10,11... | collective-permute-start | bytes 1966088 | tf_op jit(solution)/shard_map/ppermute | solution.py:316
  27.8 0.0 collective-permute-done.4.w1
  27.8 1.2 %intra_more_hidden.1.total_ref = f32[1536,256]{1,0:T(8,128)S(1)} custom-call(bf16[1536,256]{1,0:T(8,128)(2,1)S(1)} %get-tuple-element.32.rows_ref, f32[1536,256]{1,0:T(8,128)S(1)} %get-tuple-element.34.total_ref, bf16[1280,256]{1,0:T(8,128)(2,1)S(1)} %collective-permute-done.4.w1, ...), custom_call_target="tpu_custom_call", output_to_operand_aliasing={{}: (1, {})} | custom-call | flops 1000000000 | bytes 3000000 | tf_op jit(solution)/shard_map/intra_more_hidden/pallas_call | solution.py:423
  28.9 0.6 collective-permute-done.5.w_ref.w3
  29.5 0.7 intra_last_hidden.1
  30.2 21.5 %all_to_all.10 = bf16[32,48,256]{2,1,0:T(8,128)(2,1)S(1)} all-to-all(bf16[32,48,256]{2,1,0:T(8,128)(2,1)S(1)} %bitcast.11), channel_id=1, replica_groups=mesh['seq'=32,'mp'=4] {'seq'}, dimensions={0} | all-to-all | bytes 1572864 | tf_op jit(solution)/shard_map/all_to_all | solution.py:443
  51.6 13.1 %inter_layer.1 = bf16[32,2,24,256]{3,2,1,0:T(8,128)(2,1)S(1)} custom-call(bf16[32,2,24,256]{3,2,1,0:T(8,128)(2,1)S(1)} %bitcast.12, bf16[1280,256]{1,0:T(8,128)(2,1)S(1)} %get-tuple-element.35.w0, bf16[1280,256]{1,0:T(8,128)(2,1)S(1)} %collective-permute-done.4.w1, bf16[1280,256]{1,0:T(8,128)(2,1)S(1)} %collective-permute-done.3.w2, ...), custom_call_target="tpu_custom_call" | custom-call | flops 30000001024 | bytes 4000000 | tf_op jit(solution)/shard_map/inter_layer/pallas_call | solution.py:444
  64.8 20.5 %all_to_all.11.p0 = bf16[64,24,256]{2,1,0:T(8,128)(2,1)S(1)} all-to-all(bf16[64,24,256]{2,1,0:T(8,128)(2,1)S(1)} %bitcast.13), channel_id=1, replica_groups={{0,2,4,6,8,10,12,14,16,18,20,22,24,26,28,30,32,34,36,38,40,42,44,46,48,..., dimensions={0} | all-to-all | bytes 1572864 | tf_op jit(solution)/shard_map/all_to_all | solution.py:458
  85.3 2.9 %collective-permute-start.6 = (bf16[64,24,256]{2,1,0:T(8,128)(2,1)S(1)}, bf16[64,24,256]{2,1,0:T(8,128)(2,1)S(1)}, u32[]{:S(2)}, u32[]{:S(2)}) collective-permute-start(bf16[64,24,256]{2,1,0:T(8,128)(2,1)S(1)} %all_to_all.11.p0), channel_id=1, source_target_pairs={{0,1},{1,0},{2,3},{3,2},{4,5},{5,4},{6,7},{7,6},{8,9},{9,8},{10,11... | collective-permute-start | bytes 2359304 | tf_op jit(solution)/shard_map/ppermute | solution.py:316
  88.1 1.9 %collective-permute-done.6.p1 = bf16[64,24,256]{2,1,0:T(8,128)(2,1)S(1)} collective-permute-done((bf16[64,24,256]{2,1,0:T(8,128)(2,1)S(1)}, bf16[64,24,256]{2,1,0:T(8,128)(2,1)S(1)}, u32[]{:S(2)}, u32[]{:S(2)}) %collective-permute-start.6) | collective-permute-done | bytes 786464 | tf_op jit(solution)/shard_map/ppermute | solution.py:316
  90.0 2.0 %assemble.1 = bf16[3000,256]{1,0:T(8,128)(2,1)} custom-call(s32[1]{0:T(128)} %bitcast.mine_ref, bf16[64,24,256]{2,1,0:T(8,128)(2,1)S(1)} %all_to_all.11.p0, bf16[64,24,256]{2,1,0:T(8,128)(2,1)S(1)} %collective-permute-done.6.p1), custom_call_target="tpu_custom_call" | custom-call | flops 1000000000 | bytes 4000000 | tf_op jit(solution)/shard_map/assemble/pallas_call | solution.py:462
Async XLA Ops:
  1.3 7.7 %collective-permute-start = (bf16[256,256]{1,0:T(8,128)(2,1)S(1)}, bf16[256,256]{1,0:T(8,128)(2,1)S(1)}, u32[]{:S(2)}, u32[]{:S(2)}) collective-permute-start(bf16[256,256]{1,0:T(8,128)(2,1)S(1)} %get-tuple-element.22.w0.f0), channel_id=1, source_target_pairs={{0,2},{1,3},{2,0},{3,1},{4,6},{5,7},{6,4},{7,5},{8,10},{9,11},{10,... | collective-permute-start | bytes 393224 | tf_op jit(solution)/shard_map/ppermute | solution.py:316
  9.0 16.7 %collective-permute-start.3 = (bf16[1280,256]{1,0:T(8,128)(2,1)S(1)}, bf16[1280,256]{1,0:T(8,128)(2,1)S(1)}, u32[]{:S(2)}, u32[]{:S(2)}) collective-permute-start(bf16[1280,256]{1,0:T(8,128)(2,1)S(1)} %get-tuple-element.35.w0), channel_id=1, source_target_pairs={{0,2},{1,3},{2,0},{3,1},{4,6},{5,7},{6,4},{7,5},{8,10},{9,11},{10,... | collective-permute-start | bytes 1966088 | tf_op jit(solution)/shard_map/ppermute | solution.py:316
  11.7 3.4 %collective-permute-start.1 = (bf16[256,256]{1,0:T(8,128)(2,1)S(1)}, bf16[256,256]{1,0:T(8,128)(2,1)S(1)}, u32[]{:S(2)}, u32[]{:S(2)}) collective-permute-start(bf16[256,256]{1,0:T(8,128)(2,1)S(1)} %get-tuple-element.22.w0.f0), channel_id=1, source_target_pairs={{0,1},{1,0},{2,3},{3,2},{4,5},{5,4},{6,7},{7,6},{8,9},{9,8},{10,11... | collective-permute-start | bytes 393224 | tf_op jit(solution)/shard_map/ppermute | solution.py:316
  13.5 1.5 %collective-permute-start.2 = (bf16[256,256]{1,0:T(8,128)(2,1)S(1)}, bf16[256,256]{1,0:T(8,128)(2,1)S(1)}, u32[]{:S(2)}, u32[]{:S(2)}) collective-permute-start(bf16[256,256]{1,0:T(8,128)(2,1)S(1)} %collective-permute-done.w2.f2), channel_id=1, source_target_pairs={{0,1},{1,0},{2,3},{3,2},{4,5},{5,4},{6,7},{7,6},{8,9},{9,8},{10,11... | collective-permute-start | bytes 393224 | tf_op jit(solution)/shard_map/ppermute | solution.py:316
  22.5 5.3 %collective-permute-start.4 = (bf16[1280,256]{1,0:T(8,128)(2,1)S(1)}, bf16[1280,256]{1,0:T(8,128)(2,1)S(1)}, u32[]{:S(2)}, u32[]{:S(2)}) collective-permute-start(bf16[1280,256]{1,0:T(8,128)(2,1)S(1)} %get-tuple-element.35.w0), channel_id=1, source_target_pairs={{0,1},{1,0},{2,3},{3,2},{4,5},{5,4},{6,7},{7,6},{8,9},{9,8},{10,11... | collective-permute-start | bytes 1966088 | tf_op jit(solution)/shard_map/ppermute | solution.py:316
  25.7 3.8 %collective-permute-start.5 = (bf16[1280,256]{1,0:T(8,128)(2,1)S(1)}, bf16[1280,256]{1,0:T(8,128)(2,1)S(1)}, u32[]{:S(2)}, u32[]{:S(2)}) collective-permute-start(bf16[1280,256]{1,0:T(8,128)(2,1)S(1)} %collective-permute-done.3.w2), channel_id=1, source_target_pairs={{0,1},{1,0},{2,3},{3,2},{4,5},{5,4},{6,7},{7,6},{8,9},{9,8},{10,11... | collective-permute-start | bytes 1966088 | tf_op jit(solution)/shard_map/ppermute | solution.py:316
  85.3 4.8 %collective-permute-start.6 = (bf16[64,24,256]{2,1,0:T(8,128)(2,1)S(1)}, bf16[64,24,256]{2,1,0:T(8,128)(2,1)S(1)}, u32[]{:S(2)}, u32[]{:S(2)}) collective-permute-start(bf16[64,24,256]{2,1,0:T(8,128)(2,1)S(1)} %all_to_all.11.p0), channel_id=1, source_target_pairs={{0,1},{1,0},{2,3},{3,2},{4,5},{5,4},{6,7},{7,6},{8,9},{9,8},{10,11... | collective-permute-start | bytes 2359304 | tf_op jit(solution)/shard_map/ppermute | solution.py:316

commit v7 on v6

--- a/solution.py
+++ b/solution.py
@@ -53,7 +53,7 @@
     values = dot(weights_ref[2], rows, 1, 1).astype(BF)
     for h in range(HEADS):
         value_ref[h, 0:HD, :] = values[HD * h : HD * h + HD, :]
-        value_ref[h, HD:48, :] = jnp.ones((48 - HD, rows.shape[0]), BF)
+        value_ref[h, HD:40, :] = jnp.ones((40 - HD, rows.shape[0]), BF)
 
 
 def attend(query_ref, key_ref, value_ref, attended_ref):
@@ -148,7 +148,7 @@
     keys = dot(rows, weights_ref[1], 1, 1).astype(BF)
     query = dot(weights_ref[0], jnp.concatenate(few, axis=0), 1, 1) * Q_SCALE
     values = dot(weights_ref[2], rows, 1, 1).astype(BF)
-    ones = jnp.ones((16, 256), BF)
+    ones = jnp.ones((8, 256), BF)
 
     def scores(u):
         at = slice(256 * u, 256 * u + 256)
@@ -269,15 +269,23 @@
                 o_ref[:, copy] = summed.astype(BF)
 
 
-def assemble(mine_ref, p0, p1, o_ref, rows_ref, done_ref, sems):
+def turn_pieces(piece_ref, o_ref):
     turn = swapped(32, 3)
-    for piece, core, z in ((p, core, z) for core, p in enumerate((p0, p1)) for z in range(2)):
-        at = pl.multiple_of((2 * z + ((mine_ref[0] & 1) ^ core)) * 32, 32)
+    for z in range(2):
         for part in range(3):
-            taken = [piece[2 * s + z, 8 * part : 8 * part + 8, :].astype(F32) for s in range(32)]
+            taken = [piece_ref[2 * s + z, 8 * part : 8 * part + 8, :].astype(F32) for s in range(32)]
             rows = dot(turn, jnp.concatenate(taken, axis=0).astype(BF)).astype(BF)
             for u in range(8):
-                rows_ref[8 * part + u, pl.ds(at, 32), :] = rows[32 * u : 32 * u + 32]
+                o_ref[z, 8 * part + u] = rows[32 * u : 32 * u + 32]
+
+
+def assemble(mine_ref, own_ref, p1, o_ref, rows_ref, done_ref, turned_ref, sems):
+    turn_pieces(p1, turned_ref)
+    for core, source in enumerate((own_ref, turned_ref)):
+        for z in range(2):
+            at = pl.multiple_of((2 * z + ((mine_ref[0] & 1) ^ core)) * 32, 32)
+            for u in range(rows_ref.shape[0]):
+                rows_ref[u, pl.ds(at, 32), :] = source[z, u]
     to = lax.broadcasted_iota(jnp.int32, (128, 256), 0)
     source = lax.broadcasted_iota(jnp.int32, (128, 256), 1)
     copies = []
@@ -307,7 +315,7 @@
         pltpu.VMEM((4, D, D), BF),
         pltpu.VMEM((D, length), BF),
         pltpu.VMEM((HEADS, length, 128), BF),
-        pltpu.VMEM((HEADS, 48, length), BF),
+        pltpu.VMEM((HEADS, 40, length), BF),
         pltpu.VMEM((D, length), F32),
     ]
 
@@ -458,7 +466,16 @@
     back = lax.all_to_all(
         back, ("seq", "mp"), split_axis=0, concat_axis=0, tiled=True, axis_index_groups=groups
     )
-    pieces = [back, by(back, 1)]
+    own = pl.pallas_call(
+        turn_pieces,
+        out_shape=jax.ShapeDtypeStruct((2, count, 32, D), BF),
+        in_specs=[IN_VMEM],
+        out_specs=IN_VMEM,
+        compiler_params=params(8),
+        cost_estimate=pl.CostEstimate(flops=10**8, bytes_accessed=10**6, transcendentals=0),
+        name="turn_pieces",
+    )(back)
+    pieces = [own, by(back, 1)]
     return pl.pallas_call(
         assemble,
         out_shape=jax.ShapeDtypeStruct((HALF * count, D), BF),
@@ -469,6 +486,7 @@
             scratch_shapes=[
                 pltpu.VMEM((count, 128, D), BF),
                 pltpu.VMEM((HALF * count, D), BF),
+                pltpu.VMEM((2, count, 32, D), BF),
                 pltpu.SemaphoreType.DMA((6,)),
             ],
         ),

time: 92.4 us -> 92.2 us (level)
  no operation moved by 1% of the time
where the time goes in v7:
time: 92.2 us; the launch traced here: 92 us
  blocking collectives  42 us (46%)
  Pallas kernels  32 us (35%)
  starting transfers between devices  14.5 us (16%)
  waiting for transfers between devices  3.31 us (4%)
    all_to_all x1, blocking collectives, on_device(): got = lax.all_to_all(sent, 'seq', split_axis=0, concat_axis=0, tiled=True)  21.5 us
    all_to_all x1, blocking collectives, on_device(): lax.all_to_all(back, ('seq', 'mp'), split_axis=0, concat_axis=0, tiled=Tr...  20.5 us
    ppermute x7, starting transfers between devices, by(): return lax.ppermute(shard, 'mp', [(i, i ^ k) for i in range(MP)])  14.5 us
    pallas_call x1, Pallas kernels, on_device(): pl.pallas_call(inter_layer, out_shape=jax.ShapeDtypeStruct((seq_count, 2,...  13.1 us
    pallas_call x1, Pallas kernels, on_device(): pl.pallas_call(intra_attention, out_shape=jax.ShapeDtypeStruct((count, 64...  7.44 us
    ppermute x7, waiting for transfers between devices, by(): return lax.ppermute(shard, 'mp', [(i, i ^ k) for i in range(MP)])  3.31 us
    pallas_call x1, Pallas kernels, on_device(): pl.pallas_call(prepare_early, out_shape=halves, grid_spec=pltpu.PrefetchS...  3.22 us
  transfers between devices with their start and end apart: 7, of which 3 were waited for; matrix products, arithmetic and copies ran while one was open for 0% of the time, Pallas kernels for 16%

profile of v7, /device:TPU:1, one launch (start us, length us, event | category | flops | bytes accessed | tf_op | source)
XLA Modules:
  0.0 92.0 jit_solution(786434325354577190)
XLA Ops:
  0.0 1.3 %pack.1 = (bf16[256,256]{1,0:T(8,128)(2,1)S(1)}, bf16[1280,256]{1,0:T(8,128)(2,1)S(1)}) custom-call(bf16[192,256]{1,0:T(8,128)(2,1)} %bitcast.14, bf16[64,256]{1,0:T(8,128)(2,1)} %refs_1_.1, bf16[192,256]{1,0:T(8,128)(2,1)} %bitcast.15, bf16[64,256]{1,0:T(8,128)(2,1)} %refs_3_.1, bf16[256,256]{1,0:T(8,128)(2,1)} %refs_4_.1, bf16[256,256]{1,0:T(8,128)(2,1)} %refs_5_.1, ...), custom_call_target="tpu_custom_call" | custom-call | tf_op jit(solution)/shard_map/pack/pallas_call | solution.py:345
  1.3 4.5 %collective-permute-start = (bf16[256,256]{1,0:T(8,128)(2,1)S(1)}, bf16[256,256]{1,0:T(8,128)(2,1)S(1)}, u32[]{:S(2)}, u32[]{:S(2)}) collective-permute-start(bf16[256,256]{1,0:T(8,128)(2,1)S(1)} %get-tuple-element.22.w0.f0), channel_id=1, source_target_pairs={{0,2},{1,3},{2,0},{3,1},{4,6},{5,7},{6,4},{7,5},{8,10},{9,11},{10,... | collective-permute-start | bytes 393224 | tf_op jit(solution)/shard_map/ppermute | solution.py:324
  5.8 3.2 %prepare_early.1 = (bf16[24,128,256]{2,1,0:T(8,128)(2,1)S(1)}, bf16[32,24,256]{2,1,0:T(8,128)(2,1)S(1)}, bf16[128,24,256]{2,1,0:T(8,128)(2,1)S(1)}) custom-call(s32[1]{0:T(128)} %bitcast.mine_ref, bf16[250,24,256]{2,1,0:T(8,128)(2,1)} %bitcast.16), custom_call_target="tpu_custom_call" | custom-call | flops 1000000000 | bytes 4000000 | tf_op jit(solution)/shard_map/prepare_early/pallas_call | solution.py:363
  9.0 0.0 collective-permute-done.w2.f2
  9.0 2.6 %collective-permute-start.3 = (bf16[1280,256]{1,0:T(8,128)(2,1)S(1)}, bf16[1280,256]{1,0:T(8,128)(2,1)S(1)}, u32[]{:S(2)}, u32[]{:S(2)}) collective-permute-start(bf16[1280,256]{1,0:T(8,128)(2,1)S(1)} %get-tuple-element.35.w0), channel_id=1, source_target_pairs={{0,2},{1,3},{2,0},{3,1},{4,6},{5,7},{6,4},{7,5},{8,10},{9,11},{10,... | collective-permute-start | bytes 1966088 | tf_op jit(solution)/shard_map/ppermute | solution.py:324
  11.7 1.8 %collective-permute-start.1 = (bf16[256,256]{1,0:T(8,128)(2,1)S(1)}, bf16[256,256]{1,0:T(8,128)(2,1)S(1)}, u32[]{:S(2)}, u32[]{:S(2)}) collective-permute-start(bf16[256,256]{1,0:T(8,128)(2,1)S(1)} %get-tuple-element.22.w0.f0), channel_id=1, source_target_pairs={{0,1},{1,0},{2,3},{3,2},{4,5},{5,4},{6,7},{7,6},{8,9},{9,8},{10,11... | collective-permute-start | bytes 393224 | tf_op jit(solution)/shard_map/ppermute | solution.py:324
  13.5 0.0 collective-permute-start.2
  13.5 1.5 %prepare_late.1 = (bf16[24,128,256]{2,1,0:T(8,128)(2,1)S(1)}, bf16[32,24,256]{2,1,0:T(8,128)(2,1)S(1)}) custom-call(s32[1]{0:T(128)} %bitcast.mine_ref, bf16[128,24,256]{2,1,0:T(8,128)(2,1)S(1)} %get-tuple-element.26.x_ref), custom_call_target="tpu_custom_call" | custom-call | flops 100000000 | bytes 100000 | tf_op jit(solution)/shard_map/prepare_late/pallas_call | solution.py:382
  15.0 0.0 collective-permute-done.1.w1.f1
  15.0 0.0 collective-permute-done.2.w3.f3
  15.0 7.4 %intra_attention.1.a_ref = bf16[24,64,256]{2,1,0:T(8,128)(2,1)S(1)} custom-call(s32[1]{0:T(128)} %bitcast.mine_ref, bf16[24,128,256]{2,1,0:T(8,128)(2,1)S(1)} %get-tuple-element.25.early_ref, bf16[24,128,256]{2,1,0:T(8,128)(2,1)S(1)} %get-tuple-element.27.late_ref, bf16[256,256]{1,0:T(8,128)(2,1)S(1)} %get-tuple-element.22.w0.f0, ...), custom_call_target="tpu_custom_call" | custom-call | flops 1000000000 | bytes 1000000 | tf_op jit(solution)/shard_map/intra_attention/pallas_call | solution.py:398
  22.5 0.6 collective-permute-start.4
  23.1 1.4 %intra_feed_forward.1 = (bf16[1536,256]{1,0:T(8,128)(2,1)S(1)}, f32[1536,256]{1,0:T(8,128)S(1)}) custom-call(bf16[24,64,256]{2,1,0:T(8,128)(2,1)S(1)} %intra_attention.1.a_ref, bf16[32,24,256]{2,1,0:T(8,128)(2,1)S(1)} %get-tuple-element.30.xq0_ref, bf16[32,24,256]{2,1,0:T(8,128)(2,1)S(1)} %get-tuple-element.31.xq1_ref, ...), custom_call_target="tpu_custom_call" | custom-call | flops 100000000 | bytes 100000 | tf_op jit(solution)/shard_map/intra_feed_forward/pallas_call | solution.py:417
  24.5 1.2 %collective-permute-done.3.w2 = bf16[1280,256]{1,0:T(8,128)(2,1)S(1)} collective-permute-done((bf16[1280,256]{1,0:T(8,128)(2,1)S(1)}, bf16[1280,256]{1,0:T(8,128)(2,1)S(1)}, u32[]{:S(2)}, u32[]{:S(2)}) %collective-permute-start.3) | collective-permute-done | bytes 655392 | tf_op jit(solution)/shard_map/ppermute | solution.py:324
  25.7 2.1 %collective-permute-start.5 = (bf16[1280,256]{1,0:T(8,128)(2,1)S(1)}, bf16[1280,256]{1,0:T(8,128)(2,1)S(1)}, u32[]{:S(2)}, u32[]{:S(2)}) collective-permute-start(bf16[1280,256]{1,0:T(8,128)(2,1)S(1)} %collective-permute-done.3.w2), channel_id=1, source_target_pairs={{0,1},{1,0},{2,3},{3,2},{4,5},{5,4},{6,7},{7,6},{8,9},{9,8},{10,11... | collective-permute-start | bytes 1966088 | tf_op jit(solution)/shard_map/ppermute | solution.py:324
  27.8 0.0 collective-permute-done.4.w1
  27.8 1.2 %intra_more_hidden.1.total_ref = f32[1536,256]{1,0:T(8,128)S(1)} custom-call(bf16[1536,256]{1,0:T(8,128)(2,1)S(1)} %get-tuple-element.32.rows_ref, f32[1536,256]{1,0:T(8,128)S(1)} %get-tuple-element.34.total_ref, bf16[1280,256]{1,0:T(8,128)(2,1)S(1)} %collective-permute-done.4.w1, ...), custom_call_target="tpu_custom_call", output_to_operand_aliasing={{}: (1, {})} | custom-call | flops 1000000000 | bytes 3000000 | tf_op jit(solution)/shard_map/intra_more_hidden/pallas_call | solution.py:431
  28.9 0.6 collective-permute-done.5.w_ref.w3
  29.5 0.7 intra_last_hidden.1
  30.2 21.5 %all_to_all.10 = bf16[32,48,256]{2,1,0:T(8,128)(2,1)S(1)} all-to-all(bf16[32,48,256]{2,1,0:T(8,128)(2,1)S(1)} %bitcast.11), channel_id=1, replica_groups=mesh['seq'=32,'mp'=4] {'seq'}, dimensions={0} | all-to-all | bytes 1572864 | tf_op jit(solution)/shard_map/all_to_all | solution.py:451
  51.6 13.1 %inter_layer.1 = bf16[32,2,24,256]{3,2,1,0:T(8,128)(2,1)S(1)} custom-call(bf16[32,2,24,256]{3,2,1,0:T(8,128)(2,1)S(1)} %bitcast.12, bf16[1280,256]{1,0:T(8,128)(2,1)S(1)} %get-tuple-element.35.w0, bf16[1280,256]{1,0:T(8,128)(2,1)S(1)} %collective-permute-done.4.w1, bf16[1280,256]{1,0:T(8,128)(2,1)S(1)} %collective-permute-done.3.w2, ...), custom_call_target="tpu_custom_call" | custom-call | flops 30000001024 | bytes 4000000 | tf_op jit(solution)/shard_map/inter_layer/pallas_call | solution.py:452
  64.8 20.5 %all_to_all.11.piece_ref = bf16[64,24,256]{2,1,0:T(8,128)(2,1)S(1)} all-to-all(bf16[64,24,256]{2,1,0:T(8,128)(2,1)S(1)} %bitcast.13), channel_id=1, replica_groups={{0,2,4,6,8,10,12,14,16,18,20,22,24,26,28,30,32,34,36,38,40,42,44,46,48,..., dimensions={0} | all-to-all | bytes 1572864 | tf_op jit(solution)/shard_map/all_to_all | solution.py:466
  85.3 2.9 %collective-permute-start.6 = (bf16[64,24,256]{2,1,0:T(8,128)(2,1)S(1)}, bf16[64,24,256]{2,1,0:T(8,128)(2,1)S(1)}, u32[]{:S(2)}, u32[]{:S(2)}) collective-permute-start(bf16[64,24,256]{2,1,0:T(8,128)(2,1)S(1)} %all_to_all.11.piece_ref), channel_id=1, source_target_pairs={{0,1},{1,0},{2,3},{3,2},{4,5},{5,4},{6,7},{7,6},{8,9},{9,8},{10,11... | collective-permute-start | bytes 2359304 | tf_op jit(solution)/shard_map/ppermute | solution.py:324
  88.1 0.4 turn_pieces.1.own_ref
  88.5 1.5 %collective-permute-done.6.p1 = bf16[64,24,256]{2,1,0:T(8,128)(2,1)S(1)} collective-permute-done((bf16[64,24,256]{2,1,0:T(8,128)(2,1)S(1)}, bf16[64,24,256]{2,1,0:T(8,128)(2,1)S(1)}, u32[]{:S(2)}, u32[]{:S(2)}) %collective-permute-start.6) | collective-permute-done | bytes 786464 | tf_op jit(solution)/shard_map/ppermute | solution.py:324
  90.0 1.8 %assemble.1 = bf16[3000,256]{1,0:T(8,128)(2,1)} custom-call(s32[1]{0:T(128)} %bitcast.mine_ref, bf16[2,24,32,256]{3,2,1,0:T(8,128)(2,1)S(1)} %turn_pieces.1.own_ref, bf16[64,24,256]{2,1,0:T(8,128)(2,1)S(1)} %collective-permute-done.6.p1), custom_call_target="tpu_custom_call" | custom-call | flops 1000000000 | bytes 4000000 | tf_op jit(solution)/shard_map/assemble/pallas_call | solution.py:479
Async XLA Ops:
  1.3 7.7 %collective-permute-start = (bf16[256,256]{1,0:T(8,128)(2,1)S(1)}, bf16[256,256]{1,0:T(8,128)(2,1)S(1)}, u32[]{:S(2)}, u32[]{:S(2)}) collective-permute-start(bf16[256,256]{1,0:T(8,128)(2,1)S(1)} %get-tuple-element.22.w0.f0), channel_id=1, source_target_pairs={{0,2},{1,3},{2,0},{3,1},{4,6},{5,7},{6,4},{7,5},{8,10},{9,11},{10,... | collective-permute-start | bytes 393224 | tf_op jit(solution)/shard_map/ppermute | solution.py:324
  9.0 16.7 %collective-permute-start.3 = (bf16[1280,256]{1,0:T(8,128)(2,1)S(1)}, bf16[1280,256]{1,0:T(8,128)(2,1)S(1)}, u32[]{:S(2)}, u32[]{:S(2)}) collective-permute-start(bf16[1280,256]{1,0:T(8,128)(2,1)S(1)} %get-tuple-element.35.w0), channel_id=1, source_target_pairs={{0,2},{1,3},{2,0},{3,1},{4,6},{5,7},{6,4},{7,5},{8,10},{9,11},{10,... | collective-permute-start | bytes 1966088 | tf_op jit(solution)/shard_map/ppermute | solution.py:324
  11.7 3.4 %collective-permute-start.1 = (bf16[256,256]{1,0:T(8,128)(2,1)S(1)}, bf16[256,256]{1,0:T(8,128)(2,1)S(1)}, u32[]{:S(2)}, u32[]{:S(2)}) collective-permute-start(bf16[256,256]{1,0:T(8,128)(2,1)S(1)} %get-tuple-element.22.w0.f0), channel_id=1, source_target_pairs={{0,1},{1,0},{2,3},{3,2},{4,5},{5,4},{6,7},{7,6},{8,9},{9,8},{10,11... | collective-permute-start | bytes 393224 | tf_op jit(solution)/shard_map/ppermute | solution.py:324
  13.5 1.5 %collective-permute-start.2 = (bf16[256,256]{1,0:T(8,128)(2,1)S(1)}, bf16[256,256]{1,0:T(8,128)(2,1)S(1)}, u32[]{:S(2)}, u32[]{:S(2)}) collective-permute-start(bf16[256,256]{1,0:T(8,128)(2,1)S(1)} %collective-permute-done.w2.f2), channel_id=1, source_target_pairs={{0,1},{1,0},{2,3},{3,2},{4,5},{5,4},{6,7},{7,6},{8,9},{9,8},{10,11... | collective-permute-start | bytes 393224 | tf_op jit(solution)/shard_map/ppermute | solution.py:324
  22.5 5.3 %collective-permute-start.4 = (bf16[1280,256]{1,0:T(8,128)(2,1)S(1)}, bf16[1280,256]{1,0:T(8,128)(2,1)S(1)}, u32[]{:S(2)}, u32[]{:S(2)}) collective-permute-start(bf16[1280,256]{1,0:T(8,128)(2,1)S(1)} %get-tuple-element.35.w0), channel_id=1, source_target_pairs={{0,1},{1,0},{2,3},{3,2},{4,5},{5,4},{6,7},{7,6},{8,9},{9,8},{10,11... | collective-permute-start | bytes 1966088 | tf_op jit(solution)/shard_map/ppermute | solution.py:324
  25.7 3.8 %collective-permute-start.5 = (bf16[1280,256]{1,0:T(8,128)(2,1)S(1)}, bf16[1280,256]{1,0:T(8,128)(2,1)S(1)}, u32[]{:S(2)}, u32[]{:S(2)}) collective-permute-start(bf16[1280,256]{1,0:T(8,128)(2,1)S(1)} %collective-permute-done.3.w2), channel_id=1, source_target_pairs={{0,1},{1,0},{2,3},{3,2},{4,5},{5,4},{6,7},{7,6},{8,9},{9,8},{10,11... | collective-permute-start | bytes 1966088 | tf_op jit(solution)/shard_map/ppermute | solution.py:324
  85.3 4.8 %collective-permute-start.6 = (bf16[64,24,256]{2,1,0:T(8,128)(2,1)S(1)}, bf16[64,24,256]{2,1,0:T(8,128)(2,1)S(1)}, u32[]{:S(2)}, u32[]{:S(2)}) collective-permute-start(bf16[64,24,256]{2,1,0:T(8,128)(2,1)S(1)} %all_to_all.11.piece_ref), channel_id=1, source_target_pairs={{0,1},{1,0},{2,3},{3,2},{4,5},{5,4},{6,7},{7,6},{8,9},{9,8},{10,11... | collective-permute-start | bytes 2359304 | tf_op jit(solution)/shard_map/ppermute | solution.py:324
